TPU v7x, 256 devices: a whole 4x4x8 slice. The times are simulated.
256 devices in a mesh: pipe: 8 (over z_hi, x), dp: 32 (over y, z_lo, core).
Axes of the slice: x: 4, y: 4, z: 8 (z_hi: 2, z_lo: 4; z = z_hi * 4 + z_lo), core: 2. Of those that a mesh axis runs over, the one named last changes fastest.
Arguments:
- samples: bfloat16 [160, 3, 32, 640], P('dp'), may hold values from -6 to 6
- timesteps: int32 [160], P('dp'), may hold values from 0 to 999
- cotangent: bfloat16 [160, 3, 32, 640], P('dp'), may hold values from -0.059814453 to 0.059814453
- spatial_weight: bfloat16 [8, 5760, 640], P('pipe', 'dp'), may hold values from -0.078125 to 0.078125
- temporal_weight: bfloat16 [8, 1920, 640], P('pipe', 'dp'), may hold values from -0.125 to 0.125
Outputs:
- spatial_grad: float32 [8, 5760, 640], P('pipe', 'dp')
- temporal_grad: float32 [8, 1920, 640], P('pipe', 'dp')
All inputs are finite; a program needn't handle non-finite values.
Results may differ from a plain program's by a relative error of at most 0.034.
Values may be sent and summed in bfloat16 or wider, within the bound.
A program may use at most 128 MiB of HBM per device.

v0:
```python
import math

import jax
import jax.numpy as jnp
from jax import lax
from jax.sharding import PartitionSpec as P

HEIGHT = 8
WIDTH = 4


def passed_along(value, axis, steps):
    count = lax.axis_size(axis)
    first, last = (max(0, -steps), min(count, count - steps))
    return lax.ppermute(value, axis, [(source, source + steps) for source in range(first, last)])


def embedding_of(step, channels):
    half_width = channels // 2
    frequency = jnp.exp(-math.log(10000.0) * jnp.arange(half_width, dtype=jnp.float32) / half_width)
    phases = step.astype(jnp.float32) * frequency
    return jnp.concatenate([jnp.sin(phases), jnp.cos(phases)])


def normalize(summed):
    return summed * lax.rsqrt(jnp.mean(summed * summed, axis=-1, keepdims=True) + 1e-06)


def spatial_columns(normed):
    frames, pixels, channels = normed.shape
    grid = normed.reshape(frames, HEIGHT, WIDTH, channels)
    padded = jnp.pad(grid, ((0, 0), (1, 1), (1, 1), (0, 0)))
    pieces = [
        padded[:, row : row + HEIGHT, col : col + WIDTH, :] for row in range(3) for col in range(3)
    ]
    return jnp.concatenate(pieces, axis=-1).reshape(frames * pixels, 9 * channels)


def spatial_fold(grads, frames, channels):
    parts = grads.reshape(frames, HEIGHT, WIDTH, 9, channels)
    padded = jnp.zeros((frames, HEIGHT + 2, WIDTH + 2, channels), jnp.float32)
    for row in range(3):
        for col in range(3):
            padded = padded.at[:, row : row + HEIGHT, col : col + WIDTH, :].add(
                parts[:, :, :, row * 3 + col, :]
            )
    return padded[:, 1 : HEIGHT + 1, 1 : WIDTH + 1, :].reshape(frames, HEIGHT * WIDTH, channels)


def temporal_columns(activated):
    frames, pixels, channels = activated.shape
    padded = jnp.pad(activated, ((1, 1), (0, 0), (0, 0)))
    pieces = [padded[tap : tap + frames] for tap in range(3)]
    return jnp.concatenate(pieces, axis=-1).reshape(frames * pixels, 3 * channels)


def temporal_fold(grads, frames, pixels, channels):
    parts = grads.reshape(frames, pixels, 3, channels)
    padded = jnp.zeros((frames + 2, pixels, channels), jnp.float32)
    for tap in range(3):
        padded = padded.at[tap : tap + frames].add(parts[:, :, tap, :])
    return padded[1 : frames + 1]


def section_forward(block_in, embedding, spatial, temporal):
    frames, pixels, channels = block_in.shape
    summed = block_in.astype(jnp.float32) + embedding
    normed = normalize(summed).astype(jnp.bfloat16)
    preact = jnp.dot(spatial_columns(normed), spatial, preferred_element_type=jnp.float32)
    activated = jax.nn.silu(preact).astype(jnp.bfloat16).reshape(frames, pixels, channels)
    mixed = jnp.dot(temporal_columns(activated), temporal, preferred_element_type=jnp.float32)
    return (block_in.astype(jnp.float32) + mixed.reshape(frames, pixels, channels)).astype(
        jnp.bfloat16
    )


def backward_first(block_in, embedding, spatial, temporal, upstream):
    frames, pixels, channels = block_in.shape
    summed = block_in.astype(jnp.float32) + embedding
    normed = normalize(summed).astype(jnp.bfloat16)
    columns = spatial_columns(normed)
    preact = jnp.dot(columns, spatial, preferred_element_type=jnp.float32)
    activated = jax.nn.silu(preact).astype(jnp.bfloat16).reshape(frames, pixels, channels)
    tcolumns = temporal_columns(activated)
    upstream_flat = upstream.reshape(frames * pixels, channels)
    temporal_term = jnp.dot(tcolumns.T, upstream_flat, preferred_element_type=jnp.float32)
    act_grad = temporal_fold(
        jnp.dot(upstream_flat, temporal.T, preferred_element_type=jnp.float32),
        frames,
        pixels,
        channels,
    )
    logistic = jax.nn.sigmoid(preact)
    slope = logistic * (1.0 + preact * (1.0 - logistic))
    pre_grad = (act_grad.reshape(frames * pixels, channels) * slope).astype(jnp.bfloat16)
    return (temporal_term, pre_grad, columns)


def backward_second(block_in, embedding, spatial, upstream, pre_grad, columns):
    frames, pixels, channels = block_in.shape
    summed = block_in.astype(jnp.float32) + embedding
    spatial_term = jnp.dot(columns.T, pre_grad, preferred_element_type=jnp.float32)
    norm_grad = spatial_fold(
        jnp.dot(pre_grad, spatial.T, preferred_element_type=jnp.float32), frames, channels
    )
    _, pullback = jax.vjp(normalize, summed)
    back_input = (upstream.astype(jnp.float32) + pullback(norm_grad)[0]).astype(jnp.bfloat16)
    return (back_input, spatial_term)


def section_backward(block_in, embedding, spatial, temporal, upstream):
    temporal_term, pre_grad, columns = backward_first(
        block_in, embedding, spatial, temporal, upstream
    )
    back_input, spatial_term = backward_second(
        block_in, embedding, spatial, upstream, pre_grad, columns
    )
    return (back_input, spatial_term, temporal_term)


def per_device(samples, timesteps, cotangent, spatial_weight, temporal_weight):
    sections = lax.axis_size("pipe")
    section_index = lax.axis_index("pipe")
    micro_count = samples.shape[0]
    frames, pixels, channels = (samples.shape[1], samples.shape[2], samples.shape[3])
    moments = jnp.arange(micro_count + sections - 1, dtype=jnp.int32)
    blank = jnp.zeros((frames, pixels, channels), jnp.bfloat16)
    full_spatial, full_temporal = (
        lax.all_gather(spatial_weight[0], "dp", axis=0, tiled=True),
        lax.all_gather(temporal_weight[0], "dp", axis=0, tiled=True),
    )

    def forward_step(carry, moment):
        incoming, stash = carry
        position = moment - section_index
        active = (position >= 0) & (position < micro_count)
        picked = jnp.clip(position, 0, micro_count - 1)
        own = lax.dynamic_index_in_dim(samples, picked, 0, keepdims=False)
        embedding = embedding_of(
            lax.dynamic_index_in_dim(timesteps, picked, 0, keepdims=False), channels
        )
        block_in = jnp.where(section_index == 0, own, incoming)
        result = lax.cond(
            active & (section_index < sections - 1),
            lambda: section_forward(block_in, embedding, full_spatial, full_temporal),
            lambda: blank,
        )
        stash = jnp.where(
            active, lax.dynamic_update_index_in_dim(stash, block_in, picked, 0), stash
        )
        passed = passed_along(result, "pipe", 1)
        return ((passed, stash), None)

    (_, stash), _ = lax.scan(forward_step, (blank, jnp.zeros_like(samples)), moments)
    back_spatial, back_temporal = (full_spatial, full_temporal)

    def inputs_at(moment, incoming):
        position = moment - (sections - 1 - section_index)
        active = (position >= 0) & (position < micro_count)
        picked = jnp.clip(position, 0, micro_count - 1)
        block_in = lax.dynamic_index_in_dim(stash, picked, 0, keepdims=False)
        embedding = embedding_of(
            lax.dynamic_index_in_dim(timesteps, picked, 0, keepdims=False), channels
        )
        given = lax.dynamic_index_in_dim(cotangent, picked, 0, keepdims=False)
        upstream = jnp.where(section_index == sections - 1, given, incoming)
        return (active, block_in, embedding, upstream)

    def backward_step(carry, moment):
        incoming, grad_spatial, grad_temporal = carry
        active, block_in, embedding, upstream = inputs_at(moment, incoming)

        def working():
            back_input, spatial_term, temporal_term = section_backward(
                block_in, embedding, back_spatial, back_temporal, upstream
            )
            return (back_input, grad_spatial + spatial_term, grad_temporal + temporal_term)

        def waiting():
            return (blank, grad_spatial, grad_temporal)

        back_input, grad_spatial, grad_temporal = lax.cond(active, working, waiting)
        passed = passed_along(back_input, "pipe", -1)
        return ((passed, grad_spatial, grad_temporal), None)

    start = (
        blank,
        jnp.zeros(back_spatial.shape, jnp.float32),
        jnp.zeros(back_temporal.shape, jnp.float32),
    )
    (_, grad_spatial, grad_temporal), _ = lax.scan(backward_step, start, moments)
    share_spatial, share_temporal = (
        lax.psum_scatter(
            grad_spatial.astype(jnp.bfloat16).astype(jnp.float32).astype(jnp.bfloat16),
            "dp",
            scatter_dimension=0,
            tiled=True,
        ).astype(jnp.float32),
        lax.psum_scatter(
            grad_temporal.astype(jnp.bfloat16).astype(jnp.float32).astype(jnp.bfloat16),
            "dp",
            scatter_dimension=0,
            tiled=True,
        ).astype(jnp.float32),
    )
    return (share_spatial[None], share_temporal[None])


def solution(mesh):
    return jax.shard_map(
        per_device,
        mesh=mesh,
        in_specs=(
            P("dp", None, None, None),
            P("dp"),
            P("dp", None, None, None),
            P("pipe", "dp", None),
            P("pipe", "dp", None),
        ),
        out_specs=(P("pipe", "dp", None), P("pipe", "dp", None)),
        check_vma=False,
    )
```

profile of v0, /device:TPU:1, one launch (start us, length us, event | category | flops | bytes accessed | tf_op | source)
XLA Modules:
  0.0 1464.3 jit_solution(15239330728416313697)
XLA Ops:
  11.1 67.9 %all-gather.5.cloned.1.call-done = bf16[1,1920,640]{2,0,1:T(2,128)(2,1)} async-done(((bf16[1,60,640]{2,0,1:T(2,128)(2,1)}), bf16[1,1920,640]{2,0,1:T(2,128)(2,1)}) %all-gather.5.cloned.1.call-update) | async-done | bytes 2457616 | tf_op jit(solution)/shard_map/all_gather | solution.py:130
  83.1 86.8 %all-gather.7.cloned.1.call-done = bf16[1,5760,640]{2,0,1:T(2,128)(2,1)} async-done(((bf16[1,180,640]{2,0,1:T(2,128)(2,1)}), bf16[1,5760,640]{2,0,1:T(2,128)(2,1)}) %all-gather.7.cloned.1.call-update) | async-done | bytes 7372816 | tf_op jit(solution)/shard_map/all_gather | solution.py:129
  180.3 201.1 %while.42 = (s32[]{:T(128)}, bf16[3,32,640]{2,1,0:T(8,128)(2,1)S(1)}, bf16[5,3,32,640]{3,2,1,0:T(8,128)(2,1)}, s32[12]{0:T(128)S(1)}, s32[]{:T(128)}, /*index=5*...) while((s32[]{:T(128)}, ...), condition=%wide.region_4.5_spmd, body=%wide.region_0.4_spmd.sunk | while | flops 945931648 | bytes 28892004 | solution.py:154
  291.2 11.8 collective-permute-start
  325.2 16.1 %collective-permute-start = (bf16[3,32,640]{2,1,0:T(8,128)(2,1)S(1)}, bf16[3,32,640]{2,1,0:T(8,128)(2,1)S(1)}, u32[]{:S(2)}, u32[]{:S(2)}) collective-permute-start(bf16[3,32,640]{2,1,0:T(8,128)(2,1)S(1)} %get-tuple-element.887), channel_id=1, source_target_pairs={{0,32},{32,64},{64,96},{96,128},{128,160},{160,192},{192,224},{1,3... | collective-permute-start | bytes 368648 | tf_op jit(solution)/shard_map/while/body/eval_jaxpr/ppermute | solution.py:15
  363.4 16.1 %collective-permute-start = (bf16[3,32,640]{2,1,0:T(8,128)(2,1)S(1)}, bf16[3,32,640]{2,1,0:T(8,128)(2,1)S(1)}, u32[]{:S(2)}, u32[]{:S(2)}) collective-permute-start(bf16[3,32,640]{2,1,0:T(8,128)(2,1)S(1)} %get-tuple-element.887), channel_id=1, source_target_pairs={{0,32},{32,64},{64,96},{96,128},{128,160},{160,192},{192,224},{1,3... | collective-permute-start | bytes 368648 | tf_op jit(solution)/shard_map/while/body/eval_jaxpr/ppermute | solution.py:15
  390.1 893.1 %while.43 = (s32[]{:T(128)}, bf16[3,32,640]{2,1,0:T(8,128)(2,1)S(1)}, f32[5760,640]{1,0:T(8,128)}, f32[1920,640]{1,0:T(8,128)}, s32[12]{0:T(128)S(1)}, /*index=5...) while((s32[]{:T(128)}, ...), condition=%wide.region_11.12_spmd, body=%wide.region_5.11_spmd.sunk | while | flops 2604136192 | bytes 116898472 | solution.py:191
  394.3 10.7 collective-permute-done.1
  409.0 11.0 collective-permute-done.1
  424.0 12.5 collective-permute-done.1
  440.4 11.4 collective-permute-done.1
  483.0 418.0 %collective-permute-done.1 = bf16[3,32,640]{2,1,0:T(8,128)(2,1)S(1)} collective-permute-done((bf16[3,32,640]{2,1,0:T(8,128)(2,1)S(1)}, bf16[3,32,640]{2,1,0:T(8,128)(2,1)S(1)}, u32[]{:S(2)}, u32[]{:S(2)}) %collective-permute-start.1) | collective-permute-done | bytes 122912 | tf_op jit(solution)/shard_map/while/body/eval_jaxpr/ppermute | solution.py:15
  903.6 63.4 %conditional.5 = (bf16[3,32,640]{2,1,0:T(8,128)(2,1)S(1)}, f32[5760,640]{1,0:T(8,128)}, f32[1920,640]{1,0:T(8,128)}) conditional(s32[]{:T(128)} %convert_element_type.150, (f32[5760,640]{1,0:T(8,128)}, f32[1920,640]{1,0:T(8,128)}) %tuple.165, (pred[]{:T(512)}, bf16[5,3,32,640]{3,2,1,0:T(8,128)(2,1)}, s32[]{:T(128)}, ...), branch_computations={%region_6.6_spmd, %region_7.10_spmd} | conditional | flops 2604134912 | bytes 116398888 | solution.py:182
  921.5 12.7 convolution_add_fusion
  968.3 10.3 collective-permute-done.1
  981.3 63.4 %conditional.5 = (bf16[3,32,640]{2,1,0:T(8,128)(2,1)S(1)}, f32[5760,640]{1,0:T(8,128)}, f32[1920,640]{1,0:T(8,128)}) conditional(s32[]{:T(128)} %convert_element_type.150, (f32[5760,640]{1,0:T(8,128)}, f32[1920,640]{1,0:T(8,128)}) %tuple.165, (pred[]{:T(512)}, bf16[5,3,32,640]{3,2,1,0:T(8,128)(2,1)}, s32[]{:T(128)}, ...), branch_computations={%region_6.6_spmd, %region_7.10_spmd} | conditional | flops 2604134912 | bytes 116398888 | solution.py:182
  999.2 12.7 convolution_add_fusion
  1058.9 63.4 %conditional.5 = (bf16[3,32,640]{2,1,0:T(8,128)(2,1)S(1)}, f32[5760,640]{1,0:T(8,128)}, f32[1920,640]{1,0:T(8,128)}) conditional(s32[]{:T(128)} %convert_element_type.150, (f32[5760,640]{1,0:T(8,128)}, f32[1920,640]{1,0:T(8,128)}) %tuple.165, (pred[]{:T(512)}, bf16[5,3,32,640]{3,2,1,0:T(8,128)(2,1)}, s32[]{:T(128)}, ...), branch_computations={%region_6.6_spmd, %region_7.10_spmd} | conditional | flops 2604134912 | bytes 116398888 | solution.py:182
  1076.8 12.7 convolution_add_fusion
  1136.5 63.4 %conditional.5 = (bf16[3,32,640]{2,1,0:T(8,128)(2,1)S(1)}, f32[5760,640]{1,0:T(8,128)}, f32[1920,640]{1,0:T(8,128)}) conditional(s32[]{:T(128)} %convert_element_type.150, (f32[5760,640]{1,0:T(8,128)}, f32[1920,640]{1,0:T(8,128)}) %tuple.165, (pred[]{:T(512)}, bf16[5,3,32,640]{3,2,1,0:T(8,128)(2,1)}, s32[]{:T(128)}, ...), branch_computations={%region_6.6_spmd, %region_7.10_spmd} | conditional | flops 2604134912 | bytes 116398888 | solution.py:182
  1154.5 12.7 convolution_add_fusion
  1214.2 63.4 %conditional.5 = (bf16[3,32,640]{2,1,0:T(8,128)(2,1)S(1)}, f32[5760,640]{1,0:T(8,128)}, f32[1920,640]{1,0:T(8,128)}) conditional(s32[]{:T(128)} %convert_element_type.150, (f32[5760,640]{1,0:T(8,128)}, f32[1920,640]{1,0:T(8,128)}) %tuple.165, (pred[]{:T(512)}, bf16[5,3,32,640]{3,2,1,0:T(8,128)(2,1)}, s32[]{:T(128)}, ...), branch_computations={%region_6.6_spmd, %region_7.10_spmd} | conditional | flops 2604134912 | bytes 116398888 | solution.py:182
  1232.1 12.7 convolution_add_fusion
  1294.8 143.4 %fusion.48 = (bf16[192,640]{1,0:T(8,128)(2,1)S(1)}, bf16[64,640]{1,0:T(8,128)(2,1)S(1)}) fusion(bf16[5760,640]{1,0:T(8,128)(2,1)} %convert_element_type.116, bf16[1920,640]{1,0:T(8,128)(2,1)S(1)} %convert_element_type.117), kind=kCustom, calls=%all-reduce-scatter.2 | all-reduce-scatter fusion | flops 5242882 | bytes 10159104
  (708 shorter events, 566.4 us)
Async XLA Ops:
  7.2 71.8 %all-gather.5.cloned.1.call-start = ((), (), s32[]{:S(2)}) async-start(), calls=%async_computation | async-start | bytes 5068800 | tf_op jit(solution)/shard_map/all_gather | solution.py:130
  8.9 161.0 %all-gather.7.cloned.1.call-start = ((), (), s32[]{:S(2)}) async-start(), calls=%async_computation.1 | async-start | bytes 15206400 | tf_op jit(solution)/shard_map/all_gather | solution.py:129
  205.6 6.0 collective-permute-start
  222.2 6.0 collective-permute-start
  265.0 11.9 collective-permute-start
  291.2 13.6 collective-permute-start
  309.2 11.6 collective-permute-start
  325.2 18.0 %collective-permute-start = (bf16[3,32,640]{2,1,0:T(8,128)(2,1)S(1)}, bf16[3,32,640]{2,1,0:T(8,128)(2,1)S(1)}, u32[]{:S(2)}, u32[]{:S(2)}) collective-permute-start(bf16[3,32,640]{2,1,0:T(8,128)(2,1)S(1)} %get-tuple-element.887), channel_id=1, source_target_pairs={{0,32},{32,64},{64,96},{96,128},{128,160},{160,192},{192,224},{1,3... | collective-permute-start | bytes 368648 | tf_op jit(solution)/shard_map/while/body/eval_jaxpr/ppermute | solution.py:15
  347.5 11.6 collective-permute-start
  363.4 18.0 %collective-permute-start = (bf16[3,32,640]{2,1,0:T(8,128)(2,1)S(1)}, bf16[3,32,640]{2,1,0:T(8,128)(2,1)S(1)}, u32[]{:S(2)}, u32[]{:S(2)}) collective-permute-start(bf16[3,32,640]{2,1,0:T(8,128)(2,1)S(1)} %get-tuple-element.887), channel_id=1, source_target_pairs={{0,32},{32,64},{64,96},{96,128},{128,160},{160,192},{192,224},{1,3... | collective-permute-start | bytes 368648 | tf_op jit(solution)/shard_map/while/body/eval_jaxpr/ppermute | solution.py:15
  393.0 12.0 collective-permute-start.1
  407.7 12.3 collective-permute-start.1
  422.7 13.8 collective-permute-start.1
  439.1 12.8 collective-permute-start.1
  454.5 10.8 collective-permute-start.1
  468.0 11.1 collective-permute-start.1
  481.7 419.3 %collective-permute-start.1 = (bf16[3,32,640]{2,1,0:T(8,128)(2,1)S(1)}, bf16[3,32,640]{2,1,0:T(8,128)(2,1)S(1)}, u32[]{:S(2)}, u32[]{:S(2)}) collective-permute-start(bf16[3,32,640]{2,1,0:T(8,128)(2,1)S(1)} %get-tuple-element.785), channel_id=1, source_target_pairs={{32,0},{64,32},{96,64},{128,96},{160,128},{192,160},{224,192},{33,... | collective-permute-start | bytes 368648 | tf_op jit(solution)/shard_map/while/body/eval_jaxpr/ppermute | solution.py:15
  967.0 11.6 collective-permute-start.1
  1044.6 11.6 collective-permute-start.1
  1122.3 11.6 collective-permute-start.1
  1199.9 11.6 collective-permute-start.1
  1438.1 16.7 %collective-permute-start.2 = (bf16[192,640]{1,0:T(8,128)(2,1)S(1)}, bf16[192,640]{1,0:T(8,128)(2,1)S(1)}, u32[]{:S(2)}, u32[]{:S(2)}) collective-permute-start(bf16[192,640]{1,0:T(8,128)(2,1)S(1)} %get-tuple-element.585), channel_id=1, source_target_pairs={{0,1},{1,2},{2,3},{3,4},{4,5},{5,6},{6,7},{7,8},{8,9},{9,10},{10,1... | collective-permute-start | bytes 737288
  1442.6 12.2 collective-permute-start.3
  1445.5 7.8 collective-permute-start.4
  (28 other events, 488.7 us)
Sparse Core Ops, SparseCore 0:
  10.4 68.4 all-gather.4
  81.4 88.5 all-gather.6
where the time goes:
time: 1470 us; the launch traced here: 1460 us
  waiting for transfers between devices  708 us (48%)
  local copies, waits for them, and re-layouts  192 us (13%)
  matrix products  164 us (11%)
  blocking collectives  143 us (10%)
  starting transfers between devices  121 us (8%)
  other arithmetic  85.4 us (6%)
  loops' own time  34.9 us (2%)
  between operations  15.5 us (1%)
    ppermute x24, waiting for transfers between devices, passed_along(): lax.ppermute(value, axis, [(source, source + steps) for source in range(f...  552 us
    unnamed x1, blocking collectives  143 us
    ppermute x24, starting transfers between devices, passed_along(): lax.ppermute(value, axis, [(source, source + steps) for source in range(f...  110 us
    all_gather x1, waiting for transfers between devices, per_device(): lax.all_gather(spatial_weight[0], 'dp', axis=0, tiled=True)  86.8 us
    all_gather x1, waiting for transfers between devices, per_device(): lax.all_gather(temporal_weight[0], 'dp', axis=0, tiled=True)  67.9 us
    dot_general x5, matrix products, backward_second(): jnp.dot(columns.T, pre_grad, preferred_element_type=jnp.float32)  63.4 us
    scatter-add x35, local copies, waits for them, and re-layouts, spatial_fold(): padded.at[:, row:row + HEIGHT, col:col + WIDTH, :]  56.9 us
    slice x5, local copies, waits for them, and re-layouts, spatial_fold(): parts[:, :, :, row * 3 + col, :]  47.8 us
  transfers between devices with their start and end apart: 30, of which 27 were waited for; matrix products, arithmetic and copies ran while one was open for 1% of the time, Pallas kernels for 0%

commit v1 on v0

v1 whole, which is shorter than its diff:
```python
import math

import jax
import jax.numpy as jnp
from jax import lax
from jax.sharding import PartitionSpec as P

HEIGHT = 8
WIDTH = 4


def passed_along(value, axis, steps):
    count = lax.axis_size(axis)
    first, last = (max(0, -steps), min(count, count - steps))
    return lax.ppermute(value, axis, [(source, source + steps) for source in range(first, last)])


def embedding_of(step, channels):
    half_width = channels // 2
    frequency = jnp.exp(-math.log(10000.0) * jnp.arange(half_width, dtype=jnp.float32) / half_width)
    phases = step.astype(jnp.float32) * frequency
    return jnp.concatenate([jnp.sin(phases), jnp.cos(phases)])


def normalize(summed):
    return summed * lax.rsqrt(jnp.mean(summed * summed, axis=-1, keepdims=True) + 1e-06)


def spatial_columns(normed):
    lead = normed.shape[:-2]
    channels = normed.shape[-1]
    grid = normed.reshape(lead + (HEIGHT, WIDTH, channels))
    pad = [(0, 0)] * len(lead) + [(1, 1), (1, 1), (0, 0)]
    padded = jnp.pad(grid, pad)
    pieces = [
        padded[..., row : row + HEIGHT, col : col + WIDTH, :] for row in range(3) for col in range(3)
    ]
    return jnp.concatenate(pieces, axis=-1).reshape(-1, 9 * channels)


def spatial_fold(grads, frames, channels):
    parts = grads.reshape(frames, HEIGHT, WIDTH, 9, channels)
    total = None
    for row in range(3):
        for col in range(3):
            piece = jnp.pad(
                parts[:, :, :, row * 3 + col, :],
                ((0, 0), (row, 2 - row), (col, 2 - col), (0, 0)),
            )
            total = piece if total is None else total + piece
    return total[:, 1 : HEIGHT + 1, 1 : WIDTH + 1, :].reshape(frames, HEIGHT * WIDTH, channels)


def temporal_columns(activated):
    lead = activated.shape[:-3]
    frames = activated.shape[-3]
    channels = activated.shape[-1]
    pad = [(0, 0)] * len(lead) + [(1, 1), (0, 0), (0, 0)]
    padded = jnp.pad(activated, pad)
    pieces = [padded[..., tap : tap + frames, :, :] for tap in range(3)]
    return jnp.concatenate(pieces, axis=-1).reshape(-1, 3 * channels)


def temporal_fold(grads, frames, pixels, channels):
    parts = grads.reshape(frames, pixels, 3, channels)
    total = None
    for tap in range(3):
        piece = jnp.pad(parts[:, :, tap, :], ((tap, 2 - tap), (0, 0), (0, 0)))
        total = piece if total is None else total + piece
    return total[1 : frames + 1]


def section_forward(block_in, embedding, spatial, temporal):
    frames, pixels, channels = block_in.shape
    summed = block_in.astype(jnp.float32) + embedding
    normed = normalize(summed).astype(jnp.bfloat16)
    preact = jnp.dot(spatial_columns(normed), spatial, preferred_element_type=jnp.float32)
    activated = jax.nn.silu(preact).astype(jnp.bfloat16).reshape(frames, pixels, channels)
    mixed = jnp.dot(temporal_columns(activated), temporal, preferred_element_type=jnp.float32)
    out = (block_in.astype(jnp.float32) + mixed.reshape(frames, pixels, channels)).astype(
        jnp.bfloat16
    )
    return out, normed, preact.reshape(frames, pixels, channels), activated


def section_backward(block_in, embedding, spatial, temporal, upstream, preact):
    frames, pixels, channels = block_in.shape
    summed = block_in.astype(jnp.float32) + embedding
    upstream_flat = upstream.reshape(frames * pixels, channels)
    act_grad = temporal_fold(
        jnp.dot(upstream_flat, temporal.T, preferred_element_type=jnp.float32),
        frames,
        pixels,
        channels,
    )
    logistic = jax.nn.sigmoid(preact)
    slope = logistic * (1.0 + preact * (1.0 - logistic))
    pre_grad = (act_grad * slope).astype(jnp.bfloat16)
    norm_grad = spatial_fold(
        jnp.dot(
            pre_grad.reshape(frames * pixels, channels),
            spatial.T,
            preferred_element_type=jnp.float32,
        ),
        frames,
        channels,
    )
    _, pullback = jax.vjp(normalize, summed)
    back_input = (upstream.astype(jnp.float32) + pullback(norm_grad)[0]).astype(jnp.bfloat16)
    return back_input, pre_grad


def per_device(samples, timesteps, cotangent, spatial_weight, temporal_weight):
    sections = lax.axis_size("pipe")
    n_dp = lax.axis_size("dp")
    section_index = lax.axis_index("pipe")
    micro_count = samples.shape[0]
    frames, pixels, channels = (samples.shape[1], samples.shape[2], samples.shape[3])
    moments = jnp.arange(micro_count + sections - 1, dtype=jnp.int32)
    blank = jnp.zeros((frames, pixels, channels), jnp.bfloat16)

    sp_rows = spatial_weight.shape[1]
    tm_rows = temporal_weight.shape[1]
    own_rows = jnp.concatenate([spatial_weight[0], temporal_weight[0]], axis=0)
    gathered = lax.all_gather(own_rows, "dp", axis=0, tiled=False)
    full_spatial = gathered[:, :sp_rows].reshape(n_dp * sp_rows, channels)
    full_temporal = gathered[:, sp_rows:].reshape(n_dp * tm_rows, channels)

    embeddings = jax.vmap(lambda s: embedding_of(s, channels))(timesteps)

    def slot_of(position):
        return jnp.clip(position, -1, micro_count) + 1

    def stash_put(stash, value, slot):
        return lax.dynamic_update_index_in_dim(stash, value, slot, 0)

    def forward_step(carry, moment):
        incoming, s_in, s_normed, s_preact, s_act = carry
        position = moment - section_index
        picked = jnp.clip(position, 0, micro_count - 1)
        slot = slot_of(position)
        own = lax.dynamic_index_in_dim(samples, picked, 0, keepdims=False)
        embedding = lax.dynamic_index_in_dim(embeddings, picked, 0, keepdims=False)
        block_in = jnp.where(section_index == 0, own, incoming)
        result, normed, preact, activated = section_forward(
            block_in, embedding, full_spatial, full_temporal
        )
        s_in = stash_put(s_in, block_in, slot)
        s_normed = stash_put(s_normed, normed.reshape(frames, pixels, channels), slot)
        s_preact = stash_put(s_preact, preact, slot)
        s_act = stash_put(s_act, activated, slot)
        passed = passed_along(result, "pipe", 1)
        return ((passed, s_in, s_normed, s_preact, s_act), None)

    slots = micro_count + 2
    start = (
        blank,
        jnp.zeros((slots, frames, pixels, channels), jnp.bfloat16),
        jnp.zeros((slots, frames, pixels, channels), jnp.bfloat16),
        jnp.zeros((slots, frames, pixels, channels), jnp.float32),
        jnp.zeros((slots, frames, pixels, channels), jnp.bfloat16),
    )
    (_, s_in, s_normed, s_preact, s_act), _ = lax.scan(forward_step, start, moments)

    def backward_step(carry, moment):
        incoming, s_pre, s_up = carry
        position = moment - (sections - 1 - section_index)
        picked = jnp.clip(position, 0, micro_count - 1)
        slot = slot_of(position)
        stored = jnp.clip(position, 0, micro_count - 1) + 1
        block_in = lax.dynamic_index_in_dim(s_in, stored, 0, keepdims=False)
        preact = lax.dynamic_index_in_dim(s_preact, stored, 0, keepdims=False)
        embedding = lax.dynamic_index_in_dim(embeddings, picked, 0, keepdims=False)
        given = lax.dynamic_index_in_dim(cotangent, picked, 0, keepdims=False)
        upstream = jnp.where(section_index == sections - 1, given, incoming)
        back_input, pre_grad = section_backward(
            block_in, embedding, full_spatial, full_temporal, upstream, preact
        )
        s_pre = stash_put(s_pre, pre_grad, slot)
        s_up = stash_put(s_up, upstream, slot)
        passed = passed_along(back_input, "pipe", -1)
        return ((passed, s_pre, s_up), None)

    start = (
        blank,
        jnp.zeros((slots, frames, pixels, channels), jnp.bfloat16),
        jnp.zeros((slots, frames, pixels, channels), jnp.bfloat16),
    )
    (_, s_pre, s_up), _ = lax.scan(backward_step, start, moments)

    normed_all = s_normed[1 : micro_count + 1]
    act_all = s_act[1 : micro_count + 1]
    pre_all = s_pre[1 : micro_count + 1].reshape(-1, channels)
    up_all = s_up[1 : micro_count + 1].reshape(-1, channels)
    spatial_term = lax.dot_general(
        spatial_columns(normed_all), pre_all, (((0,), (0,)), ((), ())),
        preferred_element_type=jnp.float32,
    )
    temporal_term = lax.dot_general(
        temporal_columns(act_all), up_all, (((0,), (0,)), ((), ())),
        preferred_element_type=jnp.float32,
    )
    partial_rows = jnp.concatenate(
        [
            spatial_term.astype(jnp.bfloat16).reshape(n_dp, sp_rows, channels),
            temporal_term.astype(jnp.bfloat16).reshape(n_dp, tm_rows, channels),
        ],
        axis=1,
    )
    share = lax.psum_scatter(partial_rows, "dp", scatter_dimension=0, tiled=False)
    share = share.astype(jnp.float32)
    return (share[None, :sp_rows], share[None, sp_rows:])


def solution(mesh):
    return jax.shard_map(
        per_device,
        mesh=mesh,
        in_specs=(
            P("dp", None, None, None),
            P("dp"),
            P("dp", None, None, None),
            P("pipe", "dp", None),
            P("pipe", "dp", None),
        ),
        out_specs=(P("pipe", "dp", None), P("pipe", "dp", None)),
        check_vma=False,
    )
```

time: 1470 us -> 938 us (0.64)
  waiting for transfers between devices: 708 us -> 427 us
  blocking collectives: 143 us -> 0 us
  local copies, waits for them, and re-layouts: 192 us -> 114 us
  loops' own time: 34.9 us -> 18.8 us
    ppermute x24, waiting for transfers between devices: 552 us -> 143 us  [passed_along(): lax.ppermute(value, axis, [(source, source + steps) for source in range(f...]
    reduce_scatter x0 -> x1, waiting for transfers between devices: none -> 208 us  [per_device(): lax.psum_scatter(partial_rows, 'dp', scatter_dimension=0, tiled=False)]
    unnamed x1 -> x0, blocking collectives: 143 us -> none
    all_gather x2 -> x1, waiting for transfers between devices: 155 us -> 76.1 us  [per_device(): gathered = lax.all_gather(own_rows, 'dp', axis=0, tiled=False)]
    dynamic_update_slice x0 -> x48, other arithmetic: none -> 60 us  [stash_put(): return lax.dynamic_update_index_in_dim(stash, value, slot, 0)]
    scatter-add x40 -> x0, local copies, waits for them, and re-layouts: 57 us -> none  [the longest x35 56.9 us: spatial_fold(): padded.at[:, row:row + HEIGHT, col:col + WIDTH, :]]
    dot_general x25 -> x26, matrix products: 138 us -> 104 us  [the longest x12 63.8 us: section_backward(): jnp.dot(pre_grad.reshape(frames * pixels, channels), spatial.T, preferred...]
    dot_general x5 -> x12, matrix products: 23.3 us -> 55.8 us  [section_forward(): jnp.dot(spatial_columns(normed), spatial, preferred_element_type=jnp.floa...]
  transfers between devices with their start and end apart: 30 -> 26, of which waited for: 27 -> 26; matrix products, arithmetic and copies ran while one was open for 1% -> 1% of each run, Pallas kernels for 0% -> 0%
where the time goes in v1:
time: 938 us; the launch traced here: 931 us
  waiting for transfers between devices  427 us (46%)
  matrix products  167 us (18%)
  local copies, waits for them, and re-layouts  114 us (12%)
  starting transfers between devices  109 us (12%)
  other arithmetic  80.2 us (9%)
  loops' own time  18.8 us (2%)
  between operations  14.3 us (2%)
    reduce_scatter x1, waiting for transfers between devices, per_device(): lax.psum_scatter(partial_rows, 'dp', scatter_dimension=0, tiled=False)  208 us
    ppermute x24, waiting for transfers between devices, passed_along(): lax.ppermute(value, axis, [(source, source + steps) for source in range(f...  143 us
    ppermute x24, starting transfers between devices, passed_along(): lax.ppermute(value, axis, [(source, source + steps) for source in range(f...  109 us
    all_gather x1, waiting for transfers between devices, per_device(): gathered = lax.all_gather(own_rows, 'dp', axis=0, tiled=False)  76.1 us
    dot_general x12, matrix products, section_backward(): jnp.dot(pre_grad.reshape(frames * pixels, channels), spatial.T, preferred...  63.8 us
    dynamic_update_slice x48, other arithmetic, stash_put(): return lax.dynamic_update_index_in_dim(stash, value, slot, 0)  60 us
    dot_general x12, matrix products, section_forward(): jnp.dot(spatial_columns(normed), spatial, preferred_element_type=jnp.floa...  55.8 us
    dot_general x12, matrix products, section_backward(): jnp.dot(upstream_flat, temporal.T, preferred_element_type=jnp.float32)  30.3 us
  transfers between devices with their start and end apart: 26, of which 26 were waited for; matrix products, arithmetic and copies ran while one was open for 1% of the time, Pallas kernels for 0%

profile of v1, /device:TPU:1, one launch (start us, length us, event | category | flops | bytes accessed | tf_op | source)
XLA Modules:
  0.0 930.9 jit_solution(14521185738409171667)
XLA Ops:
  9.9 76.1 %all-gather.3.cloned.1.call-done = bf16[7680,640]{1,0:T(8,128)(2,1)} async-done(((bf16[240,640]{1,0:T(8,128)(2,1)}), bf16[7680,640]{1,0:T(8,128)(2,1)}) %all-gather.3.cloned.1.call-update) | async-done | bytes 9830416 | tf_op jit(solution)/shard_map/all_gather | solution.py:125
  109.5 226.6 %while.37 = (s32[]{:T(128)}, bf16[3,32,640]{2,1,0:T(8,128)(2,1)S(1)}, bf16[7,3,32,640]{3,2,1,0:T(8,128)(2,1)S(1)}, bf16[7,3,32,640]{3,2,1,0:T(8,128)(2,1)}, f32[...) while((s32[]{:T(128)}, ...), condition=%wide.region_2.3_spmd, body=%wide.region_0.2_spmd.sunk | while | flops 945868928 | bytes 29872000 | solution.py:163
  178.2 10.1 %collective-permute-start = (bf16[3,32,640]{2,1,0:T(8,128)(2,1)S(1)}, bf16[3,32,640]{2,1,0:T(8,128)(2,1)S(1)}, u32[]{:S(2)}, u32[]{:S(2)}) collective-permute-start(bf16[3,32,640]{2,1,0:T(8,128)(2,1)S(1)} %fusion.69), channel_id=1, source_target_pairs={{0,32},{32,64},{64,96},{96,128},{128,160},{160,192},{192,224},{1,3... | collective-permute-start | bytes 368648 | tf_op jit(solution)/shard_map/while/body/eval_jaxpr/ppermute | solution.py:15
  199.4 9.7 %collective-permute-start = (bf16[3,32,640]{2,1,0:T(8,128)(2,1)S(1)}, bf16[3,32,640]{2,1,0:T(8,128)(2,1)S(1)}, u32[]{:S(2)}, u32[]{:S(2)}) collective-permute-start(bf16[3,32,640]{2,1,0:T(8,128)(2,1)S(1)} %fusion.69), channel_id=1, source_target_pairs={{0,32},{32,64},{64,96},{96,128},{128,160},{160,192},{192,224},{1,3... | collective-permute-start | bytes 368648 | tf_op jit(solution)/shard_map/while/body/eval_jaxpr/ppermute | solution.py:15
  220.2 9.8 %collective-permute-start = (bf16[3,32,640]{2,1,0:T(8,128)(2,1)S(1)}, bf16[3,32,640]{2,1,0:T(8,128)(2,1)S(1)}, u32[]{:S(2)}, u32[]{:S(2)}) collective-permute-start(bf16[3,32,640]{2,1,0:T(8,128)(2,1)S(1)} %fusion.69), channel_id=1, source_target_pairs={{0,32},{32,64},{64,96},{96,128},{128,160},{160,192},{192,224},{1,3... | collective-permute-start | bytes 368648 | tf_op jit(solution)/shard_map/while/body/eval_jaxpr/ppermute | solution.py:15
  241.1 9.8 %collective-permute-start = (bf16[3,32,640]{2,1,0:T(8,128)(2,1)S(1)}, bf16[3,32,640]{2,1,0:T(8,128)(2,1)S(1)}, u32[]{:S(2)}, u32[]{:S(2)}) collective-permute-start(bf16[3,32,640]{2,1,0:T(8,128)(2,1)S(1)} %fusion.69), channel_id=1, source_target_pairs={{0,32},{32,64},{64,96},{96,128},{128,160},{160,192},{192,224},{1,3... | collective-permute-start | bytes 368648 | tf_op jit(solution)/shard_map/while/body/eval_jaxpr/ppermute | solution.py:15
  261.9 9.8 %collective-permute-start = (bf16[3,32,640]{2,1,0:T(8,128)(2,1)S(1)}, bf16[3,32,640]{2,1,0:T(8,128)(2,1)S(1)}, u32[]{:S(2)}, u32[]{:S(2)}) collective-permute-start(bf16[3,32,640]{2,1,0:T(8,128)(2,1)S(1)} %fusion.69), channel_id=1, source_target_pairs={{0,32},{32,64},{64,96},{96,128},{128,160},{160,192},{192,224},{1,3... | collective-permute-start | bytes 368648 | tf_op jit(solution)/shard_map/while/body/eval_jaxpr/ppermute | solution.py:15
  282.8 9.8 %collective-permute-start = (bf16[3,32,640]{2,1,0:T(8,128)(2,1)S(1)}, bf16[3,32,640]{2,1,0:T(8,128)(2,1)S(1)}, u32[]{:S(2)}, u32[]{:S(2)}) collective-permute-start(bf16[3,32,640]{2,1,0:T(8,128)(2,1)S(1)} %fusion.69), channel_id=1, source_target_pairs={{0,32},{32,64},{64,96},{96,128},{128,160},{160,192},{192,224},{1,3... | collective-permute-start | bytes 368648 | tf_op jit(solution)/shard_map/while/body/eval_jaxpr/ppermute | solution.py:15
  303.6 9.8 %collective-permute-start = (bf16[3,32,640]{2,1,0:T(8,128)(2,1)S(1)}, bf16[3,32,640]{2,1,0:T(8,128)(2,1)S(1)}, u32[]{:S(2)}, u32[]{:S(2)}) collective-permute-start(bf16[3,32,640]{2,1,0:T(8,128)(2,1)S(1)} %fusion.69), channel_id=1, source_target_pairs={{0,32},{32,64},{64,96},{96,128},{128,160},{160,192},{192,224},{1,3... | collective-permute-start | bytes 368648 | tf_op jit(solution)/shard_map/while/body/eval_jaxpr/ppermute | solution.py:15
  324.5 9.8 %collective-permute-start = (bf16[3,32,640]{2,1,0:T(8,128)(2,1)S(1)}, bf16[3,32,640]{2,1,0:T(8,128)(2,1)S(1)}, u32[]{:S(2)}, u32[]{:S(2)}) collective-permute-start(bf16[3,32,640]{2,1,0:T(8,128)(2,1)S(1)} %fusion.69), channel_id=1, source_target_pairs={{0,32},{32,64},{64,96},{96,128},{128,160},{160,192},{192,224},{1,3... | collective-permute-start | bytes 368648 | tf_op jit(solution)/shard_map/while/body/eval_jaxpr/ppermute | solution.py:15
  338.2 309.8 %while.38 = (s32[]{:T(128)}, bf16[3,32,640]{2,1,0:T(8,128)(2,1)S(1)}, bf16[7,3,32,640]{3,2,1,0:T(8,128)(2,1)}, bf16[7,3,32,640]{3,2,1,0:T(8,128)(2,1)}, pred[]{:...) while((s32[]{:T(128)}, ...), condition=%wide.region_6.7_spmd, body=%wide.region_3.6_spmd.sunk | while | flops 946099520 | bytes 27389848 | solution.py:189
  353.2 10.7 %collective-permute-done.1 = bf16[3,32,640]{2,1,0:T(8,128)(2,1)S(1)} collective-permute-done((bf16[3,32,640]{2,1,0:T(8,128)(2,1)S(1)}, bf16[3,32,640]{2,1,0:T(8,128)(2,1)S(1)}, u32[]{:S(2)}, u32[]{:S(2)}) %collective-permute-start.1) | collective-permute-done | bytes 122912 | tf_op jit(solution)/shard_map/while/body/eval_jaxpr/ppermute | solution.py:15
  379.0 10.7 %collective-permute-done.1 = bf16[3,32,640]{2,1,0:T(8,128)(2,1)S(1)} collective-permute-done((bf16[3,32,640]{2,1,0:T(8,128)(2,1)S(1)}, bf16[3,32,640]{2,1,0:T(8,128)(2,1)S(1)}, u32[]{:S(2)}, u32[]{:S(2)}) %collective-permute-start.1) | collective-permute-done | bytes 122912 | tf_op jit(solution)/shard_map/while/body/eval_jaxpr/ppermute | solution.py:15
  404.8 10.8 %collective-permute-done.1 = bf16[3,32,640]{2,1,0:T(8,128)(2,1)S(1)} collective-permute-done((bf16[3,32,640]{2,1,0:T(8,128)(2,1)S(1)}, bf16[3,32,640]{2,1,0:T(8,128)(2,1)S(1)}, u32[]{:S(2)}, u32[]{:S(2)}) %collective-permute-start.1) | collective-permute-done | bytes 122912 | tf_op jit(solution)/shard_map/while/body/eval_jaxpr/ppermute | solution.py:15
  430.7 10.7 %collective-permute-done.1 = bf16[3,32,640]{2,1,0:T(8,128)(2,1)S(1)} collective-permute-done((bf16[3,32,640]{2,1,0:T(8,128)(2,1)S(1)}, bf16[3,32,640]{2,1,0:T(8,128)(2,1)S(1)}, u32[]{:S(2)}, u32[]{:S(2)}) %collective-permute-start.1) | collective-permute-done | bytes 122912 | tf_op jit(solution)/shard_map/while/body/eval_jaxpr/ppermute | solution.py:15
  456.5 10.3 %collective-permute-done.1 = bf16[3,32,640]{2,1,0:T(8,128)(2,1)S(1)} collective-permute-done((bf16[3,32,640]{2,1,0:T(8,128)(2,1)S(1)}, bf16[3,32,640]{2,1,0:T(8,128)(2,1)S(1)}, u32[]{:S(2)}, u32[]{:S(2)}) %collective-permute-start.1) | collective-permute-done | bytes 122912 | tf_op jit(solution)/shard_map/while/body/eval_jaxpr/ppermute | solution.py:15
  481.9 10.3 %collective-permute-done.1 = bf16[3,32,640]{2,1,0:T(8,128)(2,1)S(1)} collective-permute-done((bf16[3,32,640]{2,1,0:T(8,128)(2,1)S(1)}, bf16[3,32,640]{2,1,0:T(8,128)(2,1)S(1)}, u32[]{:S(2)}, u32[]{:S(2)}) %collective-permute-start.1) | collective-permute-done | bytes 122912 | tf_op jit(solution)/shard_map/while/body/eval_jaxpr/ppermute | solution.py:15
  507.3 10.4 %collective-permute-done.1 = bf16[3,32,640]{2,1,0:T(8,128)(2,1)S(1)} collective-permute-done((bf16[3,32,640]{2,1,0:T(8,128)(2,1)S(1)}, bf16[3,32,640]{2,1,0:T(8,128)(2,1)S(1)}, u32[]{:S(2)}, u32[]{:S(2)}) %collective-permute-start.1) | collective-permute-done | bytes 122912 | tf_op jit(solution)/shard_map/while/body/eval_jaxpr/ppermute | solution.py:15
  532.7 10.3 %collective-permute-done.1 = bf16[3,32,640]{2,1,0:T(8,128)(2,1)S(1)} collective-permute-done((bf16[3,32,640]{2,1,0:T(8,128)(2,1)S(1)}, bf16[3,32,640]{2,1,0:T(8,128)(2,1)S(1)}, u32[]{:S(2)}, u32[]{:S(2)}) %collective-permute-start.1) | collective-permute-done | bytes 122912 | tf_op jit(solution)/shard_map/while/body/eval_jaxpr/ppermute | solution.py:15
  558.1 10.4 %collective-permute-done.1 = bf16[3,32,640]{2,1,0:T(8,128)(2,1)S(1)} collective-permute-done((bf16[3,32,640]{2,1,0:T(8,128)(2,1)S(1)}, bf16[3,32,640]{2,1,0:T(8,128)(2,1)S(1)}, u32[]{:S(2)}, u32[]{:S(2)}) %collective-permute-start.1) | collective-permute-done | bytes 122912 | tf_op jit(solution)/shard_map/while/body/eval_jaxpr/ppermute | solution.py:15
  583.5 10.3 %collective-permute-done.1 = bf16[3,32,640]{2,1,0:T(8,128)(2,1)S(1)} collective-permute-done((bf16[3,32,640]{2,1,0:T(8,128)(2,1)S(1)}, bf16[3,32,640]{2,1,0:T(8,128)(2,1)S(1)}, u32[]{:S(2)}, u32[]{:S(2)}) %collective-permute-start.1) | collective-permute-done | bytes 122912 | tf_op jit(solution)/shard_map/while/body/eval_jaxpr/ppermute | solution.py:15
  608.9 11.4 %collective-permute-done.1 = bf16[3,32,640]{2,1,0:T(8,128)(2,1)S(1)} collective-permute-done((bf16[3,32,640]{2,1,0:T(8,128)(2,1)S(1)}, bf16[3,32,640]{2,1,0:T(8,128)(2,1)S(1)}, u32[]{:S(2)}, u32[]{:S(2)}) %collective-permute-start.1) | collective-permute-done | bytes 122912 | tf_op jit(solution)/shard_map/while/body/eval_jaxpr/ppermute | solution.py:15
  635.4 12.5 %collective-permute-done.1 = bf16[3,32,640]{2,1,0:T(8,128)(2,1)S(1)} collective-permute-done((bf16[3,32,640]{2,1,0:T(8,128)(2,1)S(1)}, bf16[3,32,640]{2,1,0:T(8,128)(2,1)S(1)}, u32[]{:S(2)}, u32[]{:S(2)}) %collective-permute-start.1) | collective-permute-done | bytes 122912 | tf_op jit(solution)/shard_map/while/body/eval_jaxpr/ppermute | solution.py:15
  711.7 208.4 %reduce-scatter.2.cloned.1.call-done = bf16[1,240,640]{2,1,0:T(8,128)(2,1)} async-done(((bf16[32,240,640]{2,1,0:T(8,128)(2,1)}), bf16[1,240,640]{2,1,0:T(8,128)(2,1)}) %reduce-scatter.2.cloned.1.call-update) | async-done | bytes 307216 | tf_op jit(solution)/shard_map/reduce_scatter | solution.py:210
  (711 shorter events, 405.9 us)
Async XLA Ops:
  7.2 78.9 %all-gather.3.cloned.1.call-start = ((), (), s32[]{:S(2)}) async-start(), calls=%async_computation.2 | async-start | bytes 10137600 | tf_op jit(solution)/shard_map/all_gather | solution.py:125
  9.0 911.1 %reduce-scatter.2.cloned.1.call-start = ((), (), s32[]{:S(2)}) async-start(), calls=%async_computation.1 | async-start | bytes 10137600 | tf_op jit(solution)/shard_map/reduce_scatter | solution.py:210
  133.4 6.0 collective-permute-start
  148.5 5.6 collective-permute-start
  178.2 11.9 %collective-permute-start = (bf16[3,32,640]{2,1,0:T(8,128)(2,1)S(1)}, bf16[3,32,640]{2,1,0:T(8,128)(2,1)S(1)}, u32[]{:S(2)}, u32[]{:S(2)}) collective-permute-start(bf16[3,32,640]{2,1,0:T(8,128)(2,1)S(1)} %fusion.69), channel_id=1, source_target_pairs={{0,32},{32,64},{64,96},{96,128},{128,160},{160,192},{192,224},{1,3... | collective-permute-start | bytes 368648 | tf_op jit(solution)/shard_map/while/body/eval_jaxpr/ppermute | solution.py:15
  199.4 11.6 %collective-permute-start = (bf16[3,32,640]{2,1,0:T(8,128)(2,1)S(1)}, bf16[3,32,640]{2,1,0:T(8,128)(2,1)S(1)}, u32[]{:S(2)}, u32[]{:S(2)}) collective-permute-start(bf16[3,32,640]{2,1,0:T(8,128)(2,1)S(1)} %fusion.69), channel_id=1, source_target_pairs={{0,32},{32,64},{64,96},{96,128},{128,160},{160,192},{192,224},{1,3... | collective-permute-start | bytes 368648 | tf_op jit(solution)/shard_map/while/body/eval_jaxpr/ppermute | solution.py:15
  220.2 11.7 %collective-permute-start = (bf16[3,32,640]{2,1,0:T(8,128)(2,1)S(1)}, bf16[3,32,640]{2,1,0:T(8,128)(2,1)S(1)}, u32[]{:S(2)}, u32[]{:S(2)}) collective-permute-start(bf16[3,32,640]{2,1,0:T(8,128)(2,1)S(1)} %fusion.69), channel_id=1, source_target_pairs={{0,32},{32,64},{64,96},{96,128},{128,160},{160,192},{192,224},{1,3... | collective-permute-start | bytes 368648 | tf_op jit(solution)/shard_map/while/body/eval_jaxpr/ppermute | solution.py:15
  241.1 11.6 %collective-permute-start = (bf16[3,32,640]{2,1,0:T(8,128)(2,1)S(1)}, bf16[3,32,640]{2,1,0:T(8,128)(2,1)S(1)}, u32[]{:S(2)}, u32[]{:S(2)}) collective-permute-start(bf16[3,32,640]{2,1,0:T(8,128)(2,1)S(1)} %fusion.69), channel_id=1, source_target_pairs={{0,32},{32,64},{64,96},{96,128},{128,160},{160,192},{192,224},{1,3... | collective-permute-start | bytes 368648 | tf_op jit(solution)/shard_map/while/body/eval_jaxpr/ppermute | solution.py:15
  261.9 11.7 %collective-permute-start = (bf16[3,32,640]{2,1,0:T(8,128)(2,1)S(1)}, bf16[3,32,640]{2,1,0:T(8,128)(2,1)S(1)}, u32[]{:S(2)}, u32[]{:S(2)}) collective-permute-start(bf16[3,32,640]{2,1,0:T(8,128)(2,1)S(1)} %fusion.69), channel_id=1, source_target_pairs={{0,32},{32,64},{64,96},{96,128},{128,160},{160,192},{192,224},{1,3... | collective-permute-start | bytes 368648 | tf_op jit(solution)/shard_map/while/body/eval_jaxpr/ppermute | solution.py:15
  282.8 11.6 %collective-permute-start = (bf16[3,32,640]{2,1,0:T(8,128)(2,1)S(1)}, bf16[3,32,640]{2,1,0:T(8,128)(2,1)S(1)}, u32[]{:S(2)}, u32[]{:S(2)}) collective-permute-start(bf16[3,32,640]{2,1,0:T(8,128)(2,1)S(1)} %fusion.69), channel_id=1, source_target_pairs={{0,32},{32,64},{64,96},{96,128},{128,160},{160,192},{192,224},{1,3... | collective-permute-start | bytes 368648 | tf_op jit(solution)/shard_map/while/body/eval_jaxpr/ppermute | solution.py:15
  303.6 11.6 %collective-permute-start = (bf16[3,32,640]{2,1,0:T(8,128)(2,1)S(1)}, bf16[3,32,640]{2,1,0:T(8,128)(2,1)S(1)}, u32[]{:S(2)}, u32[]{:S(2)}) collective-permute-start(bf16[3,32,640]{2,1,0:T(8,128)(2,1)S(1)} %fusion.69), channel_id=1, source_target_pairs={{0,32},{32,64},{64,96},{96,128},{128,160},{160,192},{192,224},{1,3... | collective-permute-start | bytes 368648 | tf_op jit(solution)/shard_map/while/body/eval_jaxpr/ppermute | solution.py:15
  324.5 11.6 %collective-permute-start = (bf16[3,32,640]{2,1,0:T(8,128)(2,1)S(1)}, bf16[3,32,640]{2,1,0:T(8,128)(2,1)S(1)}, u32[]{:S(2)}, u32[]{:S(2)}) collective-permute-start(bf16[3,32,640]{2,1,0:T(8,128)(2,1)S(1)} %fusion.69), channel_id=1, source_target_pairs={{0,32},{32,64},{64,96},{96,128},{128,160},{160,192},{192,224},{1,3... | collective-permute-start | bytes 368648 | tf_op jit(solution)/shard_map/while/body/eval_jaxpr/ppermute | solution.py:15
  351.9 12.0 %collective-permute-start.1 = (bf16[3,32,640]{2,1,0:T(8,128)(2,1)S(1)}, bf16[3,32,640]{2,1,0:T(8,128)(2,1)S(1)}, u32[]{:S(2)}, u32[]{:S(2)}) collective-permute-start(bf16[3,32,640]{2,1,0:T(8,128)(2,1)S(1)} %fusion.78), channel_id=1, source_target_pairs={{32,0},{64,32},{96,64},{128,96},{160,128},{192,160},{224,192},{33,... | collective-permute-start | bytes 368648 | tf_op jit(solution)/shard_map/while/body/eval_jaxpr/ppermute | solution.py:15
  377.7 12.0 %collective-permute-start.1 = (bf16[3,32,640]{2,1,0:T(8,128)(2,1)S(1)}, bf16[3,32,640]{2,1,0:T(8,128)(2,1)S(1)}, u32[]{:S(2)}, u32[]{:S(2)}) collective-permute-start(bf16[3,32,640]{2,1,0:T(8,128)(2,1)S(1)} %fusion.78), channel_id=1, source_target_pairs={{32,0},{64,32},{96,64},{128,96},{160,128},{192,160},{224,192},{33,... | collective-permute-start | bytes 368648 | tf_op jit(solution)/shard_map/while/body/eval_jaxpr/ppermute | solution.py:15
  403.5 12.1 %collective-permute-start.1 = (bf16[3,32,640]{2,1,0:T(8,128)(2,1)S(1)}, bf16[3,32,640]{2,1,0:T(8,128)(2,1)S(1)}, u32[]{:S(2)}, u32[]{:S(2)}) collective-permute-start(bf16[3,32,640]{2,1,0:T(8,128)(2,1)S(1)} %fusion.78), channel_id=1, source_target_pairs={{32,0},{64,32},{96,64},{128,96},{160,128},{192,160},{224,192},{33,... | collective-permute-start | bytes 368648 | tf_op jit(solution)/shard_map/while/body/eval_jaxpr/ppermute | solution.py:15
  429.4 12.0 %collective-permute-start.1 = (bf16[3,32,640]{2,1,0:T(8,128)(2,1)S(1)}, bf16[3,32,640]{2,1,0:T(8,128)(2,1)S(1)}, u32[]{:S(2)}, u32[]{:S(2)}) collective-permute-start(bf16[3,32,640]{2,1,0:T(8,128)(2,1)S(1)} %fusion.78), channel_id=1, source_target_pairs={{32,0},{64,32},{96,64},{128,96},{160,128},{192,160},{224,192},{33,... | collective-permute-start | bytes 368648 | tf_op jit(solution)/shard_map/while/body/eval_jaxpr/ppermute | solution.py:15
  455.2 11.6 %collective-permute-start.1 = (bf16[3,32,640]{2,1,0:T(8,128)(2,1)S(1)}, bf16[3,32,640]{2,1,0:T(8,128)(2,1)S(1)}, u32[]{:S(2)}, u32[]{:S(2)}) collective-permute-start(bf16[3,32,640]{2,1,0:T(8,128)(2,1)S(1)} %fusion.78), channel_id=1, source_target_pairs={{32,0},{64,32},{96,64},{128,96},{160,128},{192,160},{224,192},{33,... | collective-permute-start | bytes 368648 | tf_op jit(solution)/shard_map/while/body/eval_jaxpr/ppermute | solution.py:15
  480.6 11.6 %collective-permute-start.1 = (bf16[3,32,640]{2,1,0:T(8,128)(2,1)S(1)}, bf16[3,32,640]{2,1,0:T(8,128)(2,1)S(1)}, u32[]{:S(2)}, u32[]{:S(2)}) collective-permute-start(bf16[3,32,640]{2,1,0:T(8,128)(2,1)S(1)} %fusion.78), channel_id=1, source_target_pairs={{32,0},{64,32},{96,64},{128,96},{160,128},{192,160},{224,192},{33,... | collective-permute-start | bytes 368648 | tf_op jit(solution)/shard_map/while/body/eval_jaxpr/ppermute | solution.py:15
  506.0 11.7 %collective-permute-start.1 = (bf16[3,32,640]{2,1,0:T(8,128)(2,1)S(1)}, bf16[3,32,640]{2,1,0:T(8,128)(2,1)S(1)}, u32[]{:S(2)}, u32[]{:S(2)}) collective-permute-start(bf16[3,32,640]{2,1,0:T(8,128)(2,1)S(1)} %fusion.78), channel_id=1, source_target_pairs={{32,0},{64,32},{96,64},{128,96},{160,128},{192,160},{224,192},{33,... | collective-permute-start | bytes 368648 | tf_op jit(solution)/shard_map/while/body/eval_jaxpr/ppermute | solution.py:15
  531.4 11.6 %collective-permute-start.1 = (bf16[3,32,640]{2,1,0:T(8,128)(2,1)S(1)}, bf16[3,32,640]{2,1,0:T(8,128)(2,1)S(1)}, u32[]{:S(2)}, u32[]{:S(2)}) collective-permute-start(bf16[3,32,640]{2,1,0:T(8,128)(2,1)S(1)} %fusion.78), channel_id=1, source_target_pairs={{32,0},{64,32},{96,64},{128,96},{160,128},{192,160},{224,192},{33,... | collective-permute-start | bytes 368648 | tf_op jit(solution)/shard_map/while/body/eval_jaxpr/ppermute | solution.py:15
  556.8 11.7 %collective-permute-start.1 = (bf16[3,32,640]{2,1,0:T(8,128)(2,1)S(1)}, bf16[3,32,640]{2,1,0:T(8,128)(2,1)S(1)}, u32[]{:S(2)}, u32[]{:S(2)}) collective-permute-start(bf16[3,32,640]{2,1,0:T(8,128)(2,1)S(1)} %fusion.78), channel_id=1, source_target_pairs={{32,0},{64,32},{96,64},{128,96},{160,128},{192,160},{224,192},{33,... | collective-permute-start | bytes 368648 | tf_op jit(solution)/shard_map/while/body/eval_jaxpr/ppermute | solution.py:15
  582.2 11.6 %collective-permute-start.1 = (bf16[3,32,640]{2,1,0:T(8,128)(2,1)S(1)}, bf16[3,32,640]{2,1,0:T(8,128)(2,1)S(1)}, u32[]{:S(2)}, u32[]{:S(2)}) collective-permute-start(bf16[3,32,640]{2,1,0:T(8,128)(2,1)S(1)} %fusion.78), channel_id=1, source_target_pairs={{32,0},{64,32},{96,64},{128,96},{160,128},{192,160},{224,192},{33,... | collective-permute-start | bytes 368648 | tf_op jit(solution)/shard_map/while/body/eval_jaxpr/ppermute | solution.py:15
  607.6 12.7 %collective-permute-start.1 = (bf16[3,32,640]{2,1,0:T(8,128)(2,1)S(1)}, bf16[3,32,640]{2,1,0:T(8,128)(2,1)S(1)}, u32[]{:S(2)}, u32[]{:S(2)}) collective-permute-start(bf16[3,32,640]{2,1,0:T(8,128)(2,1)S(1)} %fusion.78), channel_id=1, source_target_pairs={{32,0},{64,32},{96,64},{128,96},{160,128},{192,160},{224,192},{33,... | collective-permute-start | bytes 368648 | tf_op jit(solution)/shard_map/while/body/eval_jaxpr/ppermute | solution.py:15
  634.1 13.8 %collective-permute-start.1 = (bf16[3,32,640]{2,1,0:T(8,128)(2,1)S(1)}, bf16[3,32,640]{2,1,0:T(8,128)(2,1)S(1)}, u32[]{:S(2)}, u32[]{:S(2)}) collective-permute-start(bf16[3,32,640]{2,1,0:T(8,128)(2,1)S(1)} %fusion.78), channel_id=1, source_target_pairs={{32,0},{64,32},{96,64},{128,96},{160,128},{192,160},{224,192},{33,... | collective-permute-start | bytes 368648 | tf_op jit(solution)/shard_map/while/body/eval_jaxpr/ppermute | solution.py:15
  (22 other events, 81.3 us)
Sparse Core Ops, SparseCore 0:
  10.4 75.5 all-gather.2
  711.8 208.2 reduce-scatter.1

commit v2 on v1

--- a/solution.py
+++ b/solution.py
@@ -112,7 +112,9 @@
 
 def per_device(samples, timesteps, cotangent, spatial_weight, temporal_weight):
     sections = lax.axis_size("pipe")
-    n_dp = lax.axis_size("dp")
+    n_outer = lax.axis_size("dpo")
+    n_core = lax.axis_size("core")
+    n_dp = n_outer * n_core
     section_index = lax.axis_index("pipe")
     micro_count = samples.shape[0]
     frames, pixels, channels = (samples.shape[1], samples.shape[2], samples.shape[3])
@@ -122,7 +124,9 @@
     sp_rows = spatial_weight.shape[1]
     tm_rows = temporal_weight.shape[1]
     own_rows = jnp.concatenate([spatial_weight[0], temporal_weight[0]], axis=0)
-    gathered = lax.all_gather(own_rows, "dp", axis=0, tiled=False)
+    gathered = lax.all_gather(own_rows, "dpo", axis=0, tiled=False)
+    gathered = lax.all_gather(gathered, "core", axis=1, tiled=False)
+    gathered = gathered.reshape((n_dp,) + own_rows.shape)
     full_spatial = gathered[:, :sp_rows].reshape(n_dp * sp_rows, channels)
     full_temporal = gathered[:, sp_rows:].reshape(n_dp * tm_rows, channels)
 
@@ -207,22 +211,28 @@
         ],
         axis=1,
     )
-    share = lax.psum_scatter(partial_rows, "dp", scatter_dimension=0, tiled=False)
+    partial_rows = partial_rows.reshape((n_outer, n_core) + partial_rows.shape[1:])
+    partial_rows = jnp.swapaxes(partial_rows, 0, 1)
+    share = lax.psum_scatter(partial_rows, "core", scatter_dimension=0, tiled=False)
+    share = lax.psum_scatter(share, "dpo", scatter_dimension=0, tiled=False)
     share = share.astype(jnp.float32)
     return (share[None, :sp_rows], share[None, sp_rows:])
 
 
 def solution(mesh):
+    n_pipe, n_dp = mesh.devices.shape
+    split = jax.sharding.Mesh(mesh.devices.reshape(n_pipe, n_dp // 2, 2), ("pipe", "dpo", "core"))
+    dp = ("dpo", "core")
     return jax.shard_map(
         per_device,
-        mesh=mesh,
+        mesh=split,
         in_specs=(
-            P("dp", None, None, None),
-            P("dp"),
-            P("dp", None, None, None),
-            P("pipe", "dp", None),
-            P("pipe", "dp", None),
+            P(dp, None, None, None),
+            P(dp),
+            P(dp, None, None, None),
+            P("pipe", dp, None),
+            P("pipe", dp, None),
         ),
-        out_specs=(P("pipe", "dp", None), P("pipe", "dp", None)),
+        out_specs=(P("pipe", dp, None), P("pipe", dp, None)),
         check_vma=False,
     )

time: 938 us -> 1020 us (1.087)
  waiting for transfers between devices: 427 us -> 508 us
    unnamed x2 -> x5, waiting for transfers between devices: 0.03 us -> 99 us
    reduce_scatter x1, waiting for transfers between devices: 208 us -> 118 us  [per_device(): share = lax.psum_scatter(share, 'dpo', scatter_dimension=0, tiled=False)]
    all_gather x1 -> x2, waiting for transfers between devices: 76.1 us -> 148 us  [the longest x1 121 us: per_device(): gathered = lax.all_gather(own_rows, 'dpo', axis=0, tiled=False)]
    reshape x2 -> x0, local copies, waits for them, and re-layouts: 11.4 us -> none  [the longest x1 8.76 us: per_device(): spatial_term.astype(jnp.bfloat16).reshape(n_dp, sp_rows, channels)]
    concatenate x0 -> x2, local copies, waits for them, and re-layouts: none -> 11.4 us  [per_device(): jnp.concatenate([spatial_term.astype(jnp.bfloat16).reshape(n_dp, sp_rows,...]
  transfers between devices with their start and end apart: 26 -> 28, of which waited for: 26 -> 28; matrix products, arithmetic and copies ran while one was open for 1% -> 1% of each run, Pallas kernels for 0% -> 0%
where the time goes in v2:
time: 1020 us
  waiting for transfers between devices  508 us (50%)
  matrix products  167 us (16%)
  local copies, waits for them, and re-layouts  122 us (12%)
  starting transfers between devices  110 us (11%)
  other arithmetic  79.6 us (8%)
  loops' own time  18.6 us (2%)
  between operations  14 us (1%)
    ppermute x24, waiting for transfers between devices, passed_along(): lax.ppermute(value, axis, [(source, source + steps) for source in range(f...  142 us
    all_gather x1, waiting for transfers between devices, per_device(): gathered = lax.all_gather(own_rows, 'dpo', axis=0, tiled=False)  121 us
    reduce_scatter x1, waiting for transfers between devices, per_device(): share = lax.psum_scatter(share, 'dpo', scatter_dimension=0, tiled=False)  118 us
    ppermute x24, starting transfers between devices, passed_along(): lax.ppermute(value, axis, [(source, source + steps) for source in range(f...  110 us
    unnamed x5, waiting for transfers between devices  99 us
    dot_general x12, matrix products, section_backward(): jnp.dot(pre_grad.reshape(frames * pixels, channels), spatial.T, preferred...  63.8 us
    dynamic_update_slice x48, other arithmetic, stash_put(): return lax.dynamic_update_index_in_dim(stash, value, slot, 0)  60.1 us
    dot_general x12, matrix products, section_forward(): jnp.dot(spatial_columns(normed), spatial, preferred_element_type=jnp.floa...  55.8 us
  transfers between devices with their start and end apart: 28, of which 28 were waited for; matrix products, arithmetic and copies ran while one was open for 1% of the time, Pallas kernels for 0%

profile of v2, /device:TPU:1, one launch (start us, length us, event | category | flops | bytes accessed | tf_op | source)
XLA Modules:
  0.0 1019.5 jit_solution(12095437643285979383)
XLA Ops:
  9.0 121.3 %all-gather.5.cloned.1.call-done = bf16[3840,640]{1,0:T(8,128)(2,1)} async-done(((bf16[240,640]{1,0:T(8,128)(2,1)}), bf16[3840,640]{1,0:T(8,128)(2,1)}) %all-gather.5.cloned.1.call-update) | async-done | bytes 4915216 | tf_op jit(solution)/shard_map/all_gather | solution.py:127
  130.7 27.1 %all-gather.7.cloned.1.call-done = bf16[16,480,640]{2,1,0:T(8,128)(2,1)} async-done(((bf16[16,240,640]{2,1,0:T(8,128)(2,1)}), bf16[16,480,640]{2,1,0:T(8,128)(2,1)}) %all-gather.7.cloned.1.call-update) | async-done | bytes 9830416 | tf_op jit(solution)/shard_map/all_gather | solution.py:128
  181.3 228.3 %while.37 = (s32[]{:T(128)}, bf16[3,32,640]{2,1,0:T(8,128)(2,1)S(1)}, bf16[7,3,32,640]{3,2,1,0:T(8,128)(2,1)S(1)}, bf16[7,3,32,640]{3,2,1,0:T(8,128)(2,1)}, f32[...) while((s32[]{:T(128)}, ...), condition=%wide.region_2.3_spmd, body=%wide.region_0.2_spmd.sunk | while | flops 945868928 | bytes 29872000 | solution.py:167
  251.5 10.1 collective-permute-start
  272.8 9.8 collective-permute-start
  293.6 9.8 collective-permute-start
  335.4 9.8 collective-permute-start
  356.2 9.8 collective-permute-start
  377.1 9.8 collective-permute-start
  411.7 309.1 %while.38 = (s32[]{:T(128)}, bf16[3,32,640]{2,1,0:T(8,128)(2,1)S(1)}, bf16[7,3,32,640]{3,2,1,0:T(8,128)(2,1)}, bf16[7,3,32,640]{3,2,1,0:T(8,128)(2,1)}, pred[]{:...) while((s32[]{:T(128)}, ...), condition=%wide.region_6.7_spmd, body=%wide.region_3.6_spmd.sunk | while | flops 946099520 | bytes 27389848 | solution.py:193
  426.8 10.8 %collective-permute-done.1 = bf16[3,32,640]{2,1,0:T(8,128)(2,1)S(1)} collective-permute-done((bf16[3,32,640]{2,1,0:T(8,128)(2,1)S(1)}, bf16[3,32,640]{2,1,0:T(8,128)(2,1)S(1)}, u32[]{:S(2)}, u32[]{:S(2)}) %collective-permute-start.1) | collective-permute-done | bytes 122912 | tf_op jit(solution)/shard_map/while/body/eval_jaxpr/ppermute | solution.py:15
  452.6 10.7 %collective-permute-done.1 = bf16[3,32,640]{2,1,0:T(8,128)(2,1)S(1)} collective-permute-done((bf16[3,32,640]{2,1,0:T(8,128)(2,1)S(1)}, bf16[3,32,640]{2,1,0:T(8,128)(2,1)S(1)}, u32[]{:S(2)}, u32[]{:S(2)}) %collective-permute-start.1) | collective-permute-done | bytes 122912 | tf_op jit(solution)/shard_map/while/body/eval_jaxpr/ppermute | solution.py:15
  478.4 10.7 %collective-permute-done.1 = bf16[3,32,640]{2,1,0:T(8,128)(2,1)S(1)} collective-permute-done((bf16[3,32,640]{2,1,0:T(8,128)(2,1)S(1)}, bf16[3,32,640]{2,1,0:T(8,128)(2,1)S(1)}, u32[]{:S(2)}, u32[]{:S(2)}) %collective-permute-start.1) | collective-permute-done | bytes 122912 | tf_op jit(solution)/shard_map/while/body/eval_jaxpr/ppermute | solution.py:15
  504.2 10.7 %collective-permute-done.1 = bf16[3,32,640]{2,1,0:T(8,128)(2,1)S(1)} collective-permute-done((bf16[3,32,640]{2,1,0:T(8,128)(2,1)S(1)}, bf16[3,32,640]{2,1,0:T(8,128)(2,1)S(1)}, u32[]{:S(2)}, u32[]{:S(2)}) %collective-permute-start.1) | collective-permute-done | bytes 122912 | tf_op jit(solution)/shard_map/while/body/eval_jaxpr/ppermute | solution.py:15
  530.1 10.3 %collective-permute-done.1 = bf16[3,32,640]{2,1,0:T(8,128)(2,1)S(1)} collective-permute-done((bf16[3,32,640]{2,1,0:T(8,128)(2,1)S(1)}, bf16[3,32,640]{2,1,0:T(8,128)(2,1)S(1)}, u32[]{:S(2)}, u32[]{:S(2)}) %collective-permute-start.1) | collective-permute-done | bytes 122912 | tf_op jit(solution)/shard_map/while/body/eval_jaxpr/ppermute | solution.py:15
  555.5 10.3 %collective-permute-done.1 = bf16[3,32,640]{2,1,0:T(8,128)(2,1)S(1)} collective-permute-done((bf16[3,32,640]{2,1,0:T(8,128)(2,1)S(1)}, bf16[3,32,640]{2,1,0:T(8,128)(2,1)S(1)}, u32[]{:S(2)}, u32[]{:S(2)}) %collective-permute-start.1) | collective-permute-done | bytes 122912 | tf_op jit(solution)/shard_map/while/body/eval_jaxpr/ppermute | solution.py:15
  580.9 10.3 %collective-permute-done.1 = bf16[3,32,640]{2,1,0:T(8,128)(2,1)S(1)} collective-permute-done((bf16[3,32,640]{2,1,0:T(8,128)(2,1)S(1)}, bf16[3,32,640]{2,1,0:T(8,128)(2,1)S(1)}, u32[]{:S(2)}, u32[]{:S(2)}) %collective-permute-start.1) | collective-permute-done | bytes 122912 | tf_op jit(solution)/shard_map/while/body/eval_jaxpr/ppermute | solution.py:15
  606.3 10.4 %collective-permute-done.1 = bf16[3,32,640]{2,1,0:T(8,128)(2,1)S(1)} collective-permute-done((bf16[3,32,640]{2,1,0:T(8,128)(2,1)S(1)}, bf16[3,32,640]{2,1,0:T(8,128)(2,1)S(1)}, u32[]{:S(2)}, u32[]{:S(2)}) %collective-permute-start.1) | collective-permute-done | bytes 122912 | tf_op jit(solution)/shard_map/while/body/eval_jaxpr/ppermute | solution.py:15
  631.7 10.3 %collective-permute-done.1 = bf16[3,32,640]{2,1,0:T(8,128)(2,1)S(1)} collective-permute-done((bf16[3,32,640]{2,1,0:T(8,128)(2,1)S(1)}, bf16[3,32,640]{2,1,0:T(8,128)(2,1)S(1)}, u32[]{:S(2)}, u32[]{:S(2)}) %collective-permute-start.1) | collective-permute-done | bytes 122912 | tf_op jit(solution)/shard_map/while/body/eval_jaxpr/ppermute | solution.py:15
  657.1 10.3 %collective-permute-done.1 = bf16[3,32,640]{2,1,0:T(8,128)(2,1)S(1)} collective-permute-done((bf16[3,32,640]{2,1,0:T(8,128)(2,1)S(1)}, bf16[3,32,640]{2,1,0:T(8,128)(2,1)S(1)}, u32[]{:S(2)}, u32[]{:S(2)}) %collective-permute-start.1) | collective-permute-done | bytes 122912 | tf_op jit(solution)/shard_map/while/body/eval_jaxpr/ppermute | solution.py:15
  682.6 11.2 %collective-permute-done.1 = bf16[3,32,640]{2,1,0:T(8,128)(2,1)S(1)} collective-permute-done((bf16[3,32,640]{2,1,0:T(8,128)(2,1)S(1)}, bf16[3,32,640]{2,1,0:T(8,128)(2,1)S(1)}, u32[]{:S(2)}, u32[]{:S(2)}) %collective-permute-start.1) | collective-permute-done | bytes 122912 | tf_op jit(solution)/shard_map/while/body/eval_jaxpr/ppermute | solution.py:15
  708.8 12.0 %collective-permute-done.1 = bf16[3,32,640]{2,1,0:T(8,128)(2,1)S(1)} collective-permute-done((bf16[3,32,640]{2,1,0:T(8,128)(2,1)S(1)}, bf16[3,32,640]{2,1,0:T(8,128)(2,1)S(1)}, u32[]{:S(2)}, u32[]{:S(2)}) %collective-permute-start.1) | collective-permute-done | bytes 122912 | tf_op jit(solution)/shard_map/while/body/eval_jaxpr/ppermute | solution.py:15
  786.1 99.0 %all-reduce.19.cloned.1.call-done = bf16[2,16,240,640]{3,2,0,1:T(8,128)(2,1)} async-done(((bf16[2,16,240,640]{3,2,0,1:T(8,128)(2,1)}), bf16[2,16,240,640]{3,2,0,1:T(8,128)(2,1)}) %all-reduce.19.cloned.1.call-update) | async-done | bytes 9830416
  890.8 118.2 %reduce-scatter.5.cloned.1.call-done = bf16[1,240,640]{2,1,0:T(8,128)(2,1)} async-done(((bf16[16,240,640]{2,1,0:T(8,128)(2,1)}), bf16[1,240,640]{2,1,0:T(8,128)(2,1)}) %reduce-scatter.5.cloned.1.call-update) | async-done | bytes 307216 | tf_op jit(solution)/shard_map/reduce_scatter | solution.py:217
  (723 shorter events, 434.0 us)
Async XLA Ops:
  7.2 123.2 %all-gather.5.cloned.1.call-start = ((), (), s32[]{:S(2)}) async-start(), calls=%async_computation.2 | async-start | bytes 5222400 | tf_op jit(solution)/shard_map/all_gather | solution.py:127
  9.0 148.8 %all-gather.7.cloned.1.call-start = ((), (), s32[]{:S(2)}) async-start(), calls=%async_computation.3 | async-start | bytes 14745600 | tf_op jit(solution)/shard_map/all_gather | solution.py:128
  130.4 754.7 %all-reduce.19.cloned.1.call-start = ((), (), s32[]{:S(2)}) async-start(), calls=%async_computation.4 | async-start | bytes 19660800
  251.5 12.0 %collective-permute-start = (bf16[3,32,640]{2,1,0:T(8,128)(2,1)S(1)}, bf16[3,32,640]{2,1,0:T(8,128)(2,1)S(1)}, u32[]{:S(2)}, u32[]{:S(2)}) collective-permute-start(bf16[3,32,640]{2,1,0:T(8,128)(2,1)S(1)} %fusion.69), channel_id=1, source_target_pairs={{0,32},{32,64},{64,96},{96,128},{128,160},{160,192},{192,224},{1,3... | collective-permute-start | bytes 368648 | tf_op jit(solution)/shard_map/while/body/eval_jaxpr/ppermute | solution.py:15
  272.8 11.7 %collective-permute-start = (bf16[3,32,640]{2,1,0:T(8,128)(2,1)S(1)}, bf16[3,32,640]{2,1,0:T(8,128)(2,1)S(1)}, u32[]{:S(2)}, u32[]{:S(2)}) collective-permute-start(bf16[3,32,640]{2,1,0:T(8,128)(2,1)S(1)} %fusion.69), channel_id=1, source_target_pairs={{0,32},{32,64},{64,96},{96,128},{128,160},{160,192},{192,224},{1,3... | collective-permute-start | bytes 368648 | tf_op jit(solution)/shard_map/while/body/eval_jaxpr/ppermute | solution.py:15
  293.6 11.6 %collective-permute-start = (bf16[3,32,640]{2,1,0:T(8,128)(2,1)S(1)}, bf16[3,32,640]{2,1,0:T(8,128)(2,1)S(1)}, u32[]{:S(2)}, u32[]{:S(2)}) collective-permute-start(bf16[3,32,640]{2,1,0:T(8,128)(2,1)S(1)} %fusion.69), channel_id=1, source_target_pairs={{0,32},{32,64},{64,96},{96,128},{128,160},{160,192},{192,224},{1,3... | collective-permute-start | bytes 368648 | tf_op jit(solution)/shard_map/while/body/eval_jaxpr/ppermute | solution.py:15
  314.5 11.6 %collective-permute-start = (bf16[3,32,640]{2,1,0:T(8,128)(2,1)S(1)}, bf16[3,32,640]{2,1,0:T(8,128)(2,1)S(1)}, u32[]{:S(2)}, u32[]{:S(2)}) collective-permute-start(bf16[3,32,640]{2,1,0:T(8,128)(2,1)S(1)} %fusion.69), channel_id=1, source_target_pairs={{0,32},{32,64},{64,96},{96,128},{128,160},{160,192},{192,224},{1,3... | collective-permute-start | bytes 368648 | tf_op jit(solution)/shard_map/while/body/eval_jaxpr/ppermute | solution.py:15
  335.4 11.7 %collective-permute-start = (bf16[3,32,640]{2,1,0:T(8,128)(2,1)S(1)}, bf16[3,32,640]{2,1,0:T(8,128)(2,1)S(1)}, u32[]{:S(2)}, u32[]{:S(2)}) collective-permute-start(bf16[3,32,640]{2,1,0:T(8,128)(2,1)S(1)} %fusion.69), channel_id=1, source_target_pairs={{0,32},{32,64},{64,96},{96,128},{128,160},{160,192},{192,224},{1,3... | collective-permute-start | bytes 368648 | tf_op jit(solution)/shard_map/while/body/eval_jaxpr/ppermute | solution.py:15
  356.2 11.6 %collective-permute-start = (bf16[3,32,640]{2,1,0:T(8,128)(2,1)S(1)}, bf16[3,32,640]{2,1,0:T(8,128)(2,1)S(1)}, u32[]{:S(2)}, u32[]{:S(2)}) collective-permute-start(bf16[3,32,640]{2,1,0:T(8,128)(2,1)S(1)} %fusion.69), channel_id=1, source_target_pairs={{0,32},{32,64},{64,96},{96,128},{128,160},{160,192},{192,224},{1,3... | collective-permute-start | bytes 368648 | tf_op jit(solution)/shard_map/while/body/eval_jaxpr/ppermute | solution.py:15
  377.1 11.6 %collective-permute-start = (bf16[3,32,640]{2,1,0:T(8,128)(2,1)S(1)}, bf16[3,32,640]{2,1,0:T(8,128)(2,1)S(1)}, u32[]{:S(2)}, u32[]{:S(2)}) collective-permute-start(bf16[3,32,640]{2,1,0:T(8,128)(2,1)S(1)} %fusion.69), channel_id=1, source_target_pairs={{0,32},{32,64},{64,96},{96,128},{128,160},{160,192},{192,224},{1,3... | collective-permute-start | bytes 368648 | tf_op jit(solution)/shard_map/while/body/eval_jaxpr/ppermute | solution.py:15
  398.0 11.6 %collective-permute-start = (bf16[3,32,640]{2,1,0:T(8,128)(2,1)S(1)}, bf16[3,32,640]{2,1,0:T(8,128)(2,1)S(1)}, u32[]{:S(2)}, u32[]{:S(2)}) collective-permute-start(bf16[3,32,640]{2,1,0:T(8,128)(2,1)S(1)} %fusion.69), channel_id=1, source_target_pairs={{0,32},{32,64},{64,96},{96,128},{128,160},{160,192},{192,224},{1,3... | collective-permute-start | bytes 368648 | tf_op jit(solution)/shard_map/while/body/eval_jaxpr/ppermute | solution.py:15
  425.5 12.1 %collective-permute-start.1 = (bf16[3,32,640]{2,1,0:T(8,128)(2,1)S(1)}, bf16[3,32,640]{2,1,0:T(8,128)(2,1)S(1)}, u32[]{:S(2)}, u32[]{:S(2)}) collective-permute-start(bf16[3,32,640]{2,1,0:T(8,128)(2,1)S(1)} %fusion.78), channel_id=1, source_target_pairs={{32,0},{64,32},{96,64},{128,96},{160,128},{192,160},{224,192},{33,... | collective-permute-start | bytes 368648 | tf_op jit(solution)/shard_map/while/body/eval_jaxpr/ppermute | solution.py:15
  451.3 12.0 %collective-permute-start.1 = (bf16[3,32,640]{2,1,0:T(8,128)(2,1)S(1)}, bf16[3,32,640]{2,1,0:T(8,128)(2,1)S(1)}, u32[]{:S(2)}, u32[]{:S(2)}) collective-permute-start(bf16[3,32,640]{2,1,0:T(8,128)(2,1)S(1)} %fusion.78), channel_id=1, source_target_pairs={{32,0},{64,32},{96,64},{128,96},{160,128},{192,160},{224,192},{33,... | collective-permute-start | bytes 368648 | tf_op jit(solution)/shard_map/while/body/eval_jaxpr/ppermute | solution.py:15
  477.1 12.0 %collective-permute-start.1 = (bf16[3,32,640]{2,1,0:T(8,128)(2,1)S(1)}, bf16[3,32,640]{2,1,0:T(8,128)(2,1)S(1)}, u32[]{:S(2)}, u32[]{:S(2)}) collective-permute-start(bf16[3,32,640]{2,1,0:T(8,128)(2,1)S(1)} %fusion.78), channel_id=1, source_target_pairs={{32,0},{64,32},{96,64},{128,96},{160,128},{192,160},{224,192},{33,... | collective-permute-start | bytes 368648 | tf_op jit(solution)/shard_map/while/body/eval_jaxpr/ppermute | solution.py:15
  502.9 12.0 %collective-permute-start.1 = (bf16[3,32,640]{2,1,0:T(8,128)(2,1)S(1)}, bf16[3,32,640]{2,1,0:T(8,128)(2,1)S(1)}, u32[]{:S(2)}, u32[]{:S(2)}) collective-permute-start(bf16[3,32,640]{2,1,0:T(8,128)(2,1)S(1)} %fusion.78), channel_id=1, source_target_pairs={{32,0},{64,32},{96,64},{128,96},{160,128},{192,160},{224,192},{33,... | collective-permute-start | bytes 368648 | tf_op jit(solution)/shard_map/while/body/eval_jaxpr/ppermute | solution.py:15
  528.8 11.6 %collective-permute-start.1 = (bf16[3,32,640]{2,1,0:T(8,128)(2,1)S(1)}, bf16[3,32,640]{2,1,0:T(8,128)(2,1)S(1)}, u32[]{:S(2)}, u32[]{:S(2)}) collective-permute-start(bf16[3,32,640]{2,1,0:T(8,128)(2,1)S(1)} %fusion.78), channel_id=1, source_target_pairs={{32,0},{64,32},{96,64},{128,96},{160,128},{192,160},{224,192},{33,... | collective-permute-start | bytes 368648 | tf_op jit(solution)/shard_map/while/body/eval_jaxpr/ppermute | solution.py:15
  554.2 11.6 %collective-permute-start.1 = (bf16[3,32,640]{2,1,0:T(8,128)(2,1)S(1)}, bf16[3,32,640]{2,1,0:T(8,128)(2,1)S(1)}, u32[]{:S(2)}, u32[]{:S(2)}) collective-permute-start(bf16[3,32,640]{2,1,0:T(8,128)(2,1)S(1)} %fusion.78), channel_id=1, source_target_pairs={{32,0},{64,32},{96,64},{128,96},{160,128},{192,160},{224,192},{33,... | collective-permute-start | bytes 368648 | tf_op jit(solution)/shard_map/while/body/eval_jaxpr/ppermute | solution.py:15
  579.6 11.6 %collective-permute-start.1 = (bf16[3,32,640]{2,1,0:T(8,128)(2,1)S(1)}, bf16[3,32,640]{2,1,0:T(8,128)(2,1)S(1)}, u32[]{:S(2)}, u32[]{:S(2)}) collective-permute-start(bf16[3,32,640]{2,1,0:T(8,128)(2,1)S(1)} %fusion.78), channel_id=1, source_target_pairs={{32,0},{64,32},{96,64},{128,96},{160,128},{192,160},{224,192},{33,... | collective-permute-start | bytes 368648 | tf_op jit(solution)/shard_map/while/body/eval_jaxpr/ppermute | solution.py:15
  605.0 11.7 %collective-permute-start.1 = (bf16[3,32,640]{2,1,0:T(8,128)(2,1)S(1)}, bf16[3,32,640]{2,1,0:T(8,128)(2,1)S(1)}, u32[]{:S(2)}, u32[]{:S(2)}) collective-permute-start(bf16[3,32,640]{2,1,0:T(8,128)(2,1)S(1)} %fusion.78), channel_id=1, source_target_pairs={{32,0},{64,32},{96,64},{128,96},{160,128},{192,160},{224,192},{33,... | collective-permute-start | bytes 368648 | tf_op jit(solution)/shard_map/while/body/eval_jaxpr/ppermute | solution.py:15
  630.4 11.6 %collective-permute-start.1 = (bf16[3,32,640]{2,1,0:T(8,128)(2,1)S(1)}, bf16[3,32,640]{2,1,0:T(8,128)(2,1)S(1)}, u32[]{:S(2)}, u32[]{:S(2)}) collective-permute-start(bf16[3,32,640]{2,1,0:T(8,128)(2,1)S(1)} %fusion.78), channel_id=1, source_target_pairs={{32,0},{64,32},{96,64},{128,96},{160,128},{192,160},{224,192},{33,... | collective-permute-start | bytes 368648 | tf_op jit(solution)/shard_map/while/body/eval_jaxpr/ppermute | solution.py:15
  655.8 11.7 %collective-permute-start.1 = (bf16[3,32,640]{2,1,0:T(8,128)(2,1)S(1)}, bf16[3,32,640]{2,1,0:T(8,128)(2,1)S(1)}, u32[]{:S(2)}, u32[]{:S(2)}) collective-permute-start(bf16[3,32,640]{2,1,0:T(8,128)(2,1)S(1)} %fusion.78), channel_id=1, source_target_pairs={{32,0},{64,32},{96,64},{128,96},{160,128},{192,160},{224,192},{33,... | collective-permute-start | bytes 368648 | tf_op jit(solution)/shard_map/while/body/eval_jaxpr/ppermute | solution.py:15
  681.3 12.5 %collective-permute-start.1 = (bf16[3,32,640]{2,1,0:T(8,128)(2,1)S(1)}, bf16[3,32,640]{2,1,0:T(8,128)(2,1)S(1)}, u32[]{:S(2)}, u32[]{:S(2)}) collective-permute-start(bf16[3,32,640]{2,1,0:T(8,128)(2,1)S(1)} %fusion.78), channel_id=1, source_target_pairs={{32,0},{64,32},{96,64},{128,96},{160,128},{192,160},{224,192},{33,... | collective-permute-start | bytes 368648 | tf_op jit(solution)/shard_map/while/body/eval_jaxpr/ppermute | solution.py:15
  707.5 13.3 %collective-permute-start.1 = (bf16[3,32,640]{2,1,0:T(8,128)(2,1)S(1)}, bf16[3,32,640]{2,1,0:T(8,128)(2,1)S(1)}, u32[]{:S(2)}, u32[]{:S(2)}) collective-permute-start(bf16[3,32,640]{2,1,0:T(8,128)(2,1)S(1)} %fusion.78), channel_id=1, source_target_pairs={{32,0},{64,32},{96,64},{128,96},{160,128},{192,160},{224,192},{33,... | collective-permute-start | bytes 368648 | tf_op jit(solution)/shard_map/while/body/eval_jaxpr/ppermute | solution.py:15
  784.8 224.2 %reduce-scatter.5.cloned.1.call-start = ((), (), s32[]{:S(2)}) async-start(), calls=%async_computation.1 | async-start | bytes 5222400 | tf_op jit(solution)/shard_map/reduce_scatter | solution.py:217
  (26 other events, 216.6 us)
Sparse Core Ops, SparseCore 0:
  10.4 119.9 all-gather.4
  132.2 25.5 all-gather.6
  785.0 100.0 all-reduce.18
  891.0 118.0 reduce-scatter.4

commit v3 on v1

--- a/solution.py
+++ b/solution.py
@@ -1,18 +1,74 @@
+import functools
 import math
 
 import jax
 import jax.numpy as jnp
 from jax import lax
+from jax.experimental import pallas as pl
+from jax.experimental.pallas import tpu as pltpu
 from jax.sharding import PartitionSpec as P
 
 HEIGHT = 8
 WIDTH = 4
 
 
+def hop_kernel(steps, x_ref, out_ref, landing, send_sem, recv_sem):
+    count = lax.axis_size("pipe")
+    me = lax.axis_index("pipe")
+    row = lax.axis_index("dp")
+    dest = me + steps
+    src = me - steps
+    has_dest = (dest >= 0) & (dest < count)
+    has_src = (src >= 0) & (src < count)
+    barrier = pltpu.get_barrier_semaphore()
+    copy = pltpu.make_async_remote_copy(
+        src_ref=x_ref,
+        dst_ref=landing,
+        send_sem=send_sem,
+        recv_sem=recv_sem,
+        device_id=(dest, row),
+        device_id_type=pl.DeviceIdType.MESH,
+    )
+
+    @pl.when(has_src)
+    def _():
+        pl.semaphore_signal(barrier, inc=1, device_id=(src, row), device_id_type=pl.DeviceIdType.MESH)
+
+    @pl.when(has_dest)
+    def _():
+        pl.semaphore_wait(barrier, 1)
+        copy.start()
+
+    @pl.when(has_src)
+    def _():
+        copy.wait_recv()
+        out_ref[...] = landing[...]
+
+    @pl.when(jnp.logical_not(has_src))
+    def _():
+        out_ref[...] = jnp.zeros_like(out_ref)
+
+    @pl.when(has_dest)
+    def _():
+        copy.wait_send()
+
+
 def passed_along(value, axis, steps):
-    count = lax.axis_size(axis)
-    first, last = (max(0, -steps), min(count, count - steps))
-    return lax.ppermute(value, axis, [(source, source + steps) for source in range(first, last)])
+    assert axis == "pipe"
+    return pl.pallas_call(
+        functools.partial(hop_kernel, steps),
+        out_shape=jax.ShapeDtypeStruct(value.shape, value.dtype),
+        in_specs=[pl.BlockSpec(memory_space=pltpu.VMEM)],
+        out_specs=pl.BlockSpec(memory_space=pltpu.VMEM),
+        scratch_shapes=[
+            pltpu.VMEM(value.shape, value.dtype),
+            pltpu.SemaphoreType.DMA(()),
+            pltpu.SemaphoreType.DMA(()),
+        ],
+        compiler_params=pltpu.CompilerParams(
+            collective_id=0 if steps > 0 else 1, has_side_effects=True
+        ),
+    )(value)
 
 
 def embedding_of(step, channels):

time: 938 us -> 939 us (level)
  Pallas kernels: 0 us -> 237 us
  waiting for transfers between devices: 427 us -> 284 us
  starting transfers between devices: 109 us -> 0.08 us
    pallas_call x0 -> x24, Pallas kernels: none -> 237 us  [passed_along(): pl.pallas_call(functools.partial(hop_kernel, steps), out_shape=jax.ShapeD...]
    ppermute x24 -> x0, waiting for transfers between devices: 143 us -> none  [passed_along(): lax.ppermute(value, axis, [(source, source + steps) for source in range(f...]
    ppermute x24 -> x0, starting transfers between devices: 109 us -> none  [passed_along(): lax.ppermute(value, axis, [(source, source + steps) for source in range(f...]
  transfers between devices with their start and end apart: 26 -> 2, of which waited for: 26 -> 2; matrix products, arithmetic and copies ran while one was open for 1% -> 0% of each run, Pallas kernels for 0% -> 0%
where the time goes in v3:
time: 939 us; the launch traced here: 932 us
  waiting for transfers between devices  284 us (30%)
  Pallas kernels  237 us (25%)
  matrix products  175 us (19%)
  local copies, waits for them, and re-layouts  115 us (12%)
  other arithmetic  88.2 us (9%)
  loops' own time  18.6 us (2%)
  between operations  14.3 us (2%)
    pallas_call x24, Pallas kernels, passed_along(): pl.pallas_call(functools.partial(hop_kernel, steps), out_shape=jax.ShapeD...  237 us
    reduce_scatter x1, waiting for transfers between devices, per_device(): lax.psum_scatter(partial_rows, 'dp', scatter_dimension=0, tiled=False)  208 us
    all_gather x1, waiting for transfers between devices, per_device(): gathered = lax.all_gather(own_rows, 'dp', axis=0, tiled=False)  76.1 us
    dot_general x12, matrix products, section_backward(): jnp.dot(pre_grad.reshape(frames * pixels, channels), spatial.T, preferred...  63.8 us
    dynamic_update_slice x48, other arithmetic, stash_put(): return lax.dynamic_update_index_in_dim(stash, value, slot, 0)  60 us
    dot_general x12, matrix products, section_forward(): jnp.dot(spatial_columns(normed), spatial, preferred_element_type=jnp.floa...  55.8 us
    dot_general x12, matrix products, section_backward(): jnp.dot(upstream_flat, temporal.T, preferred_element_type=jnp.float32)  30.3 us
    concatenate x117, local copies, waits for them, and re-layouts, spatial_columns(): return jnp.concatenate(pieces, axis=-1).reshape(-1, 9 * channels)  21.2 us
  transfers between devices with their start and end apart: 2, of which 2 were waited for; matrix products, arithmetic and copies ran while one was open for 0% of the time, Pallas kernels for 0%

profile of v3, /device:TPU:1, one launch (start us, length us, event | category | flops | bytes accessed | tf_op | source)
XLA Modules:
  0.0 932.1 jit_solution(14405398568262215910)
XLA Ops:
  9.9 76.1 %all-gather.3.cloned.1.call-done = bf16[7680,640]{1,0:T(8,128)(2,1)} async-done(((bf16[240,640]{1,0:T(8,128)(2,1)}), bf16[7680,640]{1,0:T(8,128)(2,1)}) %all-gather.3.cloned.1.call-update) | async-done | bytes 9830416 | tf_op jit(solution)/shard_map/all_gather | solution.py:181
  109.5 231.9 %while.37 = (s32[]{:T(128)}, bf16[3,32,640]{2,1,0:T(8,128)(2,1)S(1)}, bf16[7,3,32,640]{3,2,1,0:T(8,128)(2,1)S(1)}, bf16[7,3,32,640]{3,2,1,0:T(8,128)(2,1)}, f32[...) while((s32[]{:T(128)}, ...), condition=%wide.region_2.3_spmd, body=%wide.region_0.2_spmd.sunk | while | flops 945868928 | bytes 29380448 | solution.py:219
  180.6 10.9 %eval_jaxpr.9 = bf16[3,32,640]{2,1,0:T(8,128)(2,1)S(1)} custom-call(bf16[3,32,640]{2,1,0:T(8,128)(2,1)} %fusion.69.x_ref), custom_call_target="tpu_custom_call" | custom-call | tf_op jit(solution)/shard_map/while/body/eval_jaxpr/pallas_call | solution.py:58
  202.2 10.6 %eval_jaxpr.9 = bf16[3,32,640]{2,1,0:T(8,128)(2,1)S(1)} custom-call(bf16[3,32,640]{2,1,0:T(8,128)(2,1)} %fusion.69.x_ref), custom_call_target="tpu_custom_call" | custom-call | tf_op jit(solution)/shard_map/while/body/eval_jaxpr/pallas_call | solution.py:58
  223.4 10.7 %eval_jaxpr.9 = bf16[3,32,640]{2,1,0:T(8,128)(2,1)S(1)} custom-call(bf16[3,32,640]{2,1,0:T(8,128)(2,1)} %fusion.69.x_ref), custom_call_target="tpu_custom_call" | custom-call | tf_op jit(solution)/shard_map/while/body/eval_jaxpr/pallas_call | solution.py:58
  244.8 10.7 %eval_jaxpr.9 = bf16[3,32,640]{2,1,0:T(8,128)(2,1)S(1)} custom-call(bf16[3,32,640]{2,1,0:T(8,128)(2,1)} %fusion.69.x_ref), custom_call_target="tpu_custom_call" | custom-call | tf_op jit(solution)/shard_map/while/body/eval_jaxpr/pallas_call | solution.py:58
  266.0 10.7 %eval_jaxpr.9 = bf16[3,32,640]{2,1,0:T(8,128)(2,1)S(1)} custom-call(bf16[3,32,640]{2,1,0:T(8,128)(2,1)} %fusion.69.x_ref), custom_call_target="tpu_custom_call" | custom-call | tf_op jit(solution)/shard_map/while/body/eval_jaxpr/pallas_call | solution.py:58
  287.3 10.7 %eval_jaxpr.9 = bf16[3,32,640]{2,1,0:T(8,128)(2,1)S(1)} custom-call(bf16[3,32,640]{2,1,0:T(8,128)(2,1)} %fusion.69.x_ref), custom_call_target="tpu_custom_call" | custom-call | tf_op jit(solution)/shard_map/while/body/eval_jaxpr/pallas_call | solution.py:58
  308.6 10.7 %eval_jaxpr.9 = bf16[3,32,640]{2,1,0:T(8,128)(2,1)S(1)} custom-call(bf16[3,32,640]{2,1,0:T(8,128)(2,1)} %fusion.69.x_ref), custom_call_target="tpu_custom_call" | custom-call | tf_op jit(solution)/shard_map/while/body/eval_jaxpr/pallas_call | solution.py:58
  329.9 10.7 %eval_jaxpr.9 = bf16[3,32,640]{2,1,0:T(8,128)(2,1)S(1)} custom-call(bf16[3,32,640]{2,1,0:T(8,128)(2,1)} %fusion.69.x_ref), custom_call_target="tpu_custom_call" | custom-call | tf_op jit(solution)/shard_map/while/body/eval_jaxpr/pallas_call | solution.py:58
  343.4 306.0 %while.38 = (s32[]{:T(128)}, bf16[3,32,640]{2,1,0:T(8,128)(2,1)S(1)}, bf16[7,3,32,640]{3,2,1,0:T(8,128)(2,1)}, bf16[7,3,32,640]{3,2,1,0:T(8,128)(2,1)}, pred[]{:...) while((s32[]{:T(128)}, ...), condition=%wide.region_6.7_spmd, body=%wide.region_3.6_spmd.sunk | while | flops 946099520 | bytes 26898296 | solution.py:245
  357.8 11.1 %eval_jaxpr.10 = bf16[3,32,640]{2,1,0:T(8,128)(2,1)S(1)} custom-call(bf16[3,32,640]{2,1,0:T(8,128)(2,1)} %fusion.78.x_ref), custom_call_target="tpu_custom_call" | custom-call | tf_op jit(solution)/shard_map/while/body/eval_jaxpr/pallas_call | solution.py:58
  383.3 11.1 %eval_jaxpr.10 = bf16[3,32,640]{2,1,0:T(8,128)(2,1)S(1)} custom-call(bf16[3,32,640]{2,1,0:T(8,128)(2,1)} %fusion.78.x_ref), custom_call_target="tpu_custom_call" | custom-call | tf_op jit(solution)/shard_map/while/body/eval_jaxpr/pallas_call | solution.py:58
  408.9 11.1 %eval_jaxpr.10 = bf16[3,32,640]{2,1,0:T(8,128)(2,1)S(1)} custom-call(bf16[3,32,640]{2,1,0:T(8,128)(2,1)} %fusion.78.x_ref), custom_call_target="tpu_custom_call" | custom-call | tf_op jit(solution)/shard_map/while/body/eval_jaxpr/pallas_call | solution.py:58
  434.4 11.1 %eval_jaxpr.10 = bf16[3,32,640]{2,1,0:T(8,128)(2,1)S(1)} custom-call(bf16[3,32,640]{2,1,0:T(8,128)(2,1)} %fusion.78.x_ref), custom_call_target="tpu_custom_call" | custom-call | tf_op jit(solution)/shard_map/while/body/eval_jaxpr/pallas_call | solution.py:58
  459.9 10.7 %eval_jaxpr.10 = bf16[3,32,640]{2,1,0:T(8,128)(2,1)S(1)} custom-call(bf16[3,32,640]{2,1,0:T(8,128)(2,1)} %fusion.78.x_ref), custom_call_target="tpu_custom_call" | custom-call | tf_op jit(solution)/shard_map/while/body/eval_jaxpr/pallas_call | solution.py:58
  485.1 10.7 %eval_jaxpr.10 = bf16[3,32,640]{2,1,0:T(8,128)(2,1)S(1)} custom-call(bf16[3,32,640]{2,1,0:T(8,128)(2,1)} %fusion.78.x_ref), custom_call_target="tpu_custom_call" | custom-call | tf_op jit(solution)/shard_map/while/body/eval_jaxpr/pallas_call | solution.py:58
  510.2 10.7 %eval_jaxpr.10 = bf16[3,32,640]{2,1,0:T(8,128)(2,1)S(1)} custom-call(bf16[3,32,640]{2,1,0:T(8,128)(2,1)} %fusion.78.x_ref), custom_call_target="tpu_custom_call" | custom-call | tf_op jit(solution)/shard_map/while/body/eval_jaxpr/pallas_call | solution.py:58
  535.3 10.7 %eval_jaxpr.10 = bf16[3,32,640]{2,1,0:T(8,128)(2,1)S(1)} custom-call(bf16[3,32,640]{2,1,0:T(8,128)(2,1)} %fusion.78.x_ref), custom_call_target="tpu_custom_call" | custom-call | tf_op jit(solution)/shard_map/while/body/eval_jaxpr/pallas_call | solution.py:58
  560.4 10.7 %eval_jaxpr.10 = bf16[3,32,640]{2,1,0:T(8,128)(2,1)S(1)} custom-call(bf16[3,32,640]{2,1,0:T(8,128)(2,1)} %fusion.78.x_ref), custom_call_target="tpu_custom_call" | custom-call | tf_op jit(solution)/shard_map/while/body/eval_jaxpr/pallas_call | solution.py:58
  585.5 10.8 %eval_jaxpr.10 = bf16[3,32,640]{2,1,0:T(8,128)(2,1)S(1)} custom-call(bf16[3,32,640]{2,1,0:T(8,128)(2,1)} %fusion.78.x_ref), custom_call_target="tpu_custom_call" | custom-call | tf_op jit(solution)/shard_map/while/body/eval_jaxpr/pallas_call | solution.py:58
  610.7 12.5 %eval_jaxpr.10 = bf16[3,32,640]{2,1,0:T(8,128)(2,1)S(1)} custom-call(bf16[3,32,640]{2,1,0:T(8,128)(2,1)} %fusion.78.x_ref), custom_call_target="tpu_custom_call" | custom-call | tf_op jit(solution)/shard_map/while/body/eval_jaxpr/pallas_call | solution.py:58
  637.7 11.6 %eval_jaxpr.10 = bf16[3,32,640]{2,1,0:T(8,128)(2,1)S(1)} custom-call(bf16[3,32,640]{2,1,0:T(8,128)(2,1)} %fusion.78.x_ref), custom_call_target="tpu_custom_call" | custom-call | tf_op jit(solution)/shard_map/while/body/eval_jaxpr/pallas_call | solution.py:58
  713.2 208.1 %reduce-scatter.2.cloned.1.call-done = bf16[1,240,640]{2,1,0:T(8,128)(2,1)} async-done(((bf16[32,240,640]{2,1,0:T(8,128)(2,1)}), bf16[1,240,640]{2,1,0:T(8,128)(2,1)}) %reduce-scatter.2.cloned.1.call-update) | async-done | bytes 307216 | tf_op jit(solution)/shard_map/reduce_scatter | solution.py:266
  (687 shorter events, 396.5 us)
Async XLA Ops:
  7.2 78.9 %all-gather.3.cloned.1.call-start = ((), (), s32[]{:S(2)}) async-start(), calls=%async_computation.2 | async-start | bytes 10137600 | tf_op jit(solution)/shard_map/all_gather | solution.py:181
  9.0 912.3 %reduce-scatter.2.cloned.1.call-start = ((), (), s32[]{:S(2)}) async-start(), calls=%async_computation.1 | async-start | bytes 10137600 | tf_op jit(solution)/shard_map/reduce_scatter | solution.py:266
  113.4 4.7 copy-start
  128.5 4.7 copy-start
  144.1 4.7 copy-start
  159.4 4.7 copy-start
  174.7 4.7 copy-start
  196.2 4.7 copy-start
  217.5 4.7 copy-start
  238.8 4.7 copy-start
  260.1 4.7 copy-start
  281.4 4.7 copy-start
  302.7 4.7 copy-start
  323.9 4.7 copy-start
  651.4 2.3 copy-start.7
  683.7 2.5 copy-start.6
  683.7 2.6 copy-start.5
  685.0 1.6 copy-start.4
  686.2 1.1 copy-start.3
  686.3 1.2 copy-start.2
  686.5 1.3 copy-start.1
  686.6 1.4 copy-start.8
Sparse Core Ops, SparseCore 0:
  10.4 75.5 all-gather.2
  713.3 207.9 reduce-scatter.1

commit v4 on v3

--- a/solution.py
+++ b/solution.py
@@ -164,6 +164,86 @@
     _, pullback = jax.vjp(normalize, summed)
     back_input = (upstream.astype(jnp.float32) + pullback(norm_grad)[0]).astype(jnp.bfloat16)
     return back_input, pre_grad
+
+
+def scatter_kernel(part_hbm, out_ref, landing, send_sem, recv_sem, own_sem):
+    count = lax.axis_size("dp")
+    me = lax.axis_index("dp")
+    stage = lax.axis_index("pipe")
+    barrier = pltpu.get_barrier_semaphore()
+
+    own = pltpu.make_async_copy(part_hbm.at[me], landing.at[me], own_sem)
+    own.start()
+
+    def greet(peer, carry):
+        @pl.when(peer != me)
+        def _():
+            pl.semaphore_signal(
+                barrier, inc=1, device_id=(stage, peer), device_id_type=pl.DeviceIdType.MESH
+            )
+        return carry
+
+    lax.fori_loop(0, count, greet, 0)
+    pl.semaphore_wait(barrier, count - 1)
+
+    def remote(peer):
+        return pltpu.make_async_remote_copy(
+            src_ref=part_hbm.at[peer],
+            dst_ref=landing.at[me],
+            send_sem=send_sem.at[peer],
+            recv_sem=recv_sem.at[me],
+            device_id=(stage, peer),
+            device_id_type=pl.DeviceIdType.MESH,
+        )
+
+    def send(step, carry):
+        peer = lax.rem(me + step, count)
+        remote(peer).start()
+        return carry
+
+    lax.fori_loop(1, count, send, 0)
+    own.wait()
+
+    def take(step, total):
+        peer = lax.rem(me + count - step, count)
+        pltpu.make_async_remote_copy(
+            src_ref=part_hbm.at[peer],
+            dst_ref=landing.at[peer],
+            send_sem=send_sem.at[peer],
+            recv_sem=recv_sem.at[peer],
+            device_id=(stage, peer),
+            device_id_type=pl.DeviceIdType.MESH,
+        ).wait_recv()
+        return total + landing[peer].astype(jnp.float32)
+
+    total = lax.fori_loop(1, count, take, landing[me].astype(jnp.float32))
+    out_ref[...] = total
+
+    def drain(step, carry):
+        peer = lax.rem(me + step, count)
+        remote(peer).wait_send()
+        return carry
+
+    lax.fori_loop(1, count, drain, 0)
+
+
+def scatter_sum(partial_rows):
+    count, rows, channels = partial_rows.shape
+    return pl.pallas_call(
+        scatter_kernel,
+        out_shape=jax.ShapeDtypeStruct((rows, channels), jnp.float32),
+        in_specs=[pl.BlockSpec(memory_space=pl.ANY)],
+        out_specs=pl.BlockSpec(memory_space=pltpu.VMEM),
+        scratch_shapes=[
+            pltpu.VMEM((count, rows, channels), partial_rows.dtype),
+            pltpu.SemaphoreType.DMA((count,)),
+            pltpu.SemaphoreType.DMA((count,)),
+            pltpu.SemaphoreType.DMA(()),
+        ],
+        compiler_params=pltpu.CompilerParams(
+            collective_id=2, has_side_effects=True, vmem_limit_bytes=48 * 1024 * 1024
+        ),
+    )(partial_rows)
 
 
 def per_device(samples, timesteps, cotangent, spatial_weight, temporal_weight):
@@ -263,8 +343,7 @@
         ],
         axis=1,
     )
-    share = lax.psum_scatter(partial_rows, "dp", scatter_dimension=0, tiled=False)
-    share = share.astype(jnp.float32)
+    share = scatter_sum(partial_rows)
     return (share[None, :sp_rows], share[None, sp_rows:])
 
 

time: 939 us -> 990 us (1.054)
  the two profiles are of different devices: /device:TPU:1 before, /device:TPU:39 now
where the time goes in v4:
time: 990 us; the launch traced here: 987 us
  Pallas kernels  504 us (51%)
  matrix products  175 us (18%)
  local copies, waits for them, and re-layouts  113 us (11%)
  other arithmetic  88.2 us (9%)
  waiting for transfers between devices  74.3 us (8%)
  loops' own time  18.6 us (2%)
  between operations  14.3 us (1%)
    pallas_call x24, Pallas kernels, passed_along(): pl.pallas_call(functools.partial(hop_kernel, steps), out_shape=jax.ShapeD...  286 us
    pallas_call x1, Pallas kernels, scatter_sum(): pl.pallas_call(scatter_kernel, out_shape=jax.ShapeDtypeStruct((rows, chan...  218 us
    all_gather x1, waiting for transfers between devices, per_device(): gathered = lax.all_gather(own_rows, 'dp', axis=0, tiled=False)  74.2 us
    dot_general x12, matrix products, section_backward(): jnp.dot(pre_grad.reshape(frames * pixels, channels), spatial.T, preferred...  63.8 us
    dynamic_update_slice x48, other arithmetic, stash_put(): return lax.dynamic_update_index_in_dim(stash, value, slot, 0)  60.1 us
    dot_general x12, matrix products, section_forward(): jnp.dot(spatial_columns(normed), spatial, preferred_element_type=jnp.floa...  55.8 us
    dot_general x12, matrix products, section_backward(): jnp.dot(upstream_flat, temporal.T, preferred_element_type=jnp.float32)  30.3 us
    concatenate x117, local copies, waits for them, and re-layouts, spatial_columns(): return jnp.concatenate(pieces, axis=-1).reshape(-1, 9 * channels)  21.2 us
  transfers between devices with their start and end apart: 1, of which 1 were waited for; matrix products, arithmetic and copies ran while one was open for 0% of the time, Pallas kernels for 0%

profile of v4, /device:TPU:39, one launch (start us, length us, event | category | flops | bytes accessed | tf_op | source)
XLA Modules:
  0.0 986.7 jit_solution(8397614808450871893)
XLA Ops:
  9.9 74.2 %all-gather.3.cloned.1.call-done = bf16[7680,640]{1,0:T(8,128)(2,1)} async-done(((bf16[240,640]{1,0:T(8,128)(2,1)}), bf16[7680,640]{1,0:T(8,128)(2,1)}) %all-gather.3.cloned.1.call-update) | async-done | bytes 9830416 | tf_op jit(solution)/shard_map/all_gather | solution.py:261
  107.5 268.5 %while.37 = (s32[]{:T(128)}, bf16[3,32,640]{2,1,0:T(8,128)(2,1)S(1)}, bf16[7,3,32,640]{3,2,1,0:T(8,128)(2,1)S(1)}, bf16[7,3,32,640]{3,2,1,0:T(8,128)(2,1)}, f32[...) while((s32[]{:T(128)}, ...), condition=%wide.region_2.3_spmd, body=%wide.region_0.2_spmd.sunk | while | flops 945868928 | bytes 29380448 | solution.py:299
  137.9 12.7 %eval_jaxpr.9 = bf16[3,32,640]{2,1,0:T(8,128)(2,1)S(1)} custom-call(bf16[3,32,640]{2,1,0:T(8,128)(2,1)} %fusion.69.x_ref), custom_call_target="tpu_custom_call" | custom-call | tf_op jit(solution)/shard_map/while/body/eval_jaxpr/pallas_call | solution.py:58
  183.0 11.9 %eval_jaxpr.9 = bf16[3,32,640]{2,1,0:T(8,128)(2,1)S(1)} custom-call(bf16[3,32,640]{2,1,0:T(8,128)(2,1)} %fusion.69.x_ref), custom_call_target="tpu_custom_call" | custom-call | tf_op jit(solution)/shard_map/while/body/eval_jaxpr/pallas_call | solution.py:58
  205.5 11.9 %eval_jaxpr.9 = bf16[3,32,640]{2,1,0:T(8,128)(2,1)S(1)} custom-call(bf16[3,32,640]{2,1,0:T(8,128)(2,1)} %fusion.69.x_ref), custom_call_target="tpu_custom_call" | custom-call | tf_op jit(solution)/shard_map/while/body/eval_jaxpr/pallas_call | solution.py:58
  228.1 11.9 %eval_jaxpr.9 = bf16[3,32,640]{2,1,0:T(8,128)(2,1)S(1)} custom-call(bf16[3,32,640]{2,1,0:T(8,128)(2,1)} %fusion.69.x_ref), custom_call_target="tpu_custom_call" | custom-call | tf_op jit(solution)/shard_map/while/body/eval_jaxpr/pallas_call | solution.py:58
  250.6 11.9 %eval_jaxpr.9 = bf16[3,32,640]{2,1,0:T(8,128)(2,1)S(1)} custom-call(bf16[3,32,640]{2,1,0:T(8,128)(2,1)} %fusion.69.x_ref), custom_call_target="tpu_custom_call" | custom-call | tf_op jit(solution)/shard_map/while/body/eval_jaxpr/pallas_call | solution.py:58
  273.2 11.9 %eval_jaxpr.9 = bf16[3,32,640]{2,1,0:T(8,128)(2,1)S(1)} custom-call(bf16[3,32,640]{2,1,0:T(8,128)(2,1)} %fusion.69.x_ref), custom_call_target="tpu_custom_call" | custom-call | tf_op jit(solution)/shard_map/while/body/eval_jaxpr/pallas_call | solution.py:58
  295.7 12.0 %eval_jaxpr.9 = bf16[3,32,640]{2,1,0:T(8,128)(2,1)S(1)} custom-call(bf16[3,32,640]{2,1,0:T(8,128)(2,1)} %fusion.69.x_ref), custom_call_target="tpu_custom_call" | custom-call | tf_op jit(solution)/shard_map/while/body/eval_jaxpr/pallas_call | solution.py:58
  318.3 11.9 %eval_jaxpr.9 = bf16[3,32,640]{2,1,0:T(8,128)(2,1)S(1)} custom-call(bf16[3,32,640]{2,1,0:T(8,128)(2,1)} %fusion.69.x_ref), custom_call_target="tpu_custom_call" | custom-call | tf_op jit(solution)/shard_map/while/body/eval_jaxpr/pallas_call | solution.py:58
  340.8 11.9 %eval_jaxpr.9 = bf16[3,32,640]{2,1,0:T(8,128)(2,1)S(1)} custom-call(bf16[3,32,640]{2,1,0:T(8,128)(2,1)} %fusion.69.x_ref), custom_call_target="tpu_custom_call" | custom-call | tf_op jit(solution)/shard_map/while/body/eval_jaxpr/pallas_call | solution.py:58
  363.3 11.9 %eval_jaxpr.9 = bf16[3,32,640]{2,1,0:T(8,128)(2,1)S(1)} custom-call(bf16[3,32,640]{2,1,0:T(8,128)(2,1)} %fusion.69.x_ref), custom_call_target="tpu_custom_call" | custom-call | tf_op jit(solution)/shard_map/while/body/eval_jaxpr/pallas_call | solution.py:58
  378.0 318.3 %while.38 = (s32[]{:T(128)}, bf16[3,32,640]{2,1,0:T(8,128)(2,1)S(1)}, bf16[7,3,32,640]{3,2,1,0:T(8,128)(2,1)}, bf16[7,3,32,640]{3,2,1,0:T(8,128)(2,1)}, pred[]{:...) while((s32[]{:T(128)}, ...), condition=%wide.region_6.7_spmd, body=%wide.region_3.6_spmd.sunk | while | flops 946099520 | bytes 26898296 | solution.py:325
  392.5 12.4 %eval_jaxpr.10 = bf16[3,32,640]{2,1,0:T(8,128)(2,1)S(1)} custom-call(bf16[3,32,640]{2,1,0:T(8,128)(2,1)} %fusion.78.x_ref), custom_call_target="tpu_custom_call" | custom-call | tf_op jit(solution)/shard_map/while/body/eval_jaxpr/pallas_call | solution.py:58
  445.3 12.2 %eval_jaxpr.10 = bf16[3,32,640]{2,1,0:T(8,128)(2,1)S(1)} custom-call(bf16[3,32,640]{2,1,0:T(8,128)(2,1)} %fusion.78.x_ref), custom_call_target="tpu_custom_call" | custom-call | tf_op jit(solution)/shard_map/while/body/eval_jaxpr/pallas_call | solution.py:58
  472.0 11.9 %eval_jaxpr.10 = bf16[3,32,640]{2,1,0:T(8,128)(2,1)S(1)} custom-call(bf16[3,32,640]{2,1,0:T(8,128)(2,1)} %fusion.78.x_ref), custom_call_target="tpu_custom_call" | custom-call | tf_op jit(solution)/shard_map/while/body/eval_jaxpr/pallas_call | solution.py:58
  498.4 11.9 %eval_jaxpr.10 = bf16[3,32,640]{2,1,0:T(8,128)(2,1)S(1)} custom-call(bf16[3,32,640]{2,1,0:T(8,128)(2,1)} %fusion.78.x_ref), custom_call_target="tpu_custom_call" | custom-call | tf_op jit(solution)/shard_map/while/body/eval_jaxpr/pallas_call | solution.py:58
  524.8 11.9 %eval_jaxpr.10 = bf16[3,32,640]{2,1,0:T(8,128)(2,1)S(1)} custom-call(bf16[3,32,640]{2,1,0:T(8,128)(2,1)} %fusion.78.x_ref), custom_call_target="tpu_custom_call" | custom-call | tf_op jit(solution)/shard_map/while/body/eval_jaxpr/pallas_call | solution.py:58
  551.2 11.9 %eval_jaxpr.10 = bf16[3,32,640]{2,1,0:T(8,128)(2,1)S(1)} custom-call(bf16[3,32,640]{2,1,0:T(8,128)(2,1)} %fusion.78.x_ref), custom_call_target="tpu_custom_call" | custom-call | tf_op jit(solution)/shard_map/while/body/eval_jaxpr/pallas_call | solution.py:58
  577.5 13.3 %eval_jaxpr.10 = bf16[3,32,640]{2,1,0:T(8,128)(2,1)S(1)} custom-call(bf16[3,32,640]{2,1,0:T(8,128)(2,1)} %fusion.78.x_ref), custom_call_target="tpu_custom_call" | custom-call | tf_op jit(solution)/shard_map/while/body/eval_jaxpr/pallas_call | solution.py:58
  605.2 11.9 %eval_jaxpr.10 = bf16[3,32,640]{2,1,0:T(8,128)(2,1)S(1)} custom-call(bf16[3,32,640]{2,1,0:T(8,128)(2,1)} %fusion.78.x_ref), custom_call_target="tpu_custom_call" | custom-call | tf_op jit(solution)/shard_map/while/body/eval_jaxpr/pallas_call | solution.py:58
  631.6 12.3 %eval_jaxpr.10 = bf16[3,32,640]{2,1,0:T(8,128)(2,1)S(1)} custom-call(bf16[3,32,640]{2,1,0:T(8,128)(2,1)} %fusion.78.x_ref), custom_call_target="tpu_custom_call" | custom-call | tf_op jit(solution)/shard_map/while/body/eval_jaxpr/pallas_call | solution.py:58
  684.5 11.9 %eval_jaxpr.10 = bf16[3,32,640]{2,1,0:T(8,128)(2,1)S(1)} custom-call(bf16[3,32,640]{2,1,0:T(8,128)(2,1)} %fusion.78.x_ref), custom_call_target="tpu_custom_call" | custom-call | tf_op jit(solution)/shard_map/while/body/eval_jaxpr/pallas_call | solution.py:58
  760.2 217.5 %shard_map.68 = f32[240,640]{1,0:T(8,128)S(1)} custom-call(bf16[32,240,640]{2,1,0:T(8,128)(2,1)} %pad_maximum_fusion.part_hbm), custom_call_target="tpu_custom_call" | custom-call | tf_op jit(solution)/shard_map/pallas_call | solution.py:232
  (685 shorter events, 420.4 us)
Async XLA Ops:
  7.2 76.9 %all-gather.3.cloned.1.call-start = ((), (), s32[]{:S(2)}) async-start(), calls=%async_computation | async-start | bytes 10137600 | tf_op jit(solution)/shard_map/all_gather | solution.py:261
  111.4 4.7 copy-start
  132.0 4.7 copy-start
  155.3 4.7 copy-start
  177.1 4.7 copy-start
  199.6 4.7 copy-start
  222.1 4.7 copy-start
  244.7 4.7 copy-start
  267.2 4.7 copy-start
  289.8 4.7 copy-start
  312.3 4.7 copy-start
  334.9 4.7 copy-start
  357.4 4.7 copy-start
  698.4 2.3 copy-start.7
  730.7 2.5 copy-start.6
  730.8 2.6 copy-start.5
  732.0 1.6 copy-start.4
  733.2 1.1 copy-start.3
  733.4 1.2 copy-start.2
  733.5 1.3 copy-start.1
  733.6 1.4 copy-start.8
Sparse Core Ops, SparseCore 0:
  10.4 73.6 all-gather.2

commit v5 on v3

--- a/solution.py
+++ b/solution.py
@@ -248,9 +248,22 @@
     act_all = s_act[1 : micro_count + 1]
     pre_all = s_pre[1 : micro_count + 1].reshape(-1, channels)
     up_all = s_up[1 : micro_count + 1].reshape(-1, channels)
-    spatial_term = lax.dot_general(
-        spatial_columns(normed_all), pre_all, (((0,), (0,)), ((), ())),
-        preferred_element_type=jnp.float32,
+    grid_all = jnp.pad(
+        normed_all.reshape(micro_count, frames, HEIGHT, WIDTH, channels),
+        ((0, 0), (0, 0), (1, 1), (1, 1), (0, 0)),
+    )
+    spatial_term = jnp.concatenate(
+        [
+            lax.dot_general(
+                grid_all[:, :, row : row + HEIGHT, col : col + WIDTH, :].reshape(-1, channels),
+                pre_all,
+                (((0,), (0,)), ((), ())),
+                preferred_element_type=jnp.float32,
+            )
+            for row in range(3)
+            for col in range(3)
+        ],
+        axis=0,
     )
     temporal_term = lax.dot_general(
         temporal_columns(act_all), up_all, (((0,), (0,)), ((), ())),

time: 939 us -> 969 us (1.032)
  other arithmetic: 88.2 us -> 110 us
  matrix products: 175 us -> 186 us
    concatenate x117 -> x108, local copies, waits for them, and re-layouts: 21.2 us -> 3.48 us  [spatial_columns(): return jnp.concatenate(pieces, axis=-1).reshape(-1, 9 * channels)]
    convert_element_type x12, other arithmetic: 9.45 us -> 20.2 us  [section_backward(): (upstream.astype(jnp.float32) + pullback(norm_grad)[0]).astype(jnp.bfloat16)]
    reduce_sum x24, other arithmetic: 2.81 us -> 13.6 us  [normalize(): jnp.mean(summed * summed, axis=-1, keepdims=True) + 1e-06]
    dot_general x1 -> x9, matrix products: 7.01 us -> 17 us  [per_device(): lax.dot_general(grid_all[:, :, row:row + HEIGHT, col:col + WIDTH, :].resh...]
where the time goes in v5:
time: 969 us; the launch traced here: 961 us
  waiting for transfers between devices  286 us (30%)
  Pallas kernels  235 us (24%)
  matrix products  186 us (19%)
  local copies, waits for them, and re-layouts  111 us (11%)
  other arithmetic  110 us (11%)
  loops' own time  18.7 us (2%)
  between operations  14.2 us (1%)
    pallas_call x24, Pallas kernels, passed_along(): pl.pallas_call(functools.partial(hop_kernel, steps), out_shape=jax.ShapeD...  235 us
    reduce_scatter x1, waiting for transfers between devices, per_device(): lax.psum_scatter(partial_rows, 'dp', scatter_dimension=0, tiled=False)  210 us
    all_gather x1, waiting for transfers between devices, per_device(): gathered = lax.all_gather(own_rows, 'dp', axis=0, tiled=False)  76.1 us
    dot_general x12, matrix products, section_backward(): jnp.dot(pre_grad.reshape(frames * pixels, channels), spatial.T, preferred...  63.8 us
    dynamic_update_slice x48, other arithmetic, stash_put(): return lax.dynamic_update_index_in_dim(stash, value, slot, 0)  60.9 us
    dot_general x12, matrix products, section_forward(): jnp.dot(spatial_columns(normed), spatial, preferred_element_type=jnp.floa...  55.8 us
    dot_general x12, matrix products, section_backward(): jnp.dot(upstream_flat, temporal.T, preferred_element_type=jnp.float32)  30.2 us
    convert_element_type x12, other arithmetic, section_backward(): (upstream.astype(jnp.float32) + pullback(norm_grad)[0]).astype(jnp.bfloat16)  20.2 us
  transfers between devices with their start and end apart: 2, of which 2 were waited for; matrix products, arithmetic and copies ran while one was open for 0% of the time, Pallas kernels for 0%

profile of v5, /device:TPU:1, one launch (start us, length us, event | category | flops | bytes accessed | tf_op | source)
XLA Modules:
  0.0 961.2 jit_solution(14188394807405305412)
XLA Ops:
  9.9 76.1 %all-gather.3.cloned.1.call-done = bf16[7680,640]{1,0:T(8,128)(2,1)} async-done(((bf16[240,640]{1,0:T(8,128)(2,1)}), bf16[7680,640]{1,0:T(8,128)(2,1)}) %all-gather.3.cloned.1.call-update) | async-done | bytes 9830416 | tf_op jit(solution)/shard_map/all_gather | solution.py:181
  110.6 239.8 %while.37 = (s32[]{:T(128)}, bf16[3,32,640]{2,1,0:T(8,128)(2,1)S(1)}, bf16[7,3,32,640]{3,2,1,0:T(8,128)(2,1)}, bf16[7,3,32,640]{3,2,1,0:T(8,128)(2,1)S(1)}, f32[...) while((s32[]{:T(128)}, ...), condition=%wide.region_2.3_spmd, body=%wide.region_0.2_spmd.sunk | while | flops 945868928 | bytes 29384152 | solution.py:219
  185.8 11.0 %eval_jaxpr.9 = bf16[3,32,640]{2,1,0:T(8,128)(2,1)S(1)} custom-call(bf16[3,32,640]{2,1,0:T(8,128)(2,1)} %fusion.94.x_ref), custom_call_target="tpu_custom_call" | custom-call | tf_op jit(solution)/shard_map/while/body/eval_jaxpr/pallas_call | solution.py:58
  208.0 10.6 %eval_jaxpr.9 = bf16[3,32,640]{2,1,0:T(8,128)(2,1)S(1)} custom-call(bf16[3,32,640]{2,1,0:T(8,128)(2,1)} %fusion.94.x_ref), custom_call_target="tpu_custom_call" | custom-call | tf_op jit(solution)/shard_map/while/body/eval_jaxpr/pallas_call | solution.py:58
  229.9 10.7 %eval_jaxpr.9 = bf16[3,32,640]{2,1,0:T(8,128)(2,1)S(1)} custom-call(bf16[3,32,640]{2,1,0:T(8,128)(2,1)} %fusion.94.x_ref), custom_call_target="tpu_custom_call" | custom-call | tf_op jit(solution)/shard_map/while/body/eval_jaxpr/pallas_call | solution.py:58
  251.9 10.7 %eval_jaxpr.9 = bf16[3,32,640]{2,1,0:T(8,128)(2,1)S(1)} custom-call(bf16[3,32,640]{2,1,0:T(8,128)(2,1)} %fusion.94.x_ref), custom_call_target="tpu_custom_call" | custom-call | tf_op jit(solution)/shard_map/while/body/eval_jaxpr/pallas_call | solution.py:58
  273.8 10.7 %eval_jaxpr.9 = bf16[3,32,640]{2,1,0:T(8,128)(2,1)S(1)} custom-call(bf16[3,32,640]{2,1,0:T(8,128)(2,1)} %fusion.94.x_ref), custom_call_target="tpu_custom_call" | custom-call | tf_op jit(solution)/shard_map/while/body/eval_jaxpr/pallas_call | solution.py:58
  295.8 10.6 %eval_jaxpr.9 = bf16[3,32,640]{2,1,0:T(8,128)(2,1)S(1)} custom-call(bf16[3,32,640]{2,1,0:T(8,128)(2,1)} %fusion.94.x_ref), custom_call_target="tpu_custom_call" | custom-call | tf_op jit(solution)/shard_map/while/body/eval_jaxpr/pallas_call | solution.py:58
  317.7 10.7 %eval_jaxpr.9 = bf16[3,32,640]{2,1,0:T(8,128)(2,1)S(1)} custom-call(bf16[3,32,640]{2,1,0:T(8,128)(2,1)} %fusion.94.x_ref), custom_call_target="tpu_custom_call" | custom-call | tf_op jit(solution)/shard_map/while/body/eval_jaxpr/pallas_call | solution.py:58
  339.7 10.7 %eval_jaxpr.9 = bf16[3,32,640]{2,1,0:T(8,128)(2,1)S(1)} custom-call(bf16[3,32,640]{2,1,0:T(8,128)(2,1)} %fusion.94.x_ref), custom_call_target="tpu_custom_call" | custom-call | tf_op jit(solution)/shard_map/while/body/eval_jaxpr/pallas_call | solution.py:58
  352.6 325.1 %while.38 = (s32[]{:T(128)}, bf16[3,32,640]{2,1,0:T(8,128)(2,1)S(1)}, bf16[7,3,32,640]{3,2,1,0:T(8,128)(2,1)}, bf16[7,3,32,640]{3,2,1,0:T(8,128)(2,1)}, pred[]{:...) while((s32[]{:T(128)}, ...), condition=%wide.region_6.7_spmd, body=%wide.region_3.6_spmd.sunk | while | flops 946099520 | bytes 26898288 | solution.py:245
  368.8 11.1 %eval_jaxpr.10 = bf16[3,32,640]{2,1,0:T(8,128)(2,1)S(1)} custom-call(bf16[3,32,640]{2,1,0:T(8,128)(2,1)} %fusion.103.x_ref), custom_call_target="tpu_custom_call" | custom-call | tf_op jit(solution)/shard_map/while/body/eval_jaxpr/pallas_call | solution.py:58
  396.1 11.1 %eval_jaxpr.10 = bf16[3,32,640]{2,1,0:T(8,128)(2,1)S(1)} custom-call(bf16[3,32,640]{2,1,0:T(8,128)(2,1)} %fusion.103.x_ref), custom_call_target="tpu_custom_call" | custom-call | tf_op jit(solution)/shard_map/while/body/eval_jaxpr/pallas_call | solution.py:58
  423.4 11.1 %eval_jaxpr.10 = bf16[3,32,640]{2,1,0:T(8,128)(2,1)S(1)} custom-call(bf16[3,32,640]{2,1,0:T(8,128)(2,1)} %fusion.103.x_ref), custom_call_target="tpu_custom_call" | custom-call | tf_op jit(solution)/shard_map/while/body/eval_jaxpr/pallas_call | solution.py:58
  450.7 11.1 %eval_jaxpr.10 = bf16[3,32,640]{2,1,0:T(8,128)(2,1)S(1)} custom-call(bf16[3,32,640]{2,1,0:T(8,128)(2,1)} %fusion.103.x_ref), custom_call_target="tpu_custom_call" | custom-call | tf_op jit(solution)/shard_map/while/body/eval_jaxpr/pallas_call | solution.py:58
  478.0 10.7 %eval_jaxpr.10 = bf16[3,32,640]{2,1,0:T(8,128)(2,1)S(1)} custom-call(bf16[3,32,640]{2,1,0:T(8,128)(2,1)} %fusion.103.x_ref), custom_call_target="tpu_custom_call" | custom-call | tf_op jit(solution)/shard_map/while/body/eval_jaxpr/pallas_call | solution.py:58
  504.9 10.7 %eval_jaxpr.10 = bf16[3,32,640]{2,1,0:T(8,128)(2,1)S(1)} custom-call(bf16[3,32,640]{2,1,0:T(8,128)(2,1)} %fusion.103.x_ref), custom_call_target="tpu_custom_call" | custom-call | tf_op jit(solution)/shard_map/while/body/eval_jaxpr/pallas_call | solution.py:58
  531.8 10.7 %eval_jaxpr.10 = bf16[3,32,640]{2,1,0:T(8,128)(2,1)S(1)} custom-call(bf16[3,32,640]{2,1,0:T(8,128)(2,1)} %fusion.103.x_ref), custom_call_target="tpu_custom_call" | custom-call | tf_op jit(solution)/shard_map/while/body/eval_jaxpr/pallas_call | solution.py:58
  558.6 10.8 %eval_jaxpr.10 = bf16[3,32,640]{2,1,0:T(8,128)(2,1)S(1)} custom-call(bf16[3,32,640]{2,1,0:T(8,128)(2,1)} %fusion.103.x_ref), custom_call_target="tpu_custom_call" | custom-call | tf_op jit(solution)/shard_map/while/body/eval_jaxpr/pallas_call | solution.py:58
  585.6 10.5 %eval_jaxpr.10 = bf16[3,32,640]{2,1,0:T(8,128)(2,1)S(1)} custom-call(bf16[3,32,640]{2,1,0:T(8,128)(2,1)} %fusion.103.x_ref), custom_call_target="tpu_custom_call" | custom-call | tf_op jit(solution)/shard_map/while/body/eval_jaxpr/pallas_call | solution.py:58
  612.4 10.7 %eval_jaxpr.10 = bf16[3,32,640]{2,1,0:T(8,128)(2,1)S(1)} custom-call(bf16[3,32,640]{2,1,0:T(8,128)(2,1)} %fusion.103.x_ref), custom_call_target="tpu_custom_call" | custom-call | tf_op jit(solution)/shard_map/while/body/eval_jaxpr/pallas_call | solution.py:58
  639.3 10.7 %eval_jaxpr.10 = bf16[3,32,640]{2,1,0:T(8,128)(2,1)S(1)} custom-call(bf16[3,32,640]{2,1,0:T(8,128)(2,1)} %fusion.103.x_ref), custom_call_target="tpu_custom_call" | custom-call | tf_op jit(solution)/shard_map/while/body/eval_jaxpr/pallas_call | solution.py:58
  666.1 11.5 %eval_jaxpr.10 = bf16[3,32,640]{2,1,0:T(8,128)(2,1)S(1)} custom-call(bf16[3,32,640]{2,1,0:T(8,128)(2,1)} %fusion.103.x_ref), custom_call_target="tpu_custom_call" | custom-call | tf_op jit(solution)/shard_map/while/body/eval_jaxpr/pallas_call | solution.py:58
  740.7 209.8 %reduce-scatter.2.cloned.1.call-done = bf16[1,240,640]{2,1,0:T(8,128)(2,1)} async-done(((bf16[32,240,640]{2,1,0:T(8,128)(2,1)}), bf16[1,240,640]{2,1,0:T(8,128)(2,1)}) %reduce-scatter.2.cloned.1.call-update) | async-done | bytes 307216 | tf_op jit(solution)/shard_map/reduce_scatter | solution.py:279
  (688 shorter events, 426.2 us)
Async XLA Ops:
  7.2 78.9 %all-gather.3.cloned.1.call-start = ((), (), s32[]{:S(2)}) async-start(), calls=%async_computation.2 | async-start | bytes 10137600 | tf_op jit(solution)/shard_map/all_gather | solution.py:181
  9.0 941.5 %reduce-scatter.2.cloned.1.call-start = ((), (), s32[]{:S(2)}) async-start(), calls=%async_computation.1 | async-start | bytes 10137600 | tf_op jit(solution)/shard_map/reduce_scatter | solution.py:279
  114.6 6.1 copy-start.3
  130.3 6.1 copy-start.3
  146.6 6.1 copy-start.3
  162.5 6.1 copy-start.3
  178.5 6.1 copy-start.3
  200.7 6.1 copy-start.3
  222.6 6.1 copy-start.3
  244.6 6.1 copy-start.3
  266.5 6.1 copy-start.3
  288.5 6.1 copy-start.3
  310.4 6.1 copy-start.3
  332.4 6.1 copy-start.3
  350.4 1.2 copy-start
  696.0 3.0 copy-start.4
  696.0 3.0 copy-start.9
  696.0 4.7 copy-start.8
  699.0 3.2 copy-start.5
  700.6 3.2 copy-start.1
  707.6 1.3 copy-start.6
  708.8 1.6 copy-start.7
  715.3 8.8 copy-start.2
Sparse Core Ops, SparseCore 0:
  10.4 75.5 all-gather.2
  740.8 209.5 reduce-scatter.1

commit v6 on v1

--- a/solution.py
+++ b/solution.py
@@ -134,40 +134,24 @@
     def stash_put(stash, value, slot):
         return lax.dynamic_update_index_in_dim(stash, value, slot, 0)
 
-    def forward_step(carry, moment):
-        incoming, s_in, s_normed, s_preact, s_act = carry
+    def forward_step(incoming, moment):
         position = moment - section_index
         picked = jnp.clip(position, 0, micro_count - 1)
-        slot = slot_of(position)
         own = lax.dynamic_index_in_dim(samples, picked, 0, keepdims=False)
         embedding = lax.dynamic_index_in_dim(embeddings, picked, 0, keepdims=False)
         block_in = jnp.where(section_index == 0, own, incoming)
         result, normed, preact, activated = section_forward(
             block_in, embedding, full_spatial, full_temporal
         )
-        s_in = stash_put(s_in, block_in, slot)
-        s_normed = stash_put(s_normed, normed.reshape(frames, pixels, channels), slot)
-        s_preact = stash_put(s_preact, preact, slot)
-        s_act = stash_put(s_act, activated, slot)
         passed = passed_along(result, "pipe", 1)
-        return ((passed, s_in, s_normed, s_preact, s_act), None)
-
-    slots = micro_count + 2
-    start = (
-        blank,
-        jnp.zeros((slots, frames, pixels, channels), jnp.bfloat16),
-        jnp.zeros((slots, frames, pixels, channels), jnp.bfloat16),
-        jnp.zeros((slots, frames, pixels, channels), jnp.float32),
-        jnp.zeros((slots, frames, pixels, channels), jnp.bfloat16),
-    )
-    (_, s_in, s_normed, s_preact, s_act), _ = lax.scan(forward_step, start, moments)
-
-    def backward_step(carry, moment):
-        incoming, s_pre, s_up = carry
+        return passed, (block_in, normed.reshape(frames, pixels, channels), preact, activated)
+
+    _, (s_in, s_normed, s_preact, s_act) = lax.scan(forward_step, blank, moments)
+
+    def backward_step(incoming, moment):
         position = moment - (sections - 1 - section_index)
         picked = jnp.clip(position, 0, micro_count - 1)
-        slot = slot_of(position)
-        stored = jnp.clip(position, 0, micro_count - 1) + 1
+        stored = picked + section_index
         block_in = lax.dynamic_index_in_dim(s_in, stored, 0, keepdims=False)
         preact = lax.dynamic_index_in_dim(s_preact, stored, 0, keepdims=False)
         embedding = lax.dynamic_index_in_dim(embeddings, picked, 0, keepdims=False)
@@ -176,22 +160,16 @@
         back_input, pre_grad = section_backward(
             block_in, embedding, full_spatial, full_temporal, upstream, preact
         )
-        s_pre = stash_put(s_pre, pre_grad, slot)
-        s_up = stash_put(s_up, upstream, slot)
         passed = passed_along(back_input, "pipe", -1)
-        return ((passed, s_pre, s_up), None)
-
-    start = (
-        blank,
-        jnp.zeros((slots, frames, pixels, channels), jnp.bfloat16),
-        jnp.zeros((slots, frames, pixels, channels), jnp.bfloat16),
-    )
-    (_, s_pre, s_up), _ = lax.scan(backward_step, start, moments)
-
-    normed_all = s_normed[1 : micro_count + 1]
-    act_all = s_act[1 : micro_count + 1]
-    pre_all = s_pre[1 : micro_count + 1].reshape(-1, channels)
-    up_all = s_up[1 : micro_count + 1].reshape(-1, channels)
+        return passed, (pre_grad, upstream)
+
+    _, (s_pre, s_up) = lax.scan(backward_step, blank, moments)
+
+    normed_all = lax.dynamic_slice_in_dim(s_normed, section_index, micro_count, 0)
+    act_all = lax.dynamic_slice_in_dim(s_act, section_index, micro_count, 0)
+    back_first = sections - 1 - section_index
+    pre_all = lax.dynamic_slice_in_dim(s_pre, back_first, micro_count, 0).reshape(-1, channels)
+    up_all = lax.dynamic_slice_in_dim(s_up, back_first, micro_count, 0).reshape(-1, channels)
     spatial_term = lax.dot_general(
         spatial_columns(normed_all), pre_all, (((0,), (0,)), ((), ())),
         preferred_element_type=jnp.float32,

time: 938 us -> 941 us (level)
  local copies, waits for them, and re-layouts: 114 us -> 125 us
  transfers between devices with their start and end apart: 26 -> 26, of which waited for: 26 -> 26; matrix products, arithmetic and copies ran while one was open for 1% -> 2% of each run, Pallas kernels for 0% -> 0%
where the time goes in v6:
time: 941 us; the launch traced here: 934 us
  waiting for transfers between devices  419 us (45%)
  matrix products  168 us (18%)
  local copies, waits for them, and re-layouts  125 us (13%)
  starting transfers between devices  109 us (12%)
  other arithmetic  80.3 us (9%)
  loops' own time  18.5 us (2%)
  between operations  14.2 us (2%)
    reduce_scatter x1, waiting for transfers between devices, per_device(): lax.psum_scatter(partial_rows, 'dp', scatter_dimension=0, tiled=False)  208 us
    ppermute x24, waiting for transfers between devices, passed_along(): lax.ppermute(value, axis, [(source, source + steps) for source in range(f...  135 us
    ppermute x24, starting transfers between devices, passed_along(): lax.ppermute(value, axis, [(source, source + steps) for source in range(f...  109 us
    all_gather x1, waiting for transfers between devices, per_device(): gathered = lax.all_gather(own_rows, 'dp', axis=0, tiled=False)  76.1 us
    dot_general x12, matrix products, section_backward(): jnp.dot(pre_grad.reshape(frames * pixels, channels), spatial.T, preferred...  63.8 us
    dynamic_update_slice x48, other arithmetic, per_device(): lax.scan(forward_step, blank, moments)  60.1 us
    dot_general x12, matrix products, section_forward(): jnp.dot(spatial_columns(normed), spatial, preferred_element_type=jnp.floa...  55.9 us
    dot_general x12, matrix products, section_backward(): jnp.dot(upstream_flat, temporal.T, preferred_element_type=jnp.float32)  30.3 us
  transfers between devices with their start and end apart: 26, of which 26 were waited for; matrix products, arithmetic and copies ran while one was open for 2% of the time, Pallas kernels for 0%

profile of v6, /device:TPU:1, one launch (start us, length us, event | category | flops | bytes accessed | tf_op | source)
XLA Modules:
  0.0 934.2 jit_solution(14308658162504371301)
XLA Ops:
  9.9 76.1 %all-gather.3.cloned.1.call-done = bf16[7680,640]{1,0:T(8,128)(2,1)} async-done(((bf16[240,640]{1,0:T(8,128)(2,1)}), bf16[7680,640]{1,0:T(8,128)(2,1)}) %all-gather.3.cloned.1.call-update) | async-done | bytes 9830416 | tf_op jit(solution)/shard_map/all_gather | solution.py:125
  109.6 226.6 %while.36 = (s32[]{:T(128)}, bf16[3,32,640]{2,1,0:T(8,128)(2,1)S(1)}, bf16[12,3,32,640]{3,2,1,0:T(8,128)(2,1)S(1)}, bf16[12,3,32,640]{3,2,1,0:T(8,128)(2,1)}, f3...) while((s32[]{:T(128)}, ...), condition=%wide.region_2.3_spmd, body=%wide.region_0.2_spmd.sunk | while | flops 945868928 | bytes 29871912 | solution.py:149
  178.3 10.1 %collective-permute-start = (bf16[3,32,640]{2,1,0:T(8,128)(2,1)S(1)}, bf16[3,32,640]{2,1,0:T(8,128)(2,1)S(1)}, u32[]{:S(2)}, u32[]{:S(2)}) collective-permute-start(bf16[3,32,640]{2,1,0:T(8,128)(2,1)S(1)} %fusion.70), channel_id=1, source_target_pairs={{0,32},{32,64},{64,96},{96,128},{128,160},{160,192},{192,224},{1,3... | collective-permute-start | bytes 368648 | tf_op jit(solution)/shard_map/while/body/eval_jaxpr/ppermute | solution.py:15
  199.5 9.8 %collective-permute-start = (bf16[3,32,640]{2,1,0:T(8,128)(2,1)S(1)}, bf16[3,32,640]{2,1,0:T(8,128)(2,1)S(1)}, u32[]{:S(2)}, u32[]{:S(2)}) collective-permute-start(bf16[3,32,640]{2,1,0:T(8,128)(2,1)S(1)} %fusion.70), channel_id=1, source_target_pairs={{0,32},{32,64},{64,96},{96,128},{128,160},{160,192},{192,224},{1,3... | collective-permute-start | bytes 368648 | tf_op jit(solution)/shard_map/while/body/eval_jaxpr/ppermute | solution.py:15
  220.3 9.8 %collective-permute-start = (bf16[3,32,640]{2,1,0:T(8,128)(2,1)S(1)}, bf16[3,32,640]{2,1,0:T(8,128)(2,1)S(1)}, u32[]{:S(2)}, u32[]{:S(2)}) collective-permute-start(bf16[3,32,640]{2,1,0:T(8,128)(2,1)S(1)} %fusion.70), channel_id=1, source_target_pairs={{0,32},{32,64},{64,96},{96,128},{128,160},{160,192},{192,224},{1,3... | collective-permute-start | bytes 368648 | tf_op jit(solution)/shard_map/while/body/eval_jaxpr/ppermute | solution.py:15
  241.1 9.8 %collective-permute-start = (bf16[3,32,640]{2,1,0:T(8,128)(2,1)S(1)}, bf16[3,32,640]{2,1,0:T(8,128)(2,1)S(1)}, u32[]{:S(2)}, u32[]{:S(2)}) collective-permute-start(bf16[3,32,640]{2,1,0:T(8,128)(2,1)S(1)} %fusion.70), channel_id=1, source_target_pairs={{0,32},{32,64},{64,96},{96,128},{128,160},{160,192},{192,224},{1,3... | collective-permute-start | bytes 368648 | tf_op jit(solution)/shard_map/while/body/eval_jaxpr/ppermute | solution.py:15
  262.0 9.8 %collective-permute-start = (bf16[3,32,640]{2,1,0:T(8,128)(2,1)S(1)}, bf16[3,32,640]{2,1,0:T(8,128)(2,1)S(1)}, u32[]{:S(2)}, u32[]{:S(2)}) collective-permute-start(bf16[3,32,640]{2,1,0:T(8,128)(2,1)S(1)} %fusion.70), channel_id=1, source_target_pairs={{0,32},{32,64},{64,96},{96,128},{128,160},{160,192},{192,224},{1,3... | collective-permute-start | bytes 368648 | tf_op jit(solution)/shard_map/while/body/eval_jaxpr/ppermute | solution.py:15
  282.9 9.8 %collective-permute-start = (bf16[3,32,640]{2,1,0:T(8,128)(2,1)S(1)}, bf16[3,32,640]{2,1,0:T(8,128)(2,1)S(1)}, u32[]{:S(2)}, u32[]{:S(2)}) collective-permute-start(bf16[3,32,640]{2,1,0:T(8,128)(2,1)S(1)} %fusion.70), channel_id=1, source_target_pairs={{0,32},{32,64},{64,96},{96,128},{128,160},{160,192},{192,224},{1,3... | collective-permute-start | bytes 368648 | tf_op jit(solution)/shard_map/while/body/eval_jaxpr/ppermute | solution.py:15
  303.7 9.8 %collective-permute-start = (bf16[3,32,640]{2,1,0:T(8,128)(2,1)S(1)}, bf16[3,32,640]{2,1,0:T(8,128)(2,1)S(1)}, u32[]{:S(2)}, u32[]{:S(2)}) collective-permute-start(bf16[3,32,640]{2,1,0:T(8,128)(2,1)S(1)} %fusion.70), channel_id=1, source_target_pairs={{0,32},{32,64},{64,96},{96,128},{128,160},{160,192},{192,224},{1,3... | collective-permute-start | bytes 368648 | tf_op jit(solution)/shard_map/while/body/eval_jaxpr/ppermute | solution.py:15
  324.6 9.8 %collective-permute-start = (bf16[3,32,640]{2,1,0:T(8,128)(2,1)S(1)}, bf16[3,32,640]{2,1,0:T(8,128)(2,1)S(1)}, u32[]{:S(2)}, u32[]{:S(2)}) collective-permute-start(bf16[3,32,640]{2,1,0:T(8,128)(2,1)S(1)} %fusion.70), channel_id=1, source_target_pairs={{0,32},{32,64},{64,96},{96,128},{128,160},{160,192},{192,224},{1,3... | collective-permute-start | bytes 368648 | tf_op jit(solution)/shard_map/while/body/eval_jaxpr/ppermute | solution.py:15
  342.2 309.6 %while.37 = (s32[]{:T(128)}, bf16[3,32,640]{2,1,0:T(8,128)(2,1)S(1)}, bf16[12,3,32,640]{3,2,1,0:T(8,128)(2,1)}, bf16[12,3,32,640]{3,2,1,0:T(8,128)(2,1)}, pred[]...) while((s32[]{:T(128)}, ...), condition=%wide.region_6.7_spmd, body=%wide.region_3.6_spmd.sunk | while | flops 946099520 | bytes 27390788 | solution.py:166
  357.3 10.7 %collective-permute-done.1 = bf16[3,32,640]{2,1,0:T(8,128)(2,1)S(1)} collective-permute-done((bf16[3,32,640]{2,1,0:T(8,128)(2,1)S(1)}, bf16[3,32,640]{2,1,0:T(8,128)(2,1)S(1)}, u32[]{:S(2)}, u32[]{:S(2)}) %collective-permute-start.1) | collective-permute-done | bytes 122912 | tf_op jit(solution)/shard_map/while/body/eval_jaxpr/ppermute | solution.py:15
  383.1 10.8 %collective-permute-done.1 = bf16[3,32,640]{2,1,0:T(8,128)(2,1)S(1)} collective-permute-done((bf16[3,32,640]{2,1,0:T(8,128)(2,1)S(1)}, bf16[3,32,640]{2,1,0:T(8,128)(2,1)S(1)}, u32[]{:S(2)}, u32[]{:S(2)}) %collective-permute-start.1) | collective-permute-done | bytes 122912 | tf_op jit(solution)/shard_map/while/body/eval_jaxpr/ppermute | solution.py:15
  408.9 10.7 %collective-permute-done.1 = bf16[3,32,640]{2,1,0:T(8,128)(2,1)S(1)} collective-permute-done((bf16[3,32,640]{2,1,0:T(8,128)(2,1)S(1)}, bf16[3,32,640]{2,1,0:T(8,128)(2,1)S(1)}, u32[]{:S(2)}, u32[]{:S(2)}) %collective-permute-start.1) | collective-permute-done | bytes 122912 | tf_op jit(solution)/shard_map/while/body/eval_jaxpr/ppermute | solution.py:15
  434.7 10.7 %collective-permute-done.1 = bf16[3,32,640]{2,1,0:T(8,128)(2,1)S(1)} collective-permute-done((bf16[3,32,640]{2,1,0:T(8,128)(2,1)S(1)}, bf16[3,32,640]{2,1,0:T(8,128)(2,1)S(1)}, u32[]{:S(2)}, u32[]{:S(2)}) %collective-permute-start.1) | collective-permute-done | bytes 122912 | tf_op jit(solution)/shard_map/while/body/eval_jaxpr/ppermute | solution.py:15
  460.5 10.3 %collective-permute-done.1 = bf16[3,32,640]{2,1,0:T(8,128)(2,1)S(1)} collective-permute-done((bf16[3,32,640]{2,1,0:T(8,128)(2,1)S(1)}, bf16[3,32,640]{2,1,0:T(8,128)(2,1)S(1)}, u32[]{:S(2)}, u32[]{:S(2)}) %collective-permute-start.1) | collective-permute-done | bytes 122912 | tf_op jit(solution)/shard_map/while/body/eval_jaxpr/ppermute | solution.py:15
  485.9 10.3 %collective-permute-done.1 = bf16[3,32,640]{2,1,0:T(8,128)(2,1)S(1)} collective-permute-done((bf16[3,32,640]{2,1,0:T(8,128)(2,1)S(1)}, bf16[3,32,640]{2,1,0:T(8,128)(2,1)S(1)}, u32[]{:S(2)}, u32[]{:S(2)}) %collective-permute-start.1) | collective-permute-done | bytes 122912 | tf_op jit(solution)/shard_map/while/body/eval_jaxpr/ppermute | solution.py:15
  511.3 10.3 %collective-permute-done.1 = bf16[3,32,640]{2,1,0:T(8,128)(2,1)S(1)} collective-permute-done((bf16[3,32,640]{2,1,0:T(8,128)(2,1)S(1)}, bf16[3,32,640]{2,1,0:T(8,128)(2,1)S(1)}, u32[]{:S(2)}, u32[]{:S(2)}) %collective-permute-start.1) | collective-permute-done | bytes 122912 | tf_op jit(solution)/shard_map/while/body/eval_jaxpr/ppermute | solution.py:15
  536.7 10.3 %collective-permute-done.1 = bf16[3,32,640]{2,1,0:T(8,128)(2,1)S(1)} collective-permute-done((bf16[3,32,640]{2,1,0:T(8,128)(2,1)S(1)}, bf16[3,32,640]{2,1,0:T(8,128)(2,1)S(1)}, u32[]{:S(2)}, u32[]{:S(2)}) %collective-permute-start.1) | collective-permute-done | bytes 122912 | tf_op jit(solution)/shard_map/while/body/eval_jaxpr/ppermute | solution.py:15
  562.1 10.3 %collective-permute-done.1 = bf16[3,32,640]{2,1,0:T(8,128)(2,1)S(1)} collective-permute-done((bf16[3,32,640]{2,1,0:T(8,128)(2,1)S(1)}, bf16[3,32,640]{2,1,0:T(8,128)(2,1)S(1)}, u32[]{:S(2)}, u32[]{:S(2)}) %collective-permute-start.1) | collective-permute-done | bytes 122912 | tf_op jit(solution)/shard_map/while/body/eval_jaxpr/ppermute | solution.py:15
  587.5 10.3 %collective-permute-done.1 = bf16[3,32,640]{2,1,0:T(8,128)(2,1)S(1)} collective-permute-done((bf16[3,32,640]{2,1,0:T(8,128)(2,1)S(1)}, bf16[3,32,640]{2,1,0:T(8,128)(2,1)S(1)}, u32[]{:S(2)}, u32[]{:S(2)}) %collective-permute-start.1) | collective-permute-done | bytes 122912 | tf_op jit(solution)/shard_map/while/body/eval_jaxpr/ppermute | solution.py:15
  612.9 11.4 %collective-permute-done.1 = bf16[3,32,640]{2,1,0:T(8,128)(2,1)S(1)} collective-permute-done((bf16[3,32,640]{2,1,0:T(8,128)(2,1)S(1)}, bf16[3,32,640]{2,1,0:T(8,128)(2,1)S(1)}, u32[]{:S(2)}, u32[]{:S(2)}) %collective-permute-start.1) | collective-permute-done | bytes 122912 | tf_op jit(solution)/shard_map/while/body/eval_jaxpr/ppermute | solution.py:15
  639.4 12.4 %collective-permute-done.1 = bf16[3,32,640]{2,1,0:T(8,128)(2,1)S(1)} collective-permute-done((bf16[3,32,640]{2,1,0:T(8,128)(2,1)S(1)}, bf16[3,32,640]{2,1,0:T(8,128)(2,1)S(1)}, u32[]{:S(2)}, u32[]{:S(2)}) %collective-permute-start.1) | collective-permute-done | bytes 122912 | tf_op jit(solution)/shard_map/while/body/eval_jaxpr/ppermute | solution.py:15
  715.6 207.8 %reduce-scatter.2.cloned.1.call-done = bf16[1,240,640]{2,1,0:T(8,128)(2,1)} async-done(((bf16[32,240,640]{2,1,0:T(8,128)(2,1)}), bf16[1,240,640]{2,1,0:T(8,128)(2,1)}) %reduce-scatter.2.cloned.1.call-update) | async-done | bytes 307216 | tf_op jit(solution)/shard_map/reduce_scatter | solution.py:188
  (708 shorter events, 410.1 us)
Async XLA Ops:
  7.2 78.9 %all-gather.3.cloned.1.call-start = ((), (), s32[]{:S(2)}) async-start(), calls=%async_computation.2 | async-start | bytes 10137600 | tf_op jit(solution)/shard_map/all_gather | solution.py:125
  9.0 914.4 %reduce-scatter.2.cloned.1.call-start = ((), (), s32[]{:S(2)}) async-start(), calls=%async_computation.1 | async-start | bytes 10137600 | tf_op jit(solution)/shard_map/reduce_scatter | solution.py:188
  133.4 6.0 collective-permute-start
  163.4 5.6 collective-permute-start
  178.3 12.0 %collective-permute-start = (bf16[3,32,640]{2,1,0:T(8,128)(2,1)S(1)}, bf16[3,32,640]{2,1,0:T(8,128)(2,1)S(1)}, u32[]{:S(2)}, u32[]{:S(2)}) collective-permute-start(bf16[3,32,640]{2,1,0:T(8,128)(2,1)S(1)} %fusion.70), channel_id=1, source_target_pairs={{0,32},{32,64},{64,96},{96,128},{128,160},{160,192},{192,224},{1,3... | collective-permute-start | bytes 368648 | tf_op jit(solution)/shard_map/while/body/eval_jaxpr/ppermute | solution.py:15
  199.5 11.6 %collective-permute-start = (bf16[3,32,640]{2,1,0:T(8,128)(2,1)S(1)}, bf16[3,32,640]{2,1,0:T(8,128)(2,1)S(1)}, u32[]{:S(2)}, u32[]{:S(2)}) collective-permute-start(bf16[3,32,640]{2,1,0:T(8,128)(2,1)S(1)} %fusion.70), channel_id=1, source_target_pairs={{0,32},{32,64},{64,96},{96,128},{128,160},{160,192},{192,224},{1,3... | collective-permute-start | bytes 368648 | tf_op jit(solution)/shard_map/while/body/eval_jaxpr/ppermute | solution.py:15
  220.3 11.6 %collective-permute-start = (bf16[3,32,640]{2,1,0:T(8,128)(2,1)S(1)}, bf16[3,32,640]{2,1,0:T(8,128)(2,1)S(1)}, u32[]{:S(2)}, u32[]{:S(2)}) collective-permute-start(bf16[3,32,640]{2,1,0:T(8,128)(2,1)S(1)} %fusion.70), channel_id=1, source_target_pairs={{0,32},{32,64},{64,96},{96,128},{128,160},{160,192},{192,224},{1,3... | collective-permute-start | bytes 368648 | tf_op jit(solution)/shard_map/while/body/eval_jaxpr/ppermute | solution.py:15
  241.1 11.7 %collective-permute-start = (bf16[3,32,640]{2,1,0:T(8,128)(2,1)S(1)}, bf16[3,32,640]{2,1,0:T(8,128)(2,1)S(1)}, u32[]{:S(2)}, u32[]{:S(2)}) collective-permute-start(bf16[3,32,640]{2,1,0:T(8,128)(2,1)S(1)} %fusion.70), channel_id=1, source_target_pairs={{0,32},{32,64},{64,96},{96,128},{128,160},{160,192},{192,224},{1,3... | collective-permute-start | bytes 368648 | tf_op jit(solution)/shard_map/while/body/eval_jaxpr/ppermute | solution.py:15
  262.0 11.6 %collective-permute-start = (bf16[3,32,640]{2,1,0:T(8,128)(2,1)S(1)}, bf16[3,32,640]{2,1,0:T(8,128)(2,1)S(1)}, u32[]{:S(2)}, u32[]{:S(2)}) collective-permute-start(bf16[3,32,640]{2,1,0:T(8,128)(2,1)S(1)} %fusion.70), channel_id=1, source_target_pairs={{0,32},{32,64},{64,96},{96,128},{128,160},{160,192},{192,224},{1,3... | collective-permute-start | bytes 368648 | tf_op jit(solution)/shard_map/while/body/eval_jaxpr/ppermute | solution.py:15
  282.9 11.6 %collective-permute-start = (bf16[3,32,640]{2,1,0:T(8,128)(2,1)S(1)}, bf16[3,32,640]{2,1,0:T(8,128)(2,1)S(1)}, u32[]{:S(2)}, u32[]{:S(2)}) collective-permute-start(bf16[3,32,640]{2,1,0:T(8,128)(2,1)S(1)} %fusion.70), channel_id=1, source_target_pairs={{0,32},{32,64},{64,96},{96,128},{128,160},{160,192},{192,224},{1,3... | collective-permute-start | bytes 368648 | tf_op jit(solution)/shard_map/while/body/eval_jaxpr/ppermute | solution.py:15
  303.7 11.7 %collective-permute-start = (bf16[3,32,640]{2,1,0:T(8,128)(2,1)S(1)}, bf16[3,32,640]{2,1,0:T(8,128)(2,1)S(1)}, u32[]{:S(2)}, u32[]{:S(2)}) collective-permute-start(bf16[3,32,640]{2,1,0:T(8,128)(2,1)S(1)} %fusion.70), channel_id=1, source_target_pairs={{0,32},{32,64},{64,96},{96,128},{128,160},{160,192},{192,224},{1,3... | collective-permute-start | bytes 368648 | tf_op jit(solution)/shard_map/while/body/eval_jaxpr/ppermute | solution.py:15
  324.6 11.6 %collective-permute-start = (bf16[3,32,640]{2,1,0:T(8,128)(2,1)S(1)}, bf16[3,32,640]{2,1,0:T(8,128)(2,1)S(1)}, u32[]{:S(2)}, u32[]{:S(2)}) collective-permute-start(bf16[3,32,640]{2,1,0:T(8,128)(2,1)S(1)} %fusion.70), channel_id=1, source_target_pairs={{0,32},{32,64},{64,96},{96,128},{128,160},{160,192},{192,224},{1,3... | collective-permute-start | bytes 368648 | tf_op jit(solution)/shard_map/while/body/eval_jaxpr/ppermute | solution.py:15
  356.0 12.0 %collective-permute-start.1 = (bf16[3,32,640]{2,1,0:T(8,128)(2,1)S(1)}, bf16[3,32,640]{2,1,0:T(8,128)(2,1)S(1)}, u32[]{:S(2)}, u32[]{:S(2)}) collective-permute-start(bf16[3,32,640]{2,1,0:T(8,128)(2,1)S(1)} %fusion.79), channel_id=1, source_target_pairs={{32,0},{64,32},{96,64},{128,96},{160,128},{192,160},{224,192},{33,... | collective-permute-start | bytes 368648 | tf_op jit(solution)/shard_map/while/body/eval_jaxpr/ppermute | solution.py:15
  381.8 12.1 %collective-permute-start.1 = (bf16[3,32,640]{2,1,0:T(8,128)(2,1)S(1)}, bf16[3,32,640]{2,1,0:T(8,128)(2,1)S(1)}, u32[]{:S(2)}, u32[]{:S(2)}) collective-permute-start(bf16[3,32,640]{2,1,0:T(8,128)(2,1)S(1)} %fusion.79), channel_id=1, source_target_pairs={{32,0},{64,32},{96,64},{128,96},{160,128},{192,160},{224,192},{33,... | collective-permute-start | bytes 368648 | tf_op jit(solution)/shard_map/while/body/eval_jaxpr/ppermute | solution.py:15
  407.6 12.0 %collective-permute-start.1 = (bf16[3,32,640]{2,1,0:T(8,128)(2,1)S(1)}, bf16[3,32,640]{2,1,0:T(8,128)(2,1)S(1)}, u32[]{:S(2)}, u32[]{:S(2)}) collective-permute-start(bf16[3,32,640]{2,1,0:T(8,128)(2,1)S(1)} %fusion.79), channel_id=1, source_target_pairs={{32,0},{64,32},{96,64},{128,96},{160,128},{192,160},{224,192},{33,... | collective-permute-start | bytes 368648 | tf_op jit(solution)/shard_map/while/body/eval_jaxpr/ppermute | solution.py:15
  433.4 12.0 %collective-permute-start.1 = (bf16[3,32,640]{2,1,0:T(8,128)(2,1)S(1)}, bf16[3,32,640]{2,1,0:T(8,128)(2,1)S(1)}, u32[]{:S(2)}, u32[]{:S(2)}) collective-permute-start(bf16[3,32,640]{2,1,0:T(8,128)(2,1)S(1)} %fusion.79), channel_id=1, source_target_pairs={{32,0},{64,32},{96,64},{128,96},{160,128},{192,160},{224,192},{33,... | collective-permute-start | bytes 368648 | tf_op jit(solution)/shard_map/while/body/eval_jaxpr/ppermute | solution.py:15
  459.2 11.6 %collective-permute-start.1 = (bf16[3,32,640]{2,1,0:T(8,128)(2,1)S(1)}, bf16[3,32,640]{2,1,0:T(8,128)(2,1)S(1)}, u32[]{:S(2)}, u32[]{:S(2)}) collective-permute-start(bf16[3,32,640]{2,1,0:T(8,128)(2,1)S(1)} %fusion.79), channel_id=1, source_target_pairs={{32,0},{64,32},{96,64},{128,96},{160,128},{192,160},{224,192},{33,... | collective-permute-start | bytes 368648 | tf_op jit(solution)/shard_map/while/body/eval_jaxpr/ppermute | solution.py:15
  484.6 11.6 %collective-permute-start.1 = (bf16[3,32,640]{2,1,0:T(8,128)(2,1)S(1)}, bf16[3,32,640]{2,1,0:T(8,128)(2,1)S(1)}, u32[]{:S(2)}, u32[]{:S(2)}) collective-permute-start(bf16[3,32,640]{2,1,0:T(8,128)(2,1)S(1)} %fusion.79), channel_id=1, source_target_pairs={{32,0},{64,32},{96,64},{128,96},{160,128},{192,160},{224,192},{33,... | collective-permute-start | bytes 368648 | tf_op jit(solution)/shard_map/while/body/eval_jaxpr/ppermute | solution.py:15
  510.0 11.6 %collective-permute-start.1 = (bf16[3,32,640]{2,1,0:T(8,128)(2,1)S(1)}, bf16[3,32,640]{2,1,0:T(8,128)(2,1)S(1)}, u32[]{:S(2)}, u32[]{:S(2)}) collective-permute-start(bf16[3,32,640]{2,1,0:T(8,128)(2,1)S(1)} %fusion.79), channel_id=1, source_target_pairs={{32,0},{64,32},{96,64},{128,96},{160,128},{192,160},{224,192},{33,... | collective-permute-start | bytes 368648 | tf_op jit(solution)/shard_map/while/body/eval_jaxpr/ppermute | solution.py:15
  535.4 11.6 %collective-permute-start.1 = (bf16[3,32,640]{2,1,0:T(8,128)(2,1)S(1)}, bf16[3,32,640]{2,1,0:T(8,128)(2,1)S(1)}, u32[]{:S(2)}, u32[]{:S(2)}) collective-permute-start(bf16[3,32,640]{2,1,0:T(8,128)(2,1)S(1)} %fusion.79), channel_id=1, source_target_pairs={{32,0},{64,32},{96,64},{128,96},{160,128},{192,160},{224,192},{33,... | collective-permute-start | bytes 368648 | tf_op jit(solution)/shard_map/while/body/eval_jaxpr/ppermute | solution.py:15
  560.8 11.6 %collective-permute-start.1 = (bf16[3,32,640]{2,1,0:T(8,128)(2,1)S(1)}, bf16[3,32,640]{2,1,0:T(8,128)(2,1)S(1)}, u32[]{:S(2)}, u32[]{:S(2)}) collective-permute-start(bf16[3,32,640]{2,1,0:T(8,128)(2,1)S(1)} %fusion.79), channel_id=1, source_target_pairs={{32,0},{64,32},{96,64},{128,96},{160,128},{192,160},{224,192},{33,... | collective-permute-start | bytes 368648 | tf_op jit(solution)/shard_map/while/body/eval_jaxpr/ppermute | solution.py:15
  586.2 11.6 %collective-permute-start.1 = (bf16[3,32,640]{2,1,0:T(8,128)(2,1)S(1)}, bf16[3,32,640]{2,1,0:T(8,128)(2,1)S(1)}, u32[]{:S(2)}, u32[]{:S(2)}) collective-permute-start(bf16[3,32,640]{2,1,0:T(8,128)(2,1)S(1)} %fusion.79), channel_id=1, source_target_pairs={{32,0},{64,32},{96,64},{128,96},{160,128},{192,160},{224,192},{33,... | collective-permute-start | bytes 368648 | tf_op jit(solution)/shard_map/while/body/eval_jaxpr/ppermute | solution.py:15
  611.6 12.7 %collective-permute-start.1 = (bf16[3,32,640]{2,1,0:T(8,128)(2,1)S(1)}, bf16[3,32,640]{2,1,0:T(8,128)(2,1)S(1)}, u32[]{:S(2)}, u32[]{:S(2)}) collective-permute-start(bf16[3,32,640]{2,1,0:T(8,128)(2,1)S(1)} %fusion.79), channel_id=1, source_target_pairs={{32,0},{64,32},{96,64},{128,96},{160,128},{192,160},{224,192},{33,... | collective-permute-start | bytes 368648 | tf_op jit(solution)/shard_map/while/body/eval_jaxpr/ppermute | solution.py:15
  638.1 13.7 %collective-permute-start.1 = (bf16[3,32,640]{2,1,0:T(8,128)(2,1)S(1)}, bf16[3,32,640]{2,1,0:T(8,128)(2,1)S(1)}, u32[]{:S(2)}, u32[]{:S(2)}) collective-permute-start(bf16[3,32,640]{2,1,0:T(8,128)(2,1)S(1)} %fusion.79), channel_id=1, source_target_pairs={{32,0},{64,32},{96,64},{128,96},{160,128},{192,160},{224,192},{33,... | collective-permute-start | bytes 368648 | tf_op jit(solution)/shard_map/while/body/eval_jaxpr/ppermute | solution.py:15
  (21 other events, 78.3 us)
Sparse Core Ops, SparseCore 0:
  10.4 75.5 all-gather.2
  715.7 207.6 reduce-scatter.1

commit v7 on v1

--- a/solution.py
+++ b/solution.py
@@ -193,18 +193,15 @@
     pre_all = s_pre[1 : micro_count + 1].reshape(-1, channels)
     up_all = s_up[1 : micro_count + 1].reshape(-1, channels)
     spatial_term = lax.dot_general(
-        spatial_columns(normed_all), pre_all, (((0,), (0,)), ((), ())),
+        spatial_columns(normed_all).reshape(-1, n_dp, sp_rows), pre_all, (((0,), (0,)), ((), ())),
         preferred_element_type=jnp.float32,
     )
     temporal_term = lax.dot_general(
-        temporal_columns(act_all), up_all, (((0,), (0,)), ((), ())),
+        temporal_columns(act_all).reshape(-1, n_dp, tm_rows), up_all, (((0,), (0,)), ((), ())),
         preferred_element_type=jnp.float32,
     )
     partial_rows = jnp.concatenate(
-        [
-            spatial_term.astype(jnp.bfloat16).reshape(n_dp, sp_rows, channels),
-            temporal_term.astype(jnp.bfloat16).reshape(n_dp, tm_rows, channels),
-        ],
+        [spatial_term.astype(jnp.bfloat16), temporal_term.astype(jnp.bfloat16)],
         axis=1,
     )
     share = lax.psum_scatter(partial_rows, "dp", scatter_dimension=0, tiled=False)

time: 938 us -> 948 us (1.011)
  local copies, waits for them, and re-layouts: 114 us -> 141 us
  other arithmetic: 80.2 us -> 53.8 us
  matrix products: 167 us -> 183 us
    another operation x5 -> x7, local copies, waits for them, and re-layouts: 3.15 us -> 39.8 us  [the longest x1 25.5 us: per_device(): spatial_columns(normed_all).reshape(-1, n_dp, sp_rows)]
    dynamic_update_slice x48, other arithmetic: 60 us -> 37.3 us  [stash_put(): return lax.dynamic_update_index_in_dim(stash, value, slot, 0)]
    concatenate x117 -> x109, local copies, waits for them, and re-layouts: 21.2 us -> 4.75 us  [spatial_columns(): return jnp.concatenate(pieces, axis=-1).reshape(-1, 9 * channels)]
    dot_general x2, matrix products: 10.2 us -> 26 us  [the longest x1 20.8 us: per_device(): lax.dot_general(spatial_columns(normed_all).reshape(-1, n_dp, sp_rows), p...]
    reshape x2 -> x0, local copies, waits for them, and re-layouts: 11.4 us -> none  [the longest x1 8.76 us: per_device(): spatial_term.astype(jnp.bfloat16).reshape(n_dp, sp_rows, channels)]
    while x120 -> x168, local copies, waits for them, and re-layouts: 1.93 us -> 13 us
  transfers between devices with their start and end apart: 26 -> 26, of which waited for: 26 -> 26; matrix products, arithmetic and copies ran while one was open for 1% -> 2% of each run, Pallas kernels for 0% -> 0%
where the time goes in v7:
time: 948 us; the launch traced here: 939 us
  waiting for transfers between devices  419 us (44%)
  matrix products  183 us (19%)
  local copies, waits for them, and re-layouts  141 us (15%)
  starting transfers between devices  109 us (11%)
  other arithmetic  53.8 us (6%)
  loops' own time  18.9 us (2%)
  between operations  14.4 us (2%)
    reduce_scatter x1, waiting for transfers between devices, per_device(): lax.psum_scatter(partial_rows, 'dp', scatter_dimension=0, tiled=False)  208 us
    ppermute x24, waiting for transfers between devices, passed_along(): lax.ppermute(value, axis, [(source, source + steps) for source in range(f...  135 us
    ppermute x24, starting transfers between devices, passed_along(): lax.ppermute(value, axis, [(source, source + steps) for source in range(f...  109 us
    all_gather x1, waiting for transfers between devices, per_device(): gathered = lax.all_gather(own_rows, 'dp', axis=0, tiled=False)  76.1 us
    dot_general x12, matrix products, section_backward(): jnp.dot(pre_grad.reshape(frames * pixels, channels), spatial.T, preferred...  63.8 us
    dot_general x12, matrix products, section_forward(): jnp.dot(spatial_columns(normed), spatial, preferred_element_type=jnp.floa...  55.8 us
    dynamic_update_slice x48, other arithmetic, stash_put(): return lax.dynamic_update_index_in_dim(stash, value, slot, 0)  37.3 us
    dot_general x12, matrix products, section_backward(): jnp.dot(upstream_flat, temporal.T, preferred_element_type=jnp.float32)  30.3 us
  transfers between devices with their start and end apart: 26, of which 26 were waited for; matrix products, arithmetic and copies ran while one was open for 2% of the time, Pallas kernels for 0%

profile of v7, /device:TPU:1, one launch (start us, length us, event | category | flops | bytes accessed | tf_op | source)
XLA Modules:
  0.0 939.4 jit_solution(12707945821360926602)
XLA Ops:
  9.9 76.1 %all-gather.3.cloned.1.call-done = bf16[7680,640]{1,0:T(8,128)(2,1)} async-done(((bf16[240,640]{1,0:T(8,128)(2,1)}), bf16[7680,640]{1,0:T(8,128)(2,1)}) %all-gather.3.cloned.1.call-update) | async-done | bytes 9830416 | tf_op jit(solution)/shard_map/all_gather | solution.py:125
  110.0 230.4 %while.37 = (s32[]{:T(128)}, bf16[3,32,640]{2,1,0:T(8,128)(2,1)S(1)}, bf16[7,3,32,640]{3,2,1,0:T(8,128)(2,1)S(1)}, bf16[7,3,32,640]{3,2,1,0:T(8,128)(2,1)S(1)}, ...) while((s32[]{:T(128)}, ...), condition=%wide.region_2.3_spmd, body=%wide.region_0.2_spmd.sunk | while | flops 945868928 | bytes 36756536 | solution.py:163
  180.3 10.1 %collective-permute-start = (bf16[3,32,640]{2,1,0:T(8,128)(2,1)S(1)}, bf16[3,32,640]{2,1,0:T(8,128)(2,1)S(1)}, u32[]{:S(2)}, u32[]{:S(2)}) collective-permute-start(bf16[3,32,640]{2,1,0:T(8,128)(2,1)S(1)} %fusion.80), channel_id=1, source_target_pairs={{0,32},{32,64},{64,96},{96,128},{128,160},{160,192},{192,224},{1,3... | collective-permute-start | bytes 368648 | tf_op jit(solution)/shard_map/while/body/eval_jaxpr/ppermute | solution.py:15
  201.8 9.8 %collective-permute-start = (bf16[3,32,640]{2,1,0:T(8,128)(2,1)S(1)}, bf16[3,32,640]{2,1,0:T(8,128)(2,1)S(1)}, u32[]{:S(2)}, u32[]{:S(2)}) collective-permute-start(bf16[3,32,640]{2,1,0:T(8,128)(2,1)S(1)} %fusion.80), channel_id=1, source_target_pairs={{0,32},{32,64},{64,96},{96,128},{128,160},{160,192},{192,224},{1,3... | collective-permute-start | bytes 368648 | tf_op jit(solution)/shard_map/while/body/eval_jaxpr/ppermute | solution.py:15
  265.2 9.8 %collective-permute-start = (bf16[3,32,640]{2,1,0:T(8,128)(2,1)S(1)}, bf16[3,32,640]{2,1,0:T(8,128)(2,1)S(1)}, u32[]{:S(2)}, u32[]{:S(2)}) collective-permute-start(bf16[3,32,640]{2,1,0:T(8,128)(2,1)S(1)} %fusion.80), channel_id=1, source_target_pairs={{0,32},{32,64},{64,96},{96,128},{128,160},{160,192},{192,224},{1,3... | collective-permute-start | bytes 368648 | tf_op jit(solution)/shard_map/while/body/eval_jaxpr/ppermute | solution.py:15
  286.4 9.8 %collective-permute-start = (bf16[3,32,640]{2,1,0:T(8,128)(2,1)S(1)}, bf16[3,32,640]{2,1,0:T(8,128)(2,1)S(1)}, u32[]{:S(2)}, u32[]{:S(2)}) collective-permute-start(bf16[3,32,640]{2,1,0:T(8,128)(2,1)S(1)} %fusion.80), channel_id=1, source_target_pairs={{0,32},{32,64},{64,96},{96,128},{128,160},{160,192},{192,224},{1,3... | collective-permute-start | bytes 368648 | tf_op jit(solution)/shard_map/while/body/eval_jaxpr/ppermute | solution.py:15
  328.7 9.8 %collective-permute-start = (bf16[3,32,640]{2,1,0:T(8,128)(2,1)S(1)}, bf16[3,32,640]{2,1,0:T(8,128)(2,1)S(1)}, u32[]{:S(2)}, u32[]{:S(2)}) collective-permute-start(bf16[3,32,640]{2,1,0:T(8,128)(2,1)S(1)} %fusion.80), channel_id=1, source_target_pairs={{0,32},{32,64},{64,96},{96,128},{128,160},{160,192},{192,224},{1,3... | collective-permute-start | bytes 368648 | tf_op jit(solution)/shard_map/while/body/eval_jaxpr/ppermute | solution.py:15
  341.5 294.5 %while.38 = (s32[]{:T(128)}, bf16[3,32,640]{2,1,0:T(8,128)(2,1)S(1)}, bf16[7,3,32,640]{3,2,1,0:T(8,128)(2,1)S(1)}, bf16[7,3,32,640]{3,2,1,0:T(8,128)(2,1)S(1)}, ...) while((s32[]{:T(128)}, ...), condition=%wide.region_6.7_spmd, body=%wide.region_3.6_spmd.sunk | while | flops 946099520 | bytes 27389336 | solution.py:189
  355.3 10.7 %collective-permute-done.1 = bf16[3,32,640]{2,1,0:T(8,128)(2,1)S(1)} collective-permute-done((bf16[3,32,640]{2,1,0:T(8,128)(2,1)S(1)}, bf16[3,32,640]{2,1,0:T(8,128)(2,1)S(1)}, u32[]{:S(2)}, u32[]{:S(2)}) %collective-permute-start.1) | collective-permute-done | bytes 122912 | tf_op jit(solution)/shard_map/while/body/eval_jaxpr/ppermute | solution.py:15
  379.8 10.7 %collective-permute-done.1 = bf16[3,32,640]{2,1,0:T(8,128)(2,1)S(1)} collective-permute-done((bf16[3,32,640]{2,1,0:T(8,128)(2,1)S(1)}, bf16[3,32,640]{2,1,0:T(8,128)(2,1)S(1)}, u32[]{:S(2)}, u32[]{:S(2)}) %collective-permute-start.1) | collective-permute-done | bytes 122912 | tf_op jit(solution)/shard_map/while/body/eval_jaxpr/ppermute | solution.py:15
  404.4 10.7 %collective-permute-done.1 = bf16[3,32,640]{2,1,0:T(8,128)(2,1)S(1)} collective-permute-done((bf16[3,32,640]{2,1,0:T(8,128)(2,1)S(1)}, bf16[3,32,640]{2,1,0:T(8,128)(2,1)S(1)}, u32[]{:S(2)}, u32[]{:S(2)}) %collective-permute-start.1) | collective-permute-done | bytes 122912 | tf_op jit(solution)/shard_map/while/body/eval_jaxpr/ppermute | solution.py:15
  428.9 10.7 %collective-permute-done.1 = bf16[3,32,640]{2,1,0:T(8,128)(2,1)S(1)} collective-permute-done((bf16[3,32,640]{2,1,0:T(8,128)(2,1)S(1)}, bf16[3,32,640]{2,1,0:T(8,128)(2,1)S(1)}, u32[]{:S(2)}, u32[]{:S(2)}) %collective-permute-start.1) | collective-permute-done | bytes 122912 | tf_op jit(solution)/shard_map/while/body/eval_jaxpr/ppermute | solution.py:15
  453.5 10.3 %collective-permute-done.1 = bf16[3,32,640]{2,1,0:T(8,128)(2,1)S(1)} collective-permute-done((bf16[3,32,640]{2,1,0:T(8,128)(2,1)S(1)}, bf16[3,32,640]{2,1,0:T(8,128)(2,1)S(1)}, u32[]{:S(2)}, u32[]{:S(2)}) %collective-permute-start.1) | collective-permute-done | bytes 122912 | tf_op jit(solution)/shard_map/while/body/eval_jaxpr/ppermute | solution.py:15
  477.6 10.3 %collective-permute-done.1 = bf16[3,32,640]{2,1,0:T(8,128)(2,1)S(1)} collective-permute-done((bf16[3,32,640]{2,1,0:T(8,128)(2,1)S(1)}, bf16[3,32,640]{2,1,0:T(8,128)(2,1)S(1)}, u32[]{:S(2)}, u32[]{:S(2)}) %collective-permute-start.1) | collective-permute-done | bytes 122912 | tf_op jit(solution)/shard_map/while/body/eval_jaxpr/ppermute | solution.py:15
  501.8 10.3 %collective-permute-done.1 = bf16[3,32,640]{2,1,0:T(8,128)(2,1)S(1)} collective-permute-done((bf16[3,32,640]{2,1,0:T(8,128)(2,1)S(1)}, bf16[3,32,640]{2,1,0:T(8,128)(2,1)S(1)}, u32[]{:S(2)}, u32[]{:S(2)}) %collective-permute-start.1) | collective-permute-done | bytes 122912 | tf_op jit(solution)/shard_map/while/body/eval_jaxpr/ppermute | solution.py:15
  525.9 10.3 %collective-permute-done.1 = bf16[3,32,640]{2,1,0:T(8,128)(2,1)S(1)} collective-permute-done((bf16[3,32,640]{2,1,0:T(8,128)(2,1)S(1)}, bf16[3,32,640]{2,1,0:T(8,128)(2,1)S(1)}, u32[]{:S(2)}, u32[]{:S(2)}) %collective-permute-start.1) | collective-permute-done | bytes 122912 | tf_op jit(solution)/shard_map/while/body/eval_jaxpr/ppermute | solution.py:15
  550.1 10.3 %collective-permute-done.1 = bf16[3,32,640]{2,1,0:T(8,128)(2,1)S(1)} collective-permute-done((bf16[3,32,640]{2,1,0:T(8,128)(2,1)S(1)}, bf16[3,32,640]{2,1,0:T(8,128)(2,1)S(1)}, u32[]{:S(2)}, u32[]{:S(2)}) %collective-permute-start.1) | collective-permute-done | bytes 122912 | tf_op jit(solution)/shard_map/while/body/eval_jaxpr/ppermute | solution.py:15
  574.2 11.6 %collective-permute-done.1 = bf16[3,32,640]{2,1,0:T(8,128)(2,1)S(1)} collective-permute-done((bf16[3,32,640]{2,1,0:T(8,128)(2,1)S(1)}, bf16[3,32,640]{2,1,0:T(8,128)(2,1)S(1)}, u32[]{:S(2)}, u32[]{:S(2)}) %collective-permute-start.1) | collective-permute-done | bytes 122912 | tf_op jit(solution)/shard_map/while/body/eval_jaxpr/ppermute | solution.py:15
  599.6 12.2 %collective-permute-done.1 = bf16[3,32,640]{2,1,0:T(8,128)(2,1)S(1)} collective-permute-done((bf16[3,32,640]{2,1,0:T(8,128)(2,1)S(1)}, bf16[3,32,640]{2,1,0:T(8,128)(2,1)S(1)}, u32[]{:S(2)}, u32[]{:S(2)}) %collective-permute-start.1) | collective-permute-done | bytes 122912 | tf_op jit(solution)/shard_map/while/body/eval_jaxpr/ppermute | solution.py:15
  625.6 10.3 %collective-permute-done.1 = bf16[3,32,640]{2,1,0:T(8,128)(2,1)S(1)} collective-permute-done((bf16[3,32,640]{2,1,0:T(8,128)(2,1)S(1)}, bf16[3,32,640]{2,1,0:T(8,128)(2,1)S(1)}, u32[]{:S(2)}, u32[]{:S(2)}) %collective-permute-start.1) | collective-permute-done | bytes 122912 | tf_op jit(solution)/shard_map/while/body/eval_jaxpr/ppermute | solution.py:15
  637.7 12.9 %reshape_reshape.7 = bf16[480,32,60]{2,1,0:T(8,128)(2,1)} reshape(bf16[5,3,32,1920]{3,2,1,0:T(8,128)(2,1)S(1)} %pad_maximum_fusion.1) | data formatting | bytes 3686400 | tf_op jit(solution)/shard_map/reshape;reshape | solution.py:200
  663.1 25.5 %reshape_reshape.6 = bf16[480,32,180]{2,1,0:T(8,128)(2,1)} reshape(bf16[5,3,8,4,5760]{4,3,2,1,0:T(4,128)(2,1)} %fusion.51) | data formatting | bytes 11059200 | tf_op jit(solution)/shard_map/reshape;reshape | solution.py:196
  693.8 20.8 %fusion.36 = bf16[32,180,640]{2,1,0:T(8,128)(2,1)S(1)} fusion(bf16[480,640,1]{1,0,2:T(8,128)(2,1)S(1)} %bitcast.187, bf16[480,32,180]{2,1,0:T(8,128)(2,1)} %reshape_reshape.6), kind=kOutput, calls=%fused_computation.95 | convolution fusion | flops 3542630400 | bytes 13516800 | tf_op jit(solution)/shard_map/dot_general | solution.py:195
  720.2 208.2 %reduce-scatter.2.cloned.1.call-done = bf16[1,240,640]{2,1,0:T(8,128)(2,1)} async-done(((bf16[32,240,640]{2,1,0:T(8,128)(2,1)}), bf16[1,240,640]{2,1,0:T(8,128)(2,1)}) %reduce-scatter.2.cloned.1.call-update) | async-done | bytes 307216 | tf_op jit(solution)/shard_map/reduce_scatter | solution.py:207
  (742 shorter events, 384.6 us)
Async XLA Ops:
  7.2 78.9 %all-gather.3.cloned.1.call-start = ((), (), s32[]{:S(2)}) async-start(), calls=%async_computation.2 | async-start | bytes 10137600 | tf_op jit(solution)/shard_map/all_gather | solution.py:125
  9.0 919.5 %reduce-scatter.2.cloned.1.call-start = ((), (), s32[]{:S(2)}) async-start(), calls=%async_computation.1 | async-start | bytes 10137600 | tf_op jit(solution)/shard_map/reduce_scatter | solution.py:207
  134.5 6.0 collective-permute-start
  150.0 5.6 collective-permute-start
  180.3 11.9 %collective-permute-start = (bf16[3,32,640]{2,1,0:T(8,128)(2,1)S(1)}, bf16[3,32,640]{2,1,0:T(8,128)(2,1)S(1)}, u32[]{:S(2)}, u32[]{:S(2)}) collective-permute-start(bf16[3,32,640]{2,1,0:T(8,128)(2,1)S(1)} %fusion.80), channel_id=1, source_target_pairs={{0,32},{32,64},{64,96},{96,128},{128,160},{160,192},{192,224},{1,3... | collective-permute-start | bytes 368648 | tf_op jit(solution)/shard_map/while/body/eval_jaxpr/ppermute | solution.py:15
  201.8 11.6 %collective-permute-start = (bf16[3,32,640]{2,1,0:T(8,128)(2,1)S(1)}, bf16[3,32,640]{2,1,0:T(8,128)(2,1)S(1)}, u32[]{:S(2)}, u32[]{:S(2)}) collective-permute-start(bf16[3,32,640]{2,1,0:T(8,128)(2,1)S(1)} %fusion.80), channel_id=1, source_target_pairs={{0,32},{32,64},{64,96},{96,128},{128,160},{160,192},{192,224},{1,3... | collective-permute-start | bytes 368648 | tf_op jit(solution)/shard_map/while/body/eval_jaxpr/ppermute | solution.py:15
  222.9 11.6 %collective-permute-start = (bf16[3,32,640]{2,1,0:T(8,128)(2,1)S(1)}, bf16[3,32,640]{2,1,0:T(8,128)(2,1)S(1)}, u32[]{:S(2)}, u32[]{:S(2)}) collective-permute-start(bf16[3,32,640]{2,1,0:T(8,128)(2,1)S(1)} %fusion.80), channel_id=1, source_target_pairs={{0,32},{32,64},{64,96},{96,128},{128,160},{160,192},{192,224},{1,3... | collective-permute-start | bytes 368648 | tf_op jit(solution)/shard_map/while/body/eval_jaxpr/ppermute | solution.py:15
  244.1 11.6 %collective-permute-start = (bf16[3,32,640]{2,1,0:T(8,128)(2,1)S(1)}, bf16[3,32,640]{2,1,0:T(8,128)(2,1)S(1)}, u32[]{:S(2)}, u32[]{:S(2)}) collective-permute-start(bf16[3,32,640]{2,1,0:T(8,128)(2,1)S(1)} %fusion.80), channel_id=1, source_target_pairs={{0,32},{32,64},{64,96},{96,128},{128,160},{160,192},{192,224},{1,3... | collective-permute-start | bytes 368648 | tf_op jit(solution)/shard_map/while/body/eval_jaxpr/ppermute | solution.py:15
  265.2 11.6 %collective-permute-start = (bf16[3,32,640]{2,1,0:T(8,128)(2,1)S(1)}, bf16[3,32,640]{2,1,0:T(8,128)(2,1)S(1)}, u32[]{:S(2)}, u32[]{:S(2)}) collective-permute-start(bf16[3,32,640]{2,1,0:T(8,128)(2,1)S(1)} %fusion.80), channel_id=1, source_target_pairs={{0,32},{32,64},{64,96},{96,128},{128,160},{160,192},{192,224},{1,3... | collective-permute-start | bytes 368648 | tf_op jit(solution)/shard_map/while/body/eval_jaxpr/ppermute | solution.py:15
  286.4 11.6 %collective-permute-start = (bf16[3,32,640]{2,1,0:T(8,128)(2,1)S(1)}, bf16[3,32,640]{2,1,0:T(8,128)(2,1)S(1)}, u32[]{:S(2)}, u32[]{:S(2)}) collective-permute-start(bf16[3,32,640]{2,1,0:T(8,128)(2,1)S(1)} %fusion.80), channel_id=1, source_target_pairs={{0,32},{32,64},{64,96},{96,128},{128,160},{160,192},{192,224},{1,3... | collective-permute-start | bytes 368648 | tf_op jit(solution)/shard_map/while/body/eval_jaxpr/ppermute | solution.py:15
  307.6 11.6 %collective-permute-start = (bf16[3,32,640]{2,1,0:T(8,128)(2,1)S(1)}, bf16[3,32,640]{2,1,0:T(8,128)(2,1)S(1)}, u32[]{:S(2)}, u32[]{:S(2)}) collective-permute-start(bf16[3,32,640]{2,1,0:T(8,128)(2,1)S(1)} %fusion.80), channel_id=1, source_target_pairs={{0,32},{32,64},{64,96},{96,128},{128,160},{160,192},{192,224},{1,3... | collective-permute-start | bytes 368648 | tf_op jit(solution)/shard_map/while/body/eval_jaxpr/ppermute | solution.py:15
  328.7 11.6 %collective-permute-start = (bf16[3,32,640]{2,1,0:T(8,128)(2,1)S(1)}, bf16[3,32,640]{2,1,0:T(8,128)(2,1)S(1)}, u32[]{:S(2)}, u32[]{:S(2)}) collective-permute-start(bf16[3,32,640]{2,1,0:T(8,128)(2,1)S(1)} %fusion.80), channel_id=1, source_target_pairs={{0,32},{32,64},{64,96},{96,128},{128,160},{160,192},{192,224},{1,3... | collective-permute-start | bytes 368648 | tf_op jit(solution)/shard_map/while/body/eval_jaxpr/ppermute | solution.py:15
  354.0 12.0 %collective-permute-start.1 = (bf16[3,32,640]{2,1,0:T(8,128)(2,1)S(1)}, bf16[3,32,640]{2,1,0:T(8,128)(2,1)S(1)}, u32[]{:S(2)}, u32[]{:S(2)}) collective-permute-start(bf16[3,32,640]{2,1,0:T(8,128)(2,1)S(1)} %fusion.89), channel_id=1, source_target_pairs={{32,0},{64,32},{96,64},{128,96},{160,128},{192,160},{224,192},{33,... | collective-permute-start | bytes 368648 | tf_op jit(solution)/shard_map/while/body/eval_jaxpr/ppermute | solution.py:15
  378.5 12.0 %collective-permute-start.1 = (bf16[3,32,640]{2,1,0:T(8,128)(2,1)S(1)}, bf16[3,32,640]{2,1,0:T(8,128)(2,1)S(1)}, u32[]{:S(2)}, u32[]{:S(2)}) collective-permute-start(bf16[3,32,640]{2,1,0:T(8,128)(2,1)S(1)} %fusion.89), channel_id=1, source_target_pairs={{32,0},{64,32},{96,64},{128,96},{160,128},{192,160},{224,192},{33,... | collective-permute-start | bytes 368648 | tf_op jit(solution)/shard_map/while/body/eval_jaxpr/ppermute | solution.py:15
  403.1 12.0 %collective-permute-start.1 = (bf16[3,32,640]{2,1,0:T(8,128)(2,1)S(1)}, bf16[3,32,640]{2,1,0:T(8,128)(2,1)S(1)}, u32[]{:S(2)}, u32[]{:S(2)}) collective-permute-start(bf16[3,32,640]{2,1,0:T(8,128)(2,1)S(1)} %fusion.89), channel_id=1, source_target_pairs={{32,0},{64,32},{96,64},{128,96},{160,128},{192,160},{224,192},{33,... | collective-permute-start | bytes 368648 | tf_op jit(solution)/shard_map/while/body/eval_jaxpr/ppermute | solution.py:15
  427.6 12.0 %collective-permute-start.1 = (bf16[3,32,640]{2,1,0:T(8,128)(2,1)S(1)}, bf16[3,32,640]{2,1,0:T(8,128)(2,1)S(1)}, u32[]{:S(2)}, u32[]{:S(2)}) collective-permute-start(bf16[3,32,640]{2,1,0:T(8,128)(2,1)S(1)} %fusion.89), channel_id=1, source_target_pairs={{32,0},{64,32},{96,64},{128,96},{160,128},{192,160},{224,192},{33,... | collective-permute-start | bytes 368648 | tf_op jit(solution)/shard_map/while/body/eval_jaxpr/ppermute | solution.py:15
  452.2 11.6 %collective-permute-start.1 = (bf16[3,32,640]{2,1,0:T(8,128)(2,1)S(1)}, bf16[3,32,640]{2,1,0:T(8,128)(2,1)S(1)}, u32[]{:S(2)}, u32[]{:S(2)}) collective-permute-start(bf16[3,32,640]{2,1,0:T(8,128)(2,1)S(1)} %fusion.89), channel_id=1, source_target_pairs={{32,0},{64,32},{96,64},{128,96},{160,128},{192,160},{224,192},{33,... | collective-permute-start | bytes 368648 | tf_op jit(solution)/shard_map/while/body/eval_jaxpr/ppermute | solution.py:15
  476.3 11.6 %collective-permute-start.1 = (bf16[3,32,640]{2,1,0:T(8,128)(2,1)S(1)}, bf16[3,32,640]{2,1,0:T(8,128)(2,1)S(1)}, u32[]{:S(2)}, u32[]{:S(2)}) collective-permute-start(bf16[3,32,640]{2,1,0:T(8,128)(2,1)S(1)} %fusion.89), channel_id=1, source_target_pairs={{32,0},{64,32},{96,64},{128,96},{160,128},{192,160},{224,192},{33,... | collective-permute-start | bytes 368648 | tf_op jit(solution)/shard_map/while/body/eval_jaxpr/ppermute | solution.py:15
  500.5 11.6 %collective-permute-start.1 = (bf16[3,32,640]{2,1,0:T(8,128)(2,1)S(1)}, bf16[3,32,640]{2,1,0:T(8,128)(2,1)S(1)}, u32[]{:S(2)}, u32[]{:S(2)}) collective-permute-start(bf16[3,32,640]{2,1,0:T(8,128)(2,1)S(1)} %fusion.89), channel_id=1, source_target_pairs={{32,0},{64,32},{96,64},{128,96},{160,128},{192,160},{224,192},{33,... | collective-permute-start | bytes 368648 | tf_op jit(solution)/shard_map/while/body/eval_jaxpr/ppermute | solution.py:15
  524.6 11.6 %collective-permute-start.1 = (bf16[3,32,640]{2,1,0:T(8,128)(2,1)S(1)}, bf16[3,32,640]{2,1,0:T(8,128)(2,1)S(1)}, u32[]{:S(2)}, u32[]{:S(2)}) collective-permute-start(bf16[3,32,640]{2,1,0:T(8,128)(2,1)S(1)} %fusion.89), channel_id=1, source_target_pairs={{32,0},{64,32},{96,64},{128,96},{160,128},{192,160},{224,192},{33,... | collective-permute-start | bytes 368648 | tf_op jit(solution)/shard_map/while/body/eval_jaxpr/ppermute | solution.py:15
  548.8 11.6 %collective-permute-start.1 = (bf16[3,32,640]{2,1,0:T(8,128)(2,1)S(1)}, bf16[3,32,640]{2,1,0:T(8,128)(2,1)S(1)}, u32[]{:S(2)}, u32[]{:S(2)}) collective-permute-start(bf16[3,32,640]{2,1,0:T(8,128)(2,1)S(1)} %fusion.89), channel_id=1, source_target_pairs={{32,0},{64,32},{96,64},{128,96},{160,128},{192,160},{224,192},{33,... | collective-permute-start | bytes 368648 | tf_op jit(solution)/shard_map/while/body/eval_jaxpr/ppermute | solution.py:15
  572.9 12.9 %collective-permute-start.1 = (bf16[3,32,640]{2,1,0:T(8,128)(2,1)S(1)}, bf16[3,32,640]{2,1,0:T(8,128)(2,1)S(1)}, u32[]{:S(2)}, u32[]{:S(2)}) collective-permute-start(bf16[3,32,640]{2,1,0:T(8,128)(2,1)S(1)} %fusion.89), channel_id=1, source_target_pairs={{32,0},{64,32},{96,64},{128,96},{160,128},{192,160},{224,192},{33,... | collective-permute-start | bytes 368648 | tf_op jit(solution)/shard_map/while/body/eval_jaxpr/ppermute | solution.py:15
  598.3 13.5 %collective-permute-start.1 = (bf16[3,32,640]{2,1,0:T(8,128)(2,1)S(1)}, bf16[3,32,640]{2,1,0:T(8,128)(2,1)S(1)}, u32[]{:S(2)}, u32[]{:S(2)}) collective-permute-start(bf16[3,32,640]{2,1,0:T(8,128)(2,1)S(1)} %fusion.89), channel_id=1, source_target_pairs={{32,0},{64,32},{96,64},{128,96},{160,128},{192,160},{224,192},{33,... | collective-permute-start | bytes 368648 | tf_op jit(solution)/shard_map/while/body/eval_jaxpr/ppermute | solution.py:15
  624.3 11.6 %collective-permute-start.1 = (bf16[3,32,640]{2,1,0:T(8,128)(2,1)S(1)}, bf16[3,32,640]{2,1,0:T(8,128)(2,1)S(1)}, u32[]{:S(2)}, u32[]{:S(2)}) collective-permute-start(bf16[3,32,640]{2,1,0:T(8,128)(2,1)S(1)} %fusion.89), channel_id=1, source_target_pairs={{32,0},{64,32},{96,64},{128,96},{160,128},{192,160},{224,192},{33,... | collective-permute-start | bytes 368648 | tf_op jit(solution)/shard_map/while/body/eval_jaxpr/ppermute | solution.py:15
  (41 other events, 218.4 us)
Sparse Core Ops, SparseCore 0:
  10.4 75.5 all-gather.2
  720.3 208.0 reduce-scatter.1

commit v8 on v1

--- a/solution.py
+++ b/solution.py
@@ -160,7 +160,7 @@
         jnp.zeros((slots, frames, pixels, channels), jnp.float32),
         jnp.zeros((slots, frames, pixels, channels), jnp.bfloat16),
     )
-    (_, s_in, s_normed, s_preact, s_act), _ = lax.scan(forward_step, start, moments)
+    (_, s_in, s_normed, s_preact, s_act), _ = lax.scan(forward_step, start, moments, unroll=2)
 
     def backward_step(carry, moment):
         incoming, s_pre, s_up = carry
@@ -186,7 +186,7 @@
         jnp.zeros((slots, frames, pixels, channels), jnp.bfloat16),
         jnp.zeros((slots, frames, pixels, channels), jnp.bfloat16),
     )
-    (_, s_pre, s_up), _ = lax.scan(backward_step, start, moments)
+    (_, s_pre, s_up), _ = lax.scan(backward_step, start, moments, unroll=2)
 
     normed_all = s_normed[1 : micro_count + 1]
     act_all = s_act[1 : micro_count + 1]

time: 938 us -> 1030 us (1.098)
  local copies, waits for them, and re-layouts: 114 us -> 216 us
  other arithmetic: 80.2 us -> 105 us
  matrix products: 167 us -> 145 us
    concatenate x117, local copies, waits for them, and re-layouts: 21.2 us -> 58.4 us  [spatial_columns(): return jnp.concatenate(pieces, axis=-1).reshape(-1, 9 * channels)]
    slice x13, local copies, waits for them, and re-layouts: 9.67 us -> 39.6 us  [spatial_columns(): padded[..., row:row + HEIGHT, col:col + WIDTH, :]]
    while x120 -> x96, local copies, waits for them, and re-layouts: 1.93 us -> 23.5 us
    dot_general x12, matrix products: 30.3 us -> 9.95 us  [section_backward(): jnp.dot(upstream_flat, temporal.T, preferred_element_type=jnp.float32)]
    dynamic_slice x24 -> x12, local copies, waits for them, and re-layouts: 14 us -> 0.86 us  [per_device(): lax.scan(forward_step, start, moments, unroll=2)]
    convert_element_type x12, other arithmetic: 1.58 us -> 12.4 us  [section_backward(): (upstream.astype(jnp.float32) + pullback(norm_grad)[0]).astype(jnp.bfloat16)]
    ppermute x24, waiting for transfers between devices: 143 us -> 132 us  [passed_along(): lax.ppermute(value, axis, [(source, source + steps) for source in range(f...]
  transfers between devices with their start and end apart: 26 -> 26, of which waited for: 26 -> 26; matrix products, arithmetic and copies ran while one was open for 1% -> 2% of each run, Pallas kernels for 0% -> 0%
where the time goes in v8:
time: 1030 us; the launch traced here: 1020 us
  waiting for transfers between devices  418 us (41%)
  local copies, waits for them, and re-layouts  216 us (21%)
  matrix products  145 us (14%)
  starting transfers between devices  109 us (11%)
  other arithmetic  105 us (10%)
  loops' own time  18.1 us (2%)
  between operations  14.3 us (1%)
    reduce_scatter x1, waiting for transfers between devices, per_device(): lax.psum_scatter(partial_rows, 'dp', scatter_dimension=0, tiled=False)  210 us
    ppermute x24, waiting for transfers between devices, passed_along(): lax.ppermute(value, axis, [(source, source + steps) for source in range(f...  132 us
    ppermute x24, starting transfers between devices, passed_along(): lax.ppermute(value, axis, [(source, source + steps) for source in range(f...  109 us
    all_gather x1, waiting for transfers between devices, per_device(): gathered = lax.all_gather(own_rows, 'dp', axis=0, tiled=False)  76.1 us
    dynamic_update_slice x48, other arithmetic, stash_put(): return lax.dynamic_update_index_in_dim(stash, value, slot, 0)  68.6 us
    dot_general x12, matrix products, section_backward(): jnp.dot(pre_grad.reshape(frames * pixels, channels), spatial.T, preferred...  63.8 us
    concatenate x117, local copies, waits for them, and re-layouts, spatial_columns(): return jnp.concatenate(pieces, axis=-1).reshape(-1, 9 * channels)  58.4 us
    dot_general x12, matrix products, section_forward(): jnp.dot(spatial_columns(normed), spatial, preferred_element_type=jnp.floa...  54 us
  transfers between devices with their start and end apart: 26, of which 26 were waited for; matrix products, arithmetic and copies ran while one was open for 2% of the time, Pallas kernels for 0%

profile of v8, /device:TPU:1, one launch (start us, length us, event | category | flops | bytes accessed | tf_op | source)
XLA Modules:
  0.0 1024.7 jit_solution(9265340951629094827)
XLA Ops:
  9.9 76.1 %all-gather.3.cloned.1.call-done = bf16[7680,640]{1,0:T(8,128)(2,1)} async-done(((bf16[240,640]{1,0:T(8,128)(2,1)}), bf16[7680,640]{1,0:T(8,128)(2,1)}) %all-gather.3.cloned.1.call-update) | async-done | bytes 9830416 | tf_op jit(solution)/shard_map/all_gather | solution.py:125
  113.4 324.7 %while.38 = (s32[]{:T(128)}, bf16[3,32,640]{2,1,0:T(8,128)(2,1)S(1)}, bf16[7,3,32,640]{3,2,1,0:T(8,128)(2,1)}, bf16[7,3,32,640]{3,2,1,0:T(8,128)(2,1)}, f32[7,3,...) while((s32[]{:T(128)}, ...), condition=%wide.region_3.4_spmd, body=%wide.region_0.3_spmd.sunk | while | flops 1891737856 | bytes 40084004 | solution.py:163
  223.9 10.1 collective-permute-start
  252.3 9.8 collective-permute-start.1
  282.3 9.8 collective-permute-start
  310.4 9.8 collective-permute-start.1
  340.3 9.8 collective-permute-start
  368.4 9.8 collective-permute-start.1
  398.4 9.8 collective-permute-start
  426.5 9.8 collective-permute-start.1
  440.2 300.3 %while.39 = (s32[]{:T(128)}, bf16[3,32,640]{2,1,0:T(8,128)(2,1)S(1)}, bf16[7,3,32,640]{3,2,1,0:T(8,128)(2,1)}, bf16[7,3,32,640]{3,2,1,0:T(8,128)(2,1)}, pred[]{:...) while((s32[]{:T(128)}, ...), condition=%wide.region_9.10_spmd, body=%wide.region_4.9_spmd.sunk | while | flops 1892199168 | bytes 54779536 | solution.py:189
  456.4 10.7 %collective-permute-done.2 = bf16[3,32,640]{2,1,0:T(8,128)(2,1)S(1)} collective-permute-done((bf16[3,32,640]{2,1,0:T(8,128)(2,1)S(1)}, bf16[3,32,640]{2,1,0:T(8,128)(2,1)S(1)}, u32[]{:S(2)}, u32[]{:S(2)}) %collective-permute-start.2) | collective-permute-done | bytes 122912 | tf_op jit(solution)/shard_map/while/body/eval_jaxpr/ppermute | solution.py:15
  479.8 10.8 %collective-permute-done.3 = bf16[3,32,640]{2,1,0:T(8,128)(2,1)S(1)} collective-permute-done((bf16[3,32,640]{2,1,0:T(8,128)(2,1)S(1)}, bf16[3,32,640]{2,1,0:T(8,128)(2,1)S(1)}, u32[]{:S(2)}, u32[]{:S(2)}) %collective-permute-start.3) | collective-permute-done | bytes 122912 | tf_op jit(solution)/shard_map/while/body/eval_jaxpr/ppermute | solution.py:15
  506.8 10.6 %collective-permute-done.2 = bf16[3,32,640]{2,1,0:T(8,128)(2,1)S(1)} collective-permute-done((bf16[3,32,640]{2,1,0:T(8,128)(2,1)S(1)}, bf16[3,32,640]{2,1,0:T(8,128)(2,1)S(1)}, u32[]{:S(2)}, u32[]{:S(2)}) %collective-permute-start.2) | collective-permute-done | bytes 122912 | tf_op jit(solution)/shard_map/while/body/eval_jaxpr/ppermute | solution.py:15
  530.2 10.7 %collective-permute-done.3 = bf16[3,32,640]{2,1,0:T(8,128)(2,1)S(1)} collective-permute-done((bf16[3,32,640]{2,1,0:T(8,128)(2,1)S(1)}, bf16[3,32,640]{2,1,0:T(8,128)(2,1)S(1)}, u32[]{:S(2)}, u32[]{:S(2)}) %collective-permute-start.3) | collective-permute-done | bytes 122912 | tf_op jit(solution)/shard_map/while/body/eval_jaxpr/ppermute | solution.py:15
  557.1 10.2 collective-permute-done.2
  580.2 10.3 %collective-permute-done.3 = bf16[3,32,640]{2,1,0:T(8,128)(2,1)S(1)} collective-permute-done((bf16[3,32,640]{2,1,0:T(8,128)(2,1)S(1)}, bf16[3,32,640]{2,1,0:T(8,128)(2,1)S(1)}, u32[]{:S(2)}, u32[]{:S(2)}) %collective-permute-start.3) | collective-permute-done | bytes 122912 | tf_op jit(solution)/shard_map/while/body/eval_jaxpr/ppermute | solution.py:15
  606.7 10.3 %collective-permute-done.2 = bf16[3,32,640]{2,1,0:T(8,128)(2,1)S(1)} collective-permute-done((bf16[3,32,640]{2,1,0:T(8,128)(2,1)S(1)}, bf16[3,32,640]{2,1,0:T(8,128)(2,1)S(1)}, u32[]{:S(2)}, u32[]{:S(2)}) %collective-permute-start.2) | collective-permute-done | bytes 122912 | tf_op jit(solution)/shard_map/while/body/eval_jaxpr/ppermute | solution.py:15
  629.8 10.3 %collective-permute-done.3 = bf16[3,32,640]{2,1,0:T(8,128)(2,1)S(1)} collective-permute-done((bf16[3,32,640]{2,1,0:T(8,128)(2,1)S(1)}, bf16[3,32,640]{2,1,0:T(8,128)(2,1)S(1)}, u32[]{:S(2)}, u32[]{:S(2)}) %collective-permute-start.3) | collective-permute-done | bytes 122912 | tf_op jit(solution)/shard_map/while/body/eval_jaxpr/ppermute | solution.py:15
  656.3 10.4 %collective-permute-done.2 = bf16[3,32,640]{2,1,0:T(8,128)(2,1)S(1)} collective-permute-done((bf16[3,32,640]{2,1,0:T(8,128)(2,1)S(1)}, bf16[3,32,640]{2,1,0:T(8,128)(2,1)S(1)}, u32[]{:S(2)}, u32[]{:S(2)}) %collective-permute-start.2) | collective-permute-done | bytes 122912 | tf_op jit(solution)/shard_map/while/body/eval_jaxpr/ppermute | solution.py:15
  679.4 11.6 %collective-permute-done.3 = bf16[3,32,640]{2,1,0:T(8,128)(2,1)S(1)} collective-permute-done((bf16[3,32,640]{2,1,0:T(8,128)(2,1)S(1)}, bf16[3,32,640]{2,1,0:T(8,128)(2,1)S(1)}, u32[]{:S(2)}, u32[]{:S(2)}) %collective-permute-start.3) | collective-permute-done | bytes 122912 | tf_op jit(solution)/shard_map/while/body/eval_jaxpr/ppermute | solution.py:15
  707.2 10.3 %collective-permute-done.2 = bf16[3,32,640]{2,1,0:T(8,128)(2,1)S(1)} collective-permute-done((bf16[3,32,640]{2,1,0:T(8,128)(2,1)S(1)}, bf16[3,32,640]{2,1,0:T(8,128)(2,1)S(1)}, u32[]{:S(2)}, u32[]{:S(2)}) %collective-permute-start.2) | collective-permute-done | bytes 122912 | tf_op jit(solution)/shard_map/while/body/eval_jaxpr/ppermute | solution.py:15
  730.3 10.1 collective-permute-done.3
  804.4 209.5 %reduce-scatter.2.cloned.1.call-done = bf16[1,240,640]{2,1,0:T(8,128)(2,1)} async-done(((bf16[32,240,640]{2,1,0:T(8,128)(2,1)}), bf16[1,240,640]{2,1,0:T(8,128)(2,1)}) %reduce-scatter.2.cloned.1.call-update) | async-done | bytes 307216 | tf_op jit(solution)/shard_map/reduce_scatter | solution.py:210
  (670 shorter events, 501.7 us)
Async XLA Ops:
  7.2 78.9 %all-gather.3.cloned.1.call-start = ((), (), s32[]{:S(2)}) async-start(), calls=%async_computation.2 | async-start | bytes 10137600 | tf_op jit(solution)/shard_map/all_gather | solution.py:125
  9.0 1004.9 %reduce-scatter.2.cloned.1.call-start = ((), (), s32[]{:S(2)}) async-start(), calls=%async_computation.1 | async-start | bytes 10137600 | tf_op jit(solution)/shard_map/reduce_scatter | solution.py:210
  153.6 6.0 collective-permute-start.1
  177.9 5.6 collective-permute-start
  223.9 12.0 %collective-permute-start = (bf16[3,32,640]{2,1,0:T(8,128)(2,1)S(1)}, bf16[3,32,640]{2,1,0:T(8,128)(2,1)S(1)}, u32[]{:S(2)}, u32[]{:S(2)}) collective-permute-start(bf16[3,32,640]{2,1,0:T(8,128)(2,1)S(1)} %fusion.140), channel_id=1, source_target_pairs={{0,32},{32,64},{64,96},{96,128},{128,160},{160,192},{192,224},{1,3... | collective-permute-start | bytes 368648 | tf_op jit(solution)/shard_map/while/body/eval_jaxpr/ppermute | solution.py:15
  252.3 11.6 %collective-permute-start.1 = (bf16[3,32,640]{2,1,0:T(8,128)(2,1)S(1)}, bf16[3,32,640]{2,1,0:T(8,128)(2,1)S(1)}, u32[]{:S(2)}, u32[]{:S(2)}) collective-permute-start(bf16[3,32,640]{2,1,0:T(8,128)(2,1)S(1)} %fusion.142), channel_id=1, source_target_pairs={{0,32},{32,64},{64,96},{96,128},{128,160},{160,192},{192,224},{1,3... | collective-permute-start | bytes 368648 | tf_op jit(solution)/shard_map/while/body/eval_jaxpr/ppermute | solution.py:15
  282.3 11.7 %collective-permute-start = (bf16[3,32,640]{2,1,0:T(8,128)(2,1)S(1)}, bf16[3,32,640]{2,1,0:T(8,128)(2,1)S(1)}, u32[]{:S(2)}, u32[]{:S(2)}) collective-permute-start(bf16[3,32,640]{2,1,0:T(8,128)(2,1)S(1)} %fusion.140), channel_id=1, source_target_pairs={{0,32},{32,64},{64,96},{96,128},{128,160},{160,192},{192,224},{1,3... | collective-permute-start | bytes 368648 | tf_op jit(solution)/shard_map/while/body/eval_jaxpr/ppermute | solution.py:15
  310.4 11.6 %collective-permute-start.1 = (bf16[3,32,640]{2,1,0:T(8,128)(2,1)S(1)}, bf16[3,32,640]{2,1,0:T(8,128)(2,1)S(1)}, u32[]{:S(2)}, u32[]{:S(2)}) collective-permute-start(bf16[3,32,640]{2,1,0:T(8,128)(2,1)S(1)} %fusion.142), channel_id=1, source_target_pairs={{0,32},{32,64},{64,96},{96,128},{128,160},{160,192},{192,224},{1,3... | collective-permute-start | bytes 368648 | tf_op jit(solution)/shard_map/while/body/eval_jaxpr/ppermute | solution.py:15
  340.3 11.7 %collective-permute-start = (bf16[3,32,640]{2,1,0:T(8,128)(2,1)S(1)}, bf16[3,32,640]{2,1,0:T(8,128)(2,1)S(1)}, u32[]{:S(2)}, u32[]{:S(2)}) collective-permute-start(bf16[3,32,640]{2,1,0:T(8,128)(2,1)S(1)} %fusion.140), channel_id=1, source_target_pairs={{0,32},{32,64},{64,96},{96,128},{128,160},{160,192},{192,224},{1,3... | collective-permute-start | bytes 368648 | tf_op jit(solution)/shard_map/while/body/eval_jaxpr/ppermute | solution.py:15
  368.4 11.6 %collective-permute-start.1 = (bf16[3,32,640]{2,1,0:T(8,128)(2,1)S(1)}, bf16[3,32,640]{2,1,0:T(8,128)(2,1)S(1)}, u32[]{:S(2)}, u32[]{:S(2)}) collective-permute-start(bf16[3,32,640]{2,1,0:T(8,128)(2,1)S(1)} %fusion.142), channel_id=1, source_target_pairs={{0,32},{32,64},{64,96},{96,128},{128,160},{160,192},{192,224},{1,3... | collective-permute-start | bytes 368648 | tf_op jit(solution)/shard_map/while/body/eval_jaxpr/ppermute | solution.py:15
  398.4 11.7 %collective-permute-start = (bf16[3,32,640]{2,1,0:T(8,128)(2,1)S(1)}, bf16[3,32,640]{2,1,0:T(8,128)(2,1)S(1)}, u32[]{:S(2)}, u32[]{:S(2)}) collective-permute-start(bf16[3,32,640]{2,1,0:T(8,128)(2,1)S(1)} %fusion.140), channel_id=1, source_target_pairs={{0,32},{32,64},{64,96},{96,128},{128,160},{160,192},{192,224},{1,3... | collective-permute-start | bytes 368648 | tf_op jit(solution)/shard_map/while/body/eval_jaxpr/ppermute | solution.py:15
  426.5 11.6 %collective-permute-start.1 = (bf16[3,32,640]{2,1,0:T(8,128)(2,1)S(1)}, bf16[3,32,640]{2,1,0:T(8,128)(2,1)S(1)}, u32[]{:S(2)}, u32[]{:S(2)}) collective-permute-start(bf16[3,32,640]{2,1,0:T(8,128)(2,1)S(1)} %fusion.142), channel_id=1, source_target_pairs={{0,32},{32,64},{64,96},{96,128},{128,160},{160,192},{192,224},{1,3... | collective-permute-start | bytes 368648 | tf_op jit(solution)/shard_map/while/body/eval_jaxpr/ppermute | solution.py:15
  455.0 12.1 %collective-permute-start.2 = (bf16[3,32,640]{2,1,0:T(8,128)(2,1)S(1)}, bf16[3,32,640]{2,1,0:T(8,128)(2,1)S(1)}, u32[]{:S(2)}, u32[]{:S(2)}) collective-permute-start(bf16[3,32,640]{2,1,0:T(8,128)(2,1)S(1)} %fusion.157), channel_id=1, source_target_pairs={{32,0},{64,32},{96,64},{128,96},{160,128},{192,160},{224,192},{33,... | collective-permute-start | bytes 368648 | tf_op jit(solution)/shard_map/while/body/eval_jaxpr/ppermute | solution.py:15
  478.5 12.1 %collective-permute-start.3 = (bf16[3,32,640]{2,1,0:T(8,128)(2,1)S(1)}, bf16[3,32,640]{2,1,0:T(8,128)(2,1)S(1)}, u32[]{:S(2)}, u32[]{:S(2)}) collective-permute-start(bf16[3,32,640]{2,1,0:T(8,128)(2,1)S(1)} %fusion.162), channel_id=1, source_target_pairs={{32,0},{64,32},{96,64},{128,96},{160,128},{192,160},{224,192},{33,... | collective-permute-start | bytes 368648 | tf_op jit(solution)/shard_map/while/body/eval_jaxpr/ppermute | solution.py:15
  505.4 12.0 %collective-permute-start.2 = (bf16[3,32,640]{2,1,0:T(8,128)(2,1)S(1)}, bf16[3,32,640]{2,1,0:T(8,128)(2,1)S(1)}, u32[]{:S(2)}, u32[]{:S(2)}) collective-permute-start(bf16[3,32,640]{2,1,0:T(8,128)(2,1)S(1)} %fusion.157), channel_id=1, source_target_pairs={{32,0},{64,32},{96,64},{128,96},{160,128},{192,160},{224,192},{33,... | collective-permute-start | bytes 368648 | tf_op jit(solution)/shard_map/while/body/eval_jaxpr/ppermute | solution.py:15
  528.9 12.0 %collective-permute-start.3 = (bf16[3,32,640]{2,1,0:T(8,128)(2,1)S(1)}, bf16[3,32,640]{2,1,0:T(8,128)(2,1)S(1)}, u32[]{:S(2)}, u32[]{:S(2)}) collective-permute-start(bf16[3,32,640]{2,1,0:T(8,128)(2,1)S(1)} %fusion.162), channel_id=1, source_target_pairs={{32,0},{64,32},{96,64},{128,96},{160,128},{192,160},{224,192},{33,... | collective-permute-start | bytes 368648 | tf_op jit(solution)/shard_map/while/body/eval_jaxpr/ppermute | solution.py:15
  555.8 11.6 %collective-permute-start.2 = (bf16[3,32,640]{2,1,0:T(8,128)(2,1)S(1)}, bf16[3,32,640]{2,1,0:T(8,128)(2,1)S(1)}, u32[]{:S(2)}, u32[]{:S(2)}) collective-permute-start(bf16[3,32,640]{2,1,0:T(8,128)(2,1)S(1)} %fusion.157), channel_id=1, source_target_pairs={{32,0},{64,32},{96,64},{128,96},{160,128},{192,160},{224,192},{33,... | collective-permute-start | bytes 368648 | tf_op jit(solution)/shard_map/while/body/eval_jaxpr/ppermute | solution.py:15
  578.9 11.6 %collective-permute-start.3 = (bf16[3,32,640]{2,1,0:T(8,128)(2,1)S(1)}, bf16[3,32,640]{2,1,0:T(8,128)(2,1)S(1)}, u32[]{:S(2)}, u32[]{:S(2)}) collective-permute-start(bf16[3,32,640]{2,1,0:T(8,128)(2,1)S(1)} %fusion.162), channel_id=1, source_target_pairs={{32,0},{64,32},{96,64},{128,96},{160,128},{192,160},{224,192},{33,... | collective-permute-start | bytes 368648 | tf_op jit(solution)/shard_map/while/body/eval_jaxpr/ppermute | solution.py:15
  605.3 11.6 %collective-permute-start.2 = (bf16[3,32,640]{2,1,0:T(8,128)(2,1)S(1)}, bf16[3,32,640]{2,1,0:T(8,128)(2,1)S(1)}, u32[]{:S(2)}, u32[]{:S(2)}) collective-permute-start(bf16[3,32,640]{2,1,0:T(8,128)(2,1)S(1)} %fusion.157), channel_id=1, source_target_pairs={{32,0},{64,32},{96,64},{128,96},{160,128},{192,160},{224,192},{33,... | collective-permute-start | bytes 368648 | tf_op jit(solution)/shard_map/while/body/eval_jaxpr/ppermute | solution.py:15
  628.5 11.6 %collective-permute-start.3 = (bf16[3,32,640]{2,1,0:T(8,128)(2,1)S(1)}, bf16[3,32,640]{2,1,0:T(8,128)(2,1)S(1)}, u32[]{:S(2)}, u32[]{:S(2)}) collective-permute-start(bf16[3,32,640]{2,1,0:T(8,128)(2,1)S(1)} %fusion.162), channel_id=1, source_target_pairs={{32,0},{64,32},{96,64},{128,96},{160,128},{192,160},{224,192},{33,... | collective-permute-start | bytes 368648 | tf_op jit(solution)/shard_map/while/body/eval_jaxpr/ppermute | solution.py:15
  654.9 11.8 %collective-permute-start.2 = (bf16[3,32,640]{2,1,0:T(8,128)(2,1)S(1)}, bf16[3,32,640]{2,1,0:T(8,128)(2,1)S(1)}, u32[]{:S(2)}, u32[]{:S(2)}) collective-permute-start(bf16[3,32,640]{2,1,0:T(8,128)(2,1)S(1)} %fusion.157), channel_id=1, source_target_pairs={{32,0},{64,32},{96,64},{128,96},{160,128},{192,160},{224,192},{33,... | collective-permute-start | bytes 368648 | tf_op jit(solution)/shard_map/while/body/eval_jaxpr/ppermute | solution.py:15
  678.1 12.9 %collective-permute-start.3 = (bf16[3,32,640]{2,1,0:T(8,128)(2,1)S(1)}, bf16[3,32,640]{2,1,0:T(8,128)(2,1)S(1)}, u32[]{:S(2)}, u32[]{:S(2)}) collective-permute-start(bf16[3,32,640]{2,1,0:T(8,128)(2,1)S(1)} %fusion.162), channel_id=1, source_target_pairs={{32,0},{64,32},{96,64},{128,96},{160,128},{192,160},{224,192},{33,... | collective-permute-start | bytes 368648 | tf_op jit(solution)/shard_map/while/body/eval_jaxpr/ppermute | solution.py:15
  705.8 11.7 %collective-permute-start.2 = (bf16[3,32,640]{2,1,0:T(8,128)(2,1)S(1)}, bf16[3,32,640]{2,1,0:T(8,128)(2,1)S(1)}, u32[]{:S(2)}, u32[]{:S(2)}) collective-permute-start(bf16[3,32,640]{2,1,0:T(8,128)(2,1)S(1)} %fusion.157), channel_id=1, source_target_pairs={{32,0},{64,32},{96,64},{128,96},{160,128},{192,160},{224,192},{33,... | collective-permute-start | bytes 368648 | tf_op jit(solution)/shard_map/while/body/eval_jaxpr/ppermute | solution.py:15
  729.0 11.4 %collective-permute-start.3 = (bf16[3,32,640]{2,1,0:T(8,128)(2,1)S(1)}, bf16[3,32,640]{2,1,0:T(8,128)(2,1)S(1)}, u32[]{:S(2)}, u32[]{:S(2)}) collective-permute-start(bf16[3,32,640]{2,1,0:T(8,128)(2,1)S(1)} %fusion.162), channel_id=1, source_target_pairs={{32,0},{64,32},{96,64},{128,96},{160,128},{192,160},{224,192},{33,... | collective-permute-start | bytes 368648 | tf_op jit(solution)/shard_map/while/body/eval_jaxpr/ppermute | solution.py:15
  (11 other events, 27.0 us)
Sparse Core Ops, SparseCore 0:
  10.4 75.5 all-gather.2
  804.5 209.3 reduce-scatter.1
